TPU v7x, 32 devices: a whole 2x2x4 slice. The times are simulated.
32 devices in a mesh: body: 2 (over y), row: 4 (over z), sub: 4 (over x, core).
Axes of the slice: x: 2, y: 2, z: 4, core: 2. Of those that a mesh axis runs over, the one named last changes fastest.
Arguments:
- positions: float32 [8, 3, 10240], P(('body', 'sub'), None, 'row'), parts along dimension 0, may hold values from 0 to 1
- panel_area: float32 [8, 10240], P(('body', 'sub'), 'row'), parts along dimension 0, may hold values from 0.3 to 3
- self_term: float32 [8, 10240], P(('body', 'sub'), 'row'), parts along dimension 0, may hold values from 3 to 8
- excitation: float32 [8, 8, 10240], P(('body', 'sub'), None, 'row'), parts along dimension 0, may hold values from -6 to 6
- adjacency: int32 [8, 2], P('body'), parts along dimension 0, may hold values from 0 to 3, as said below
- block_list: int32 [8, 2, 32], P('body'), parts along dimension 0, may hold values from 0 to 319, as said below
- block_count: int32 [8, 2], P('body'), parts along dimension 0, may hold values from 1 to 32, as said below
Outputs:
- currents: float32 [8, 8, 10240], P(('body', 'sub'), None, 'row'), parts along dimension 0
- residual: float32 [8, 8, 10240], P(('body', 'sub'), None, 'row'), parts along dimension 0
There are 2 independent parts, one for each index of `body`. A program takes and returns all parts, laid end to end along the dimension named above; each array names one. Nothing has to cross between parts.
Inputs may be any that keep to these rules, and one draw needn't show every extreme that they name: `adjacency`: each subdomain lists 2 different subdomains other than itself. `block_list`: in each pair the first block_count entries are different; later entries are not used. `block_count`: some pair has exactly 32 blocks.
All inputs are finite; a program needn't handle non-finite values.
Results may differ from a plain program's by a relative error of at most 0.0003.
Values sent between devices are 32-bit elements; how exact they have to be, the bound alone decides.
No kernel may reach another device: no remote copies, remote signals or barrier semaphores. Data moves between devices by JAX's collectives and lax.ppermute only.
A program may use at most 192 MiB of HBM per device.

v0:
```python
import math

import jax
import jax.numpy as jnp
from jax import lax
from jax.sharding import PartitionSpec as P

BLK = 32
OUTER = 2


KAPPA = 40.0
COUPLE = 1.0
EPS = 1e-06
column_block = 2048


def kernel_tile(near, far, area, scale):
    squared = jnp.zeros(near.shape[1:] + far.shape[-1:], jnp.float32)
    for coord in range(3):
        spacing = near[coord][..., :, None] - far[coord][..., None, :]
        squared = squared + spacing * spacing
    radius = jnp.sqrt(squared)
    return jnp.cos(KAPPA * radius) / (1.0 + radius) * (area * scale)[..., None, :]


def pick_source(table, chosen):
    shaped = chosen.reshape(chosen.shape + (1,) * (table.ndim - 1))
    return jnp.sum(jnp.where(shaped, table, jnp.zeros_like(table)), axis=0)


def on_device(positions, panel_area, self_term, excitation, adjacency, block_list, block_count):
    width = excitation.shape[1]
    rows_here = excitation.shape[2]
    near = positions[0]
    diagonal = self_term[0]
    gathered_pos, gathered_area = (
        lax.all_gather(positions[0], "row", axis=1, tiled=True),
        lax.all_gather(panel_area[0], "row", axis=0, tiled=True),
    )
    other_pos, other_area = (
        lax.all_gather(positions, "sub", axis=0, tiled=True),
        lax.all_gather(panel_area, "sub", axis=0, tiled=True),
    )
    total_cols = gathered_pos.shape[1]
    scale = 1.0 / math.sqrt(total_cols)
    subdomains = adjacency.shape[0]
    local_blocks = rows_here // BLK

    def build_step(counter, stored):
        offset = counter * column_block
        block_pos = lax.dynamic_slice_in_dim(gathered_pos, offset, column_block, 1)
        block_area = lax.dynamic_slice_in_dim(gathered_area, offset, column_block, 0)
        tile = kernel_tile(near, block_pos, block_area, scale)
        return lax.dynamic_update_slice_in_dim(stored, tile, offset, 1)

    self_rows = lax.fori_loop(
        0, total_cols // column_block, build_step, jnp.zeros((rows_here, total_cols), jnp.float32)
    )

    def apply_self(field):
        product = lax.dot_general(
            lax.all_gather(field[None], "row", axis=2, tiled=True)[0],
            self_rows,
            (((1,), (1,)), ((), ())),
            precision=lax.Precision.HIGHEST,
            preferred_element_type=jnp.float32,
        )
        return diagonal[None, :] * field + product

    currents = jnp.zeros((width, rows_here), jnp.float32)
    residual = excitation[0]
    for outer_step in range(OUTER):
        if outer_step > 0:
            all_currents = lax.all_gather(currents[None], "sub", axis=0, tiled=True)
            mine = jnp.arange(subdomains, dtype=jnp.int32) == lax.axis_index("sub")
            my_adjacency = jnp.sum(jnp.where(mine[:, None], adjacency, 0), axis=0)
            my_lists = jnp.sum(jnp.where(mine[:, None, None], block_list, 0), axis=0)
            my_counts = jnp.sum(jnp.where(mine[:, None], block_count, 0), axis=0)
            first_block = lax.axis_index("row") * local_blocks
            global_ids = first_block + jnp.arange(local_blocks, dtype=jnp.int32)
            total = jnp.zeros((width, local_blocks, BLK), jnp.float32)
            for slot in range(adjacency.shape[1]):
                chosen = jnp.arange(subdomains, dtype=jnp.int32) == my_adjacency[slot]
                src_pos = pick_source(other_pos, chosen)
                src_area = pick_source(other_area, chosen)
                src_cur = pick_source(all_currents, chosen)
                tiles = kernel_tile(
                    near.reshape(3, local_blocks, BLK),
                    src_pos.reshape(3, local_blocks, BLK),
                    src_area.reshape(local_blocks, BLK),
                    COUPLE / math.sqrt(BLK),
                )
                coupling_product = jnp.einsum(
                    "bpq,ebq->ebp",
                    tiles,
                    src_cur.reshape(width, local_blocks, BLK),
                    precision=lax.Precision.HIGHEST,
                )
                listed = (my_lists[slot][:, None] == global_ids[None, :]) & (
                    jnp.arange(my_lists.shape[1], dtype=jnp.int32)[:, None] < my_counts[slot]
                )
                weight = jnp.sum(listed.astype(jnp.float32), axis=0)
                total = total + coupling_product * weight[None, :, None]
            coupled = total.reshape(width, rows_here)
            residual = residual - coupled
        image = apply_self(residual)
        second = apply_self(image)
        cross, square, res_second, img_second, sec_second = lax.psum(
            (
                jnp.sum(residual * image, axis=1),
                jnp.sum(image * image, axis=1),
                jnp.sum(residual * second, axis=1),
                jnp.sum(image * second, axis=1),
                jnp.sum(second * second, axis=1),
            ),
            "row",
        )
        first_alpha = cross / (square + EPS)
        currents = currents + first_alpha[:, None] * residual
        residual = residual - first_alpha[:, None] * image
        image = image - first_alpha[:, None] * second
        cross_next = (
            cross
            - first_alpha * res_second
            - first_alpha * square
            + first_alpha * first_alpha * img_second
        )
        square_next = (
            square - 2.0 * first_alpha * img_second + first_alpha * first_alpha * sec_second
        )
        next_alpha = cross_next / (square_next + EPS)
        currents = currents + next_alpha[:, None] * residual
        residual = residual - next_alpha[:, None] * image
    return (currents[None], residual[None])


def solution(mesh):
    in_specs = (
        P(("body", "sub"), None, "row"),
        P(("body", "sub"), "row"),
        P(("body", "sub"), "row"),
        P(("body", "sub"), None, "row"),
        P("body", None),
        P("body", None, None),
        P("body", None),
    )
    out_specs = (P(("body", "sub"), None, "row"), P(("body", "sub"), None, "row"))
    return jax.shard_map(
        on_device, mesh=mesh, in_specs=in_specs, out_specs=out_specs, check_vma=False
    )
```

profile of v0, /device:TPU:2, one launch (start us, length us, event | category | flops | bytes accessed | tf_op | source)
XLA Modules:
  0.0 967.0 jit_solution(10632081011282964408)
XLA Ops:
  0.6 0.8 copy.35
  1.4 13.7 %all-gather = f32[1,3,10240]{2,1,0:T(4,128)S(1)} all-gather(f32[1,3,2560]{2,1,0:T(4,128)S(1)} %copy.35), channel_id=2, replica_groups=mesh['body'=2,'row'=4,'sub'=4] {'row'}, dimensions={2}, use_global_device_ids=true | all-gather | bytes 153600 | tf_op jit(solution)/shard_map/all_gather | solution.py:38
  15.1 13.4 %all-gather.1 = f32[1,10240]{1,0:T(1,128)S(1)} all-gather(f32[1,2560]{1,0:T(1,128)} %param.10), channel_id=3, replica_groups=mesh['body'=2,'row'=4,'sub'=4] {'row'}, dimensions={1}, use_global_device_ids=true | all-gather | bytes 51200 | tf_op jit(solution)/shard_map/all_gather | solution.py:39
  28.5 32.6 %broadcast_in_dim.112 = f32[2560,10240]{1,0:T(8,128)} broadcast(f32[]{:T(128)} %constant.64.clone.1), dimensions={} | broadcast | bytes 104857600 | tf_op jit(solution)/shard_map/broadcast_in_dim | solution.py:58
  61.1 422.5 %while.13 = (s32[]{:T(128)}, f32[2560,10240]{1,0:T(8,128)}, f32[3,2560]{1,0:T(4,128)S(1)}, f32[3,10240]{1,0:T(4,128)S(1)}, f32[10240]{0:T(1024)S(1)}, /*index=5*...) while((s32[]{:T(128)}, f32[2560,10240]{1,0:T(8,128)}, f32[3,2560]{1,0:T(4,128)S(1)}, ...), condition=%wide.region_1.0_spmd, body=%wide.region_0.0_spmd.sunk | while | flops 62916616 | bytes 21162184 | solution.py:57
  61.1 0.1 constant_dynamic-slice_fusion.2
  61.3 0.1 slice_reduce_fusion.13
  61.3 84.3 %multiply_dynamic-update-slice_fusion.2 = f32[2560,10240]{1,0:T(8,128)} fusion(f32[2560,10240]{1,0:T(8,128)} %get-tuple-element.225, s32[]{:T(128)S(6)} %select_n.68, f32[2048]{0:T(1024)S(1)} %dynamic-slice_multiply_fusion.2, f32[2048]{0:T(1024)S(1)} %bitcast.78, f32[2560]{0:T(1024)S(1)} %get-tuple-element.208, f32[2048]{0:T(1024)S(1)} %bitcast.77, ...), kind=kLoop, calls=%fused_computation.clone.1 | loop fusion | flops 62914560 | bytes 21035012 | tf_op jit(solution)/shard_map/while/body/eval_jaxpr/dynamic_update_slice | solution.py:55
  145.6 0.1 constant_dynamic-slice_fusion.2
  145.8 84.3 %multiply_dynamic-update-slice_fusion.2 = f32[2560,10240]{1,0:T(8,128)} fusion(f32[2560,10240]{1,0:T(8,128)} %get-tuple-element.225, s32[]{:T(128)S(6)} %select_n.68, f32[2048]{0:T(1024)S(1)} %dynamic-slice_multiply_fusion.2, f32[2048]{0:T(1024)S(1)} %bitcast.78, f32[2560]{0:T(1024)S(1)} %get-tuple-element.208, f32[2048]{0:T(1024)S(1)} %bitcast.77, ...), kind=kLoop, calls=%fused_computation.clone.1 | loop fusion | flops 62914560 | bytes 21035012 | tf_op jit(solution)/shard_map/while/body/eval_jaxpr/dynamic_update_slice | solution.py:55
  230.1 0.1 constant_dynamic-slice_fusion.2
  230.3 84.3 %multiply_dynamic-update-slice_fusion.2 = f32[2560,10240]{1,0:T(8,128)} fusion(f32[2560,10240]{1,0:T(8,128)} %get-tuple-element.225, s32[]{:T(128)S(6)} %select_n.68, f32[2048]{0:T(1024)S(1)} %dynamic-slice_multiply_fusion.2, f32[2048]{0:T(1024)S(1)} %bitcast.78, f32[2560]{0:T(1024)S(1)} %get-tuple-element.208, f32[2048]{0:T(1024)S(1)} %bitcast.77, ...), kind=kLoop, calls=%fused_computation.clone.1 | loop fusion | flops 62914560 | bytes 21035012 | tf_op jit(solution)/shard_map/while/body/eval_jaxpr/dynamic_update_slice | solution.py:55
  314.6 0.1 constant_dynamic-slice_fusion.2
  314.9 84.3 %multiply_dynamic-update-slice_fusion.2 = f32[2560,10240]{1,0:T(8,128)} fusion(f32[2560,10240]{1,0:T(8,128)} %get-tuple-element.225, s32[]{:T(128)S(6)} %select_n.68, f32[2048]{0:T(1024)S(1)} %dynamic-slice_multiply_fusion.2, f32[2048]{0:T(1024)S(1)} %bitcast.78, f32[2560]{0:T(1024)S(1)} %get-tuple-element.208, f32[2048]{0:T(1024)S(1)} %bitcast.77, ...), kind=kLoop, calls=%fused_computation.clone.1 | loop fusion | flops 62914560 | bytes 21035012 | tf_op jit(solution)/shard_map/while/body/eval_jaxpr/dynamic_update_slice | solution.py:55
  399.1 0.1 constant_dynamic-slice_fusion.2
  399.3 84.3 %multiply_dynamic-update-slice_fusion.2 = f32[2560,10240]{1,0:T(8,128)} fusion(f32[2560,10240]{1,0:T(8,128)} %get-tuple-element.225, s32[]{:T(128)S(6)} %select_n.68, f32[2048]{0:T(1024)S(1)} %dynamic-slice_multiply_fusion.2, f32[2048]{0:T(1024)S(1)} %bitcast.78, f32[2560]{0:T(1024)S(1)} %get-tuple-element.208, f32[2048]{0:T(1024)S(1)} %bitcast.77, ...), kind=kLoop, calls=%fused_computation.clone.1 | loop fusion | flops 62914560 | bytes 21035012 | tf_op jit(solution)/shard_map/while/body/eval_jaxpr/dynamic_update_slice | solution.py:55
  483.7 14.8 %all_gather.29 = f32[1,8,10240]{2,1,0:T(8,128)S(1)} all-gather(f32[1,8,2560]{2,1,0:T(8,128)S(1)} %copy-done), channel_id=1, replica_groups=mesh['body'=2,'row'=4,'sub'=4] {'row'}, dimensions={2}, use_global_device_ids=true | all-gather | bytes 409600 | tf_op jit(solution)/shard_map/all_gather | solution.py:63
  498.4 91.5 %fusion = f32[8,2560]{1,0:T(8,128)S(1)} fusion(f32[2560,10240]{1,0:T(8,128)} %get-tuple-element.96, f32[1,8,10240]{2,1,0:T(8,128)S(1)} %all_gather.29, f32[1,8,2560]{2,1,0:T(8,128)S(1)} %copy-done, f32[2560]{0:T(1024)S(1)} %reduce.3), kind=kOutput, calls=%fused_computation.10 | convolution fusion | flops 2516623360 | bytes 105359360 | tf_op jit(solution)/shard_map/dot_general | solution.py:62
  589.9 14.3 %all-gather.2 = f32[8,10240]{1,0:T(8,128)S(1)} all-gather(f32[8,2560]{1,0:T(8,128)S(1)} %fusion), channel_id=4, replica_groups=mesh['body'=2,'row'=4,'sub'=4] {'row'}, dimensions={1}, use_global_device_ids=true | all-gather | bytes 409600 | tf_op jit(solution)/shard_map/all_gather | solution.py:63
  604.2 89.2 %fusion.68 = (f32[8]{0:T(128)S(1)}, f32[8]{0:T(128)S(1)}, f32[8]{0:T(128)S(1)}, f32[8]{0:T(128)S(1)}, f32[8]{0:T(128)S(1)}, /*index=5*/f32[8,2560]{1,0:T(8,128)S(1)}) fusion(f32[1,8,2560]{2,1,0:T(8,128)S(1)} %copy-done, f32[8,2560]{1,0:T(8,128)S(1)} %fusion, f32[8,10240]{1,0:T(8,128)S(1)} %all-gather.2, f32[2560,10240]{1,0:T(8,128)} %get-tuple-element.96, ...), kind=kOutput, calls=%fused_computation.79 | convolution fusion | flops 2516828160 | bytes 105441440 | tf_op jit(solution)/shard_map/dot_general | solution.py:62
  693.4 12.0 %all-reduce.1 = (f32[8]{0:T(128)S(1)}, f32[8]{0:T(128)S(1)}, f32[8]{0:T(128)S(1)}, f32[8]{0:T(128)S(1)}, f32[8]{0:T(128)S(1)}) all-reduce(f32[8]{0:T(128)S(1)} %get-tuple-element.113, f32[8]{0:T(128)S(1)} %get-tuple-element.112, f32[8]{0:T(128)S(1)} %get-tuple-element.111, ...), channel_id=1, replica_groups=mesh['body'=2,'row'=4,'sub'=4] {'row'}, use_global_device_ids=true, to_apply=%region_11.0 | all-reduce | flops 40 | bytes 320 | tf_op jit(solution)/shard_map/psum | solution.py:109
  705.5 0.1 fusion.67
  705.6 6.0 all-gather.3
  711.6 0.1 select_reduce_fusion.3
  711.7 0.6 fusion.76
  712.3 0.6 iota_compare_fusion.1
  713.0 0.6 iota_compare_fusion.4
  713.5 0.1 fusion.61
  713.7 0.1 reshape.115
  713.8 5.5 all_gather.32
  719.3 0.1 select_reduce_fusion.1
  719.8 0.7 iota_compare_fusion
  720.4 0.7 iota_compare_fusion.2
  721.1 0.1 select_reduce_fusion.2
  721.2 0.1 convert_reduce_fusion.1
  721.3 5.4 all-gather.6
  726.7 0.1 fusion.69
  727.3 10.7 %fusion.40 = f32[80,8,32]{2,1,0:T(8,128)S(1)} fusion(f32[80,32]{1,0:T(8,128)S(1)} %mul.352, f32[80,32]{1,0:T(8,128)S(1)} %sub.279, f32[80,32]{1,0:T(8,128)S(1)} %sub.276, f32[80,32]{1,0:T(8,128)S(1)} %sub.273, f32[80,32]{1,0:T(8,128)S(1)} %sub.268, f32[80,32]{1,0:T(8,128)S(1)} %sub.263, f32[80,32]{1,0:T(8,128)S(1)} %sub.258, ...), kind=kOutput, calls=%fused_computation.44 | convolution fusion | flops 8867840 | bytes 235840 | tf_op jit(solution)/shard_map/bpq,ebq->ebp/dot_general | solution.py:94
  737.9 0.1 reshape.114
  738.5 10.7 %fusion.37 = f32[8,80,32]{2,0,1:T(8,128)S(1)} fusion(f32[80,8,32]{2,1,0:T(8,128)S(1)} %fusion.40, f32[80,32]{1,0:T(8,128)S(1)} %mul.341, f32[80,32]{1,0:T(8,128)S(1)} %sub.270, f32[80,32]{1,0:T(8,128)S(1)} %sub.268, f32[80,32]{1,0:T(8,128)S(1)} %sub.265, f32[80,32]{1,0:T(8,128)S(1)} %sub.263, f32[80,32]{1,0:T(8,128)S(1)} %sub.260, f32[80,32]{1,0:T(8,128)S(1)} %sub.258, ...), kind=kOutput, calls=%fused_computation.43 | convolution fusion | flops 8888320 | bytes 317760 | tf_op jit(solution)/shard_map/bpq,ebq->ebp/dot_general | solution.py:94
  749.3 0.2 reshape.116
  749.4 0.1 subtract_subtract_fusion
  749.5 14.8 %all-gather.4 = f32[8,10240]{1,0:T(8,128)S(1)} all-gather(f32[8,2560]{1,0:T(8,128)S(1)} %subtract_subtract_fusion), channel_id=6, replica_groups=mesh['body'=2,'row'=4,'sub'=4] {'row'}, dimensions={1}, use_global_device_ids=true | all-gather | bytes 409600 | tf_op jit(solution)/shard_map/all_gather | solution.py:63
  764.3 89.0 %convolution_add_fusion.1 = f32[8,2560]{1,0:T(8,128)S(1)} fusion(f32[8,10240]{1,0:T(8,128)S(1)} %all-gather.4, f32[2560,10240]{1,0:T(8,128)} %get-tuple-element.96, f32[8,2560]{1,0:T(8,128)S(1)} %subtract_subtract_fusion, f32[2560]{0:T(1024)S(1)} %reduce.3), kind=kOutput, calls=%fused_computation.7 | convolution fusion | flops 2516623360 | bytes 105359360 | tf_op jit(solution)/shard_map/dot_general | solution.py:62
  853.3 14.5 %all-gather.5 = f32[8,10240]{1,0:T(8,128)S(1)} all-gather(f32[8,2560]{1,0:T(8,128)S(1)} %convolution_add_fusion.1), channel_id=7, replica_groups=mesh['body'=2,'row'=4,'sub'=4] {'row'}, dimensions={1}, use_global_device_ids=true | all-gather | bytes 409600 | tf_op jit(solution)/shard_map/all_gather | solution.py:63
  867.8 89.2 %multiply_reduce_fusion.2 = (f32[8]{0:T(128)S(1)}, f32[8]{0:T(128)S(1)}, f32[8]{0:T(128)S(1)}, f32[8]{0:T(128)S(1)}, f32[8]{0:T(128)S(1)}, /*index=5*/f32[8,2560]{1,0:T(8,128)S(1)}) fusion(f32[8,2560]{1,0:T(8,128)S(1)} %subtract_subtract_fusion, f32[8,2560]{1,0:T(8,128)S(1)} %convolution_add_fusion.1, f32[8,10240]{1,0:T(8,128)S(1)} %all-gather.5, ...), kind=kOutput, calls=%fused_computation.85 | convolution fusion | flops 2516828160 | bytes 105441440 | tf_op jit(solution)/shard_map/dot_general | solution.py:62
  957.0 8.7 all-reduce
  965.7 0.8 subtract_bitcast_fusion
  (46 shorter events, 1.6 us)
Async XLA Ops:
  61.1 422.5 %copy-start.3 = (f32[1,2560]{1,0:T(1,128)S(1)}, f32[1,2560]{1,0:T(1,128)}, u32[]{:S(2)}) copy-start(f32[1,2560]{1,0:T(1,128)} %param.11) | copy-start | bytes 30724
  61.1 422.5 %copy-start = (f32[1,8,2560]{2,1,0:T(8,128)S(1)}, f32[1,8,2560]{2,1,0:T(8,128)}, u32[]{:S(2)}) copy-start(f32[1,8,2560]{2,1,0:T(8,128)} %param.12) | copy-start | bytes 245764
  604.2 107.3 %copy-start.5 = (s32[4,2]{0,1:T(2,128)S(1)}, s32[4,2]{0,1:T(2,128)}, u32[]{:S(2)}) copy-start(s32[4,2]{0,1:T(2,128)} %param.15) | copy-start | bytes 100
  604.2 107.3 %copy-start.6 = (s32[4,2]{0,1:T(2,128)S(1)}, s32[4,2]{0,1:T(2,128)}, u32[]{:S(2)}) copy-start(s32[4,2]{0,1:T(2,128)} %param.13) | copy-start | bytes 100
  693.4 27.7 %copy-start.4 = (s32[4,2,32]{2,1,0:T(2,128)S(1)}, s32[4,2,32]{2,1,0:T(2,128)}, u32[]{:S(2)}) copy-start(s32[4,2,32]{2,1,0:T(2,128)} %param.14) | copy-start | bytes 3076
  693.4 27.9 %copy-start.2 = (f32[1,2560]{1,0:T(1,128)S(1)}, f32[1,2560]{1,0:T(1,128)}, u32[]{:S(2)}) copy-start(f32[1,2560]{1,0:T(1,128)} %param.10) | copy-start | bytes 30724
  693.4 33.5 %copy-start.1 = (f32[1,3,2560]{2,0,1:T(1,128)S(1)}, f32[1,3,2560]{2,0,1:T(1,128)}, u32[]{:S(2)}) copy-start(f32[1,3,2560]{2,0,1:T(1,128)} %param.9) | copy-start | bytes 92164
where the time goes:
time: 976 us; the launch traced here: 967 us
  other arithmetic  426 us (44%)
  matrix products  380 us (39%)
  blocking collectives  123 us (13%)
  local copies, waits for them, and re-layouts  36.4 us (4%)
    dynamic_update_slice x5, other arithmetic, build_step(): return lax.dynamic_update_slice_in_dim(stored, tile, offset, 1)  421 us
    dot_general x4, matrix products, apply_self(): lax.dot_general(lax.all_gather(field[None], 'row', axis=2, tiled=True)[0]...  359 us
    all_gather x4, blocking collectives, apply_self(): lax.all_gather(field[None], 'row', axis=2, tiled=True)[0]  58.4 us
    broadcast_in_dim x1, local copies, waits for them, and re-layouts, on_device(): jnp.zeros((rows_here, total_cols), jnp.float32)  32.6 us
    dot_general x2, matrix products, on_device(): jnp.einsum('bpq,ebq->ebp', tiles, src_cur.reshape(width, local_blocks, BL...  21.4 us
    psum x2, blocking collectives, on_device(): lax.psum((jnp.sum(residual * image, axis=1), jnp.sum(image * image, axis=...  20.8 us

commit v1 on v0

--- a/solution.py
+++ b/solution.py
@@ -1,18 +1,575 @@
+import functools
 import math
 
 import jax
 import jax.numpy as jnp
 from jax import lax
+from jax.experimental import pallas as pl
+from jax.experimental.pallas import tpu as pltpu
 from jax.sharding import PartitionSpec as P
 
 BLK = 32
 OUTER = 2
-
 
 KAPPA = 40.0
 COUPLE = 1.0
 EPS = 1e-06
 column_block = 2048
+
+F32 = jnp.float32
+BF16 = jnp.bfloat16
+TILE = 256
+CHUNK = 32
+FEATURES = 96
+WAVE = KAPPA / (2.0 * math.pi)
+ROUNDER = 12582912.0
+COSINE = (
+    0.999999210782322,
+    -19.738980355764046,
+    64.92865742103419,
+    -85.27162153430582,
+    58.790492120148535,
+    -21.07110562765538,
+)
+
+
+def to_grid(x, step):
+    shift = ROUNDER * step
+    return (x + shift) - shift
+
+
+def cos_turns(turns):
+    u = turns - to_grid(turns, 1.0)
+    s = u * u
+    value = jnp.full_like(s, COSINE[-1])
+    for coefficient in COSINE[-2::-1]:
+        value = value * s + coefficient
+    return value
+
+
+def green(squared_turns):
+    y = jnp.maximum(squared_turns, 1e-12)
+    turns = y * lax.rsqrt(y)
+    u = turns - to_grid(turns, 1.0)
+    s = u * u
+    value = COSINE[-1] * WAVE
+    for coefficient in COSINE[-2::-1]:
+        value = value * s + coefficient * WAVE
+    return value / (turns + WAVE)
+
+
+def features(points):
+    row = lax.broadcasted_iota(jnp.int32, points.shape, 0)
+    centred = jnp.where(row < 3, (points - 0.5) * WAVE, 0.0)
+    high = to_grid(centred, 2.0**-6)
+    rest = centred - high
+    mid = to_grid(rest, 2.0**-14)
+    low = rest - mid
+    coarse = jnp.sum(high * high, axis=0, keepdims=True)
+    fine = jnp.sum(2.0 * high * rest + rest * rest, axis=0, keepdims=True)
+    a = to_grid(coarse, 0.25)
+    b = to_grid(coarse - a, 2.0**-10)
+    c = coarse - a - b
+    d = fine.astype(BF16).astype(F32)
+    e = (fine - d).astype(BF16).astype(F32)
+    f = fine - d - e
+    norm = jnp.zeros_like(centred)
+    for k, piece in enumerate((a, b, c, d, e, f)):
+        norm = jnp.where(row == k, piece, norm)
+    one = jnp.where(row < 6, 1.0, 0.0)
+    zero = jnp.zeros_like(centred)
+    left = (high, norm, one, high, mid, high, low, mid, mid, low, low, zero)
+    right = (high, one, norm, mid, high, low, high, mid, low, mid, low, zero)
+    right = tuple(-2.0 * x if k not in (1, 2) else x for k, x in enumerate(right))
+    return left, right
+
+
+def two_pieces(x):
+    high = x.astype(BF16).astype(F32)
+    return jnp.concatenate([high, x - high], axis=0).astype(BF16)
+
+
+def nn(left, right):
+    return lax.dot_general(left, right, (((1,), (0,)), ((), ())), preferred_element_type=F32)
+
+
+def nt(left, right):
+    return lax.dot_general(left, right, (((1,), (1,)), ((), ())), preferred_element_type=F32)
+
+
+def prep_kernel(scale, doubled, pack_ref, left_ref, right_ref, field_ref):
+    pack = pack_ref[...]
+    count = pack.shape[1]
+    left, right = features(pack[:8])
+    right = jnp.concatenate(right, axis=0).astype(BF16)
+    field = two_pieces(pack[8:] * (pack[3:4] * scale))
+    if doubled:
+        for k in range(2):
+            right_ref[:, k * count : (k + 1) * count] = right
+            field_ref[:, k * count : (k + 1) * count] = field
+        left = jnp.concatenate(left + (jnp.zeros((128 - FEATURES, count), F32),), axis=0)
+        for k in range(count // TILE):
+            left_ref[k * TILE : (k + 1) * TILE, :] = left[:, k * TILE : (k + 1) * TILE].T.astype(BF16)
+    else:
+        half = count // 2
+        for k in range(count // TILE):
+            to = (k % 2) * half + (k // 2) * TILE
+            right_ref[:, to : to + TILE] = right[:, k * TILE : (k + 1) * TILE]
+            field_ref[:, to : to + TILE] = field[:, k * TILE : (k + 1) * TILE]
+
+
+def fill_tile(source, at, target_high, target_low, to):
+    for c in range(TILE // CHUNK):
+        rows = slice(c * CHUNK, (c + 1) * CHUNK)
+        g = green(source[rows, at : at + TILE])
+        high = g.astype(BF16)
+        target_high[rows, to : to + TILE] = high
+        target_low[rows, to : to + TILE] = (g - high.astype(F32)).astype(BF16)
+
+
+def build_own_kernel(left_ref, right_ref, field_ref, high_ref, low_ref, acc_ref, dist):
+    i = pl.program_id(0)
+    width = high_ref.shape[1]
+    tiles = width // TILE
+    here = pl.multiple_of(i * TILE, TILE)
+
+    @pl.when(i == 0)
+    def _():
+        acc_ref[...] = jnp.zeros_like(acc_ref)
+
+    dist[...] = nn(
+        left_ref[pl.ds(here, TILE), :FEATURES], right_ref[:, pl.ds(here, width)]
+    )
+    mine = field_ref[:, pl.ds(here, TILE)]
+    total = jnp.zeros((16, TILE), F32)
+    for k in range(tiles):
+        fill_tile(dist, k * TILE, high_ref, low_ref, k * TILE)
+        there = pl.ds(pl.multiple_of(here + k * TILE, TILE), TILE)
+        high = high_ref[:, k * TILE : (k + 1) * TILE]
+        low = low_ref[:, k * TILE : (k + 1) * TILE]
+        other = field_ref[:, there]
+        total = total + nt(other, high) + nt(other, low)
+        if 0 < k < tiles - 1:
+            acc_ref[:, there] += nn(mine, high) + nn(mine, low)
+    acc_ref[:, pl.ds(here, TILE)] += total
+
+
+def fold_pieces(x):
+    return x[:8] + x[8:]
+
+
+def write_partial(part_ref, acc_own, acc_oth):
+    count = acc_own.shape[1] // 2
+    half = count // 2
+    part_ref[:, :count] = fold_pieces(acc_own[:, :count] + acc_own[:, count:])
+    for b in range(3):
+        for k in range(count // TILE):
+            at = b * count + (k % 2) * half + (k // 2) * TILE
+            to = (b + 1) * count + k * TILE
+            part_ref[:, to : to + TILE] = fold_pieces(acc_oth[:, at : at + TILE])
+
+
+def build_oth_kernel(
+    parity_ref, left_ref, right_ref, own_ref, field_ref, acc_in_ref,
+    high_ref, low_ref, part_ref, dist, acc_own, acc_oth,
+):
+    i = pl.program_id(0)
+    count = left_ref.shape[0]
+    half = count // 2
+    tiles = half // TILE
+    here = pl.multiple_of(i * TILE, TILE)
+
+    @pl.when(i == 0)
+    def _():
+        acc_own[...] = acc_in_ref[...]
+        acc_oth[...] = jnp.zeros_like(acc_oth)
+
+    offsets = [
+        pl.multiple_of(b * count + ((i + parity_ref[b]) & 1) * half, TILE) for b in range(3)
+    ]
+    left = left_ref[pl.ds(here, TILE), :FEATURES]
+    mine = own_ref[:, pl.ds(here, TILE)]
+    total = jnp.zeros((16, TILE), F32)
+    dist[0] = nn(left, right_ref[:, pl.ds(offsets[0], half)])
+    for b in range(3):
+        if b < 2:
+            dist[(b + 1) % 2] = nn(left, right_ref[:, pl.ds(offsets[b + 1], half)])
+        for k in range(tiles):
+            to = b * half + k * TILE
+            fill_tile(dist.at[b % 2], k * TILE, high_ref, low_ref, to)
+            there = pl.ds(pl.multiple_of(offsets[b] + k * TILE, TILE), TILE)
+            high = high_ref[:, to : to + TILE]
+            low = low_ref[:, to : to + TILE]
+            other = field_ref[:, there]
+            total = total + nt(other, high) + nt(other, low)
+            acc_oth[:, there] += nn(mine, high) + nn(mine, low)
+    acc_own[:, pl.ds(here, TILE)] += total
+
+    @pl.when(i == pl.num_programs(0) - 1)
+    def _():
+        write_partial(part_ref, acc_own, acc_oth)
+
+
+def mr_step(even_ref, odd_ref, pack_ref, res_ref, cur_ref, new_res_ref, new_cur_ref):
+    count = even_ref.shape[1] // 2
+    image = []
+    numerator = 0.0
+    denominator = 0.0
+    for b in range(4):
+        source = odd_ref if b % 2 else even_ref
+        product = source[:, (b // 2) * count : (b // 2 + 1) * count]
+        cols = slice(b * count, (b + 1) * count)
+        res = res_ref[:, cols]
+        img = pack_ref[4:5, cols] * res + product
+        new_res_ref[:, cols] = img
+        numerator = numerator + jnp.sum(res * img, axis=1, keepdims=True)
+        denominator = denominator + jnp.sum(img * img, axis=1, keepdims=True)
+    alpha = numerator / (denominator + EPS)
+    for b in range(4):
+        cols = slice(b * count, (b + 1) * count)
+        res = res_ref[:, cols]
+        if cur_ref is None:
+            new_cur_ref[:, cols] = alpha * res
+        else:
+            new_cur_ref[:, cols] = cur_ref[:, cols] + alpha * res
+        new_res_ref[:, cols] = res - alpha * new_res_ref[:, cols]
+
+
+def step_kernel(even_ref, odd_ref, pack_ref, res_ref, cur_ref, new_res_ref, new_cur_ref):
+    mr_step(even_ref, odd_ref, pack_ref, res_ref, cur_ref, new_res_ref, new_cur_ref)
+
+
+def apply_kernel(scale, first, with_low, couple, *refs):
+    refs = list(refs)
+    parity_ref = refs.pop(0)
+    even_ref, odd_ref, pack_ref, res_ref = refs[:4]
+    refs = refs[4:]
+    cur_ref = None if first or couple else refs.pop(0)
+    own_high, oth_high = refs[:2]
+    refs = refs[2:]
+    pieces = [(own_high, oth_high)]
+    if with_low:
+        pieces.append((refs[0], refs[1]))
+        refs = refs[2:]
+    new_res_ref = refs.pop(0)
+    new_cur_ref = None if couple else refs.pop(0)
+    part_ref, own_field, oth_field, acc_own, acc_oth = refs
+
+    i = pl.program_id(0)
+    count = even_ref.shape[1] // 2
+    half = count // 2
+    here = pl.multiple_of(i * TILE, TILE)
+
+    @pl.when(i == 0)
+    def _():
+        acc_own[...] = jnp.zeros_like(acc_own)
+        acc_oth[...] = jnp.zeros_like(acc_oth)
+        if couple:
+            for b in range(4):
+                source = odd_ref if b % 2 else even_ref
+                cols = slice(b * count, (b + 1) * count)
+                new_res_ref[:, cols] = (
+                    res_ref[:, cols] - source[:, (b // 2) * count : (b // 2 + 1) * count]
+                )
+        else:
+            mr_step(even_ref, odd_ref, pack_ref, res_ref, cur_ref, new_res_ref, new_cur_ref)
+        for b in range(4):
+            for k in range(count // TILE):
+                cols = slice(b * count + k * TILE, b * count + (k + 1) * TILE)
+                field = two_pieces(new_res_ref[:, cols] * (pack_ref[3:4, cols] * scale))
+                if b == 0:
+                    own_field[:, k * TILE : (k + 1) * TILE] = field
+                    own_field[:, count + k * TILE : count + (k + 1) * TILE] = field
+                else:
+                    to = (b - 1) * count + (k % 2) * half + (k // 2) * TILE
+                    oth_field[:, to : to + TILE] = field
+
+    width = own_high.shape[1]
+    mine = own_field[:, pl.ds(here, TILE)]
+    span = pl.ds(here, width)
+    inner = pl.ds(pl.multiple_of(here + TILE, TILE), width - 2 * TILE)
+    total = jnp.zeros((16, TILE), F32)
+    for own_ref, _ in pieces:
+        total = total + nt(own_field[:, span], own_ref[...])
+        acc_own[:, inner] += nn(mine, own_ref[:, TILE : width - TILE])
+    for b in range(3):
+        there = pl.ds(
+            pl.multiple_of(b * count + ((i + parity_ref[b]) & 1) * half, TILE), half
+        )
+        for _, oth_ref in pieces:
+            block = oth_ref[:, b * half : (b + 1) * half]
+            total = total + nt(oth_field[:, there], block)
+            acc_oth[:, there] += nn(mine, block)
+    acc_own[:, pl.ds(here, TILE)] += total
+
+    @pl.when(i == pl.num_programs(0) - 1)
+    def _():
+        write_partial(part_ref, acc_own, acc_oth)
+
+
+def couple_kernel(source_ref, list_ref, count_ref, first_ref, near_ref, far_ref, cur_ref, out_ref):
+    count = near_ref.shape[1]
+    lane = lax.broadcasted_iota(jnp.int32, (1, count), 1)
+    ident = first_ref[0] + lane // BLK
+    row = lax.broadcasted_iota(jnp.int32, (128, 128), 0) // BLK
+    col = lax.broadcasted_iota(jnp.int32, (128, 128), 1) // BLK
+    same = row == col
+    total = None
+    weights = []
+    for slot in range(count_ref.shape[0]):
+        hits = jnp.zeros((1, count), F32)
+        for k in range(list_ref.shape[1]):
+            hit = (ident == list_ref[slot, k]) & (k < count_ref[slot])
+            hits = hits + jnp.where(hit, 1.0, 0.0)
+        weights.append(hits)
+    for g in range(count // 128):
+        cols = slice(g * 128, (g + 1) * 128)
+        near = near_ref[:8, cols].T
+        total = jnp.zeros((8, 128), F32)
+        for slot in range(count_ref.shape[0]):
+            far = far_ref[source_ref[slot], :, cols]
+            squared = jnp.zeros((128, 128), F32)
+            for x in range(3):
+                gap = near[:, x : x + 1] - far[x : x + 1, :]
+                squared = squared + gap * gap
+            safe = jnp.maximum(squared, 1e-30)
+            radius = safe * lax.rsqrt(safe)
+            tile = cos_turns(radius * WAVE) / (1.0 + radius)
+            tile = jnp.where(same, tile, 0.0)
+            field = cur_ref[source_ref[slot], :, cols] * (far[3:4, :] * (COUPLE / math.sqrt(BLK)))
+            high = tile.astype(BF16)
+            low = (tile - high.astype(F32)).astype(BF16)
+            pieces = two_pieces(field)
+            product = nt(pieces, high) + nt(pieces, low)
+            total = total + fold_pieces(product) * weights[slot][:, cols]
+        out_ref[:, cols] = total
+
+
+def whole(shape):
+    return pl.BlockSpec(shape, lambda i, *_: (0,) * len(shape))
+
+
+SMEM = pl.BlockSpec(memory_space=pltpu.SMEM)
+VMEM_LIMIT = 48 * 1024 * 1024
+
+
+def params(**kw):
+    return pltpu.CompilerParams(vmem_limit_bytes=VMEM_LIMIT, **kw)
+
+
+def on_plane(positions, panel_area, self_term, excitation, adjacency, block_list, block_count):
+    count = excitation.shape[2]
+    subs = adjacency.shape[0]
+    ranks = subs
+    unknowns = count * ranks
+    scale = 1.0 / math.sqrt(unknowns)
+    tiles = count // TILE
+    half = count // 2
+    own_width = (tiles // 2 + 1) * TILE
+    plane = lax.axis_index("row")
+    place = lax.axis_index("sub")
+
+    swap = [(z * subs + s, s * subs + z) for z in range(ranks) for s in range(subs)]
+
+    def over(bit):
+        return [(s, s ^ bit) for s in range(subs)]
+
+    def send(x, bit):
+        return lax.ppermute(x, "sub", over(bit))
+
+    pack = jnp.concatenate(
+        [
+            positions[0],
+            panel_area,
+            self_term,
+            jnp.zeros((3, count), F32),
+            excitation[0],
+        ],
+        axis=0,
+    )
+    pack = lax.ppermute(pack, ("row", "sub"), swap)
+
+    f32 = lambda *s: jax.ShapeDtypeStruct(s, F32)
+    b16 = lambda *s: jax.ShapeDtypeStruct(s, BF16)
+
+    left, right_own, field_own = pl.pallas_call(
+        functools.partial(prep_kernel, scale, True),
+        out_shape=(b16(count, 128), b16(FEATURES, 2 * count), b16(16, 2 * count)),
+        compiler_params=params(),
+        name="prep_own",
+    )(pack)
+
+    pack2 = send(pack, 2)
+    packs = jnp.stack([pack, pack2])
+    packs_odd = send(packs, 1)
+    full = jnp.concatenate([pack, packs_odd[0], pack2, packs_odd[1]], axis=1)
+
+    own_high, own_low, acc = pl.pallas_call(
+        build_own_kernel,
+        grid=(tiles,),
+        in_specs=[
+            whole((count, 128)),
+            whole((FEATURES, 2 * count)),
+            whole((16, 2 * count)),
+        ],
+        out_specs=(
+            pl.BlockSpec((TILE, own_width), lambda i: (i, 0)),
+            pl.BlockSpec((TILE, own_width), lambda i: (i, 0)),
+            whole((16, 2 * count)),
+        ),
+        out_shape=(b16(count, own_width), b16(count, own_width), f32(16, 2 * count)),
+        scratch_shapes=[pltpu.VMEM((TILE, own_width), F32)],
+        compiler_params=params(),
+        cost_estimate=pl.CostEstimate(
+            flops=60 * count * own_width, bytes_accessed=4 * count * own_width, transcendentals=0
+        ),
+        name="build_own",
+    )(left, right_own, field_own)
+
+    right_oth, field_oth = [], []
+    for b in range(1, 4):
+        r, f = pl.pallas_call(
+            lambda p, r, f: prep_kernel(scale, False, p, None, r, f),
+            out_shape=(b16(FEATURES, count), b16(16, count)),
+            compiler_params=params(),
+            name="prep_oth",
+        )(full[:, b * count : (b + 1) * count])
+        right_oth.append(r)
+        field_oth.append(f)
+    right_oth = jnp.concatenate(right_oth, axis=1)
+    field_oth = jnp.concatenate(field_oth, axis=1)
+
+    parity = jnp.stack([(place > (place ^ b)).astype(jnp.int32) for b in range(1, 4)])
+
+    oth_high, oth_low, part = pl.pallas_call(
+        build_oth_kernel,
+        grid_spec=pltpu.PrefetchScalarGridSpec(
+            num_scalar_prefetch=1,
+            grid=(tiles,),
+            in_specs=[
+                whole((count, 128)),
+                whole((FEATURES, 3 * count)),
+                whole((16, 2 * count)),
+                whole((16, 3 * count)),
+                whole((16, 2 * count)),
+            ],
+            out_specs=(
+                pl.BlockSpec((TILE, 3 * half), lambda i, *_: (i, 0)),
+                pl.BlockSpec((TILE, 3 * half), lambda i, *_: (i, 0)),
+                whole((8, 4 * count)),
+            ),
+            scratch_shapes=[
+                pltpu.VMEM((2, TILE, half), F32),
+                pltpu.VMEM((16, 2 * count), F32),
+                pltpu.VMEM((16, 3 * count), F32),
+            ],
+        ),
+        out_shape=(b16(count, 3 * half), b16(count, 3 * half), f32(8, 4 * count)),
+        compiler_params=params(),
+        name="build_oth",
+    )(parity, left, right_oth, field_own, field_oth, acc)
+
+    def pair(x, a, b):
+        return jnp.concatenate(
+            [x[:, a * count : (a + 1) * count], x[:, b * count : (b + 1) * count]], axis=1
+        )
+
+    def reduce_all(part):
+        got = send(pair(part, 1, 3), 1)
+        chip = pair(part, 0, 2) + got
+        got = send(chip, 2)
+        even = chip + pair(got, 1, 0)
+        odd = send(even, 1)
+        return even, odd
+
+    def apply(even, odd, res, cur, with_low, couple):
+        first = cur is None and not couple
+        operands = [even, odd, full, res]
+        specs = [
+            whole((8, 2 * count)),
+            whole((8, 2 * count)),
+            whole((16, 4 * count)),
+            whole((8, 4 * count)),
+        ]
+        if not first and not couple:
+            operands.append(cur)
+            specs.append(whole((8, 4 * count)))
+        own_spec = pl.BlockSpec((TILE, own_width), lambda i, *_: (i, 0))
+        oth_spec = pl.BlockSpec((TILE, 3 * half), lambda i, *_: (i, 0))
+        operands += [own_high, oth_high]
+        specs += [own_spec, oth_spec]
+        if with_low:
+            operands += [own_low, oth_low]
+            specs += [own_spec, oth_spec]
+        outs = 2 if couple else 3
+        return pl.pallas_call(
+            functools.partial(apply_kernel, scale, first, with_low, couple),
+            grid_spec=pltpu.PrefetchScalarGridSpec(
+                num_scalar_prefetch=1,
+                grid=(tiles,),
+                in_specs=specs,
+                out_specs=[whole((8, 4 * count))] * outs,
+                scratch_shapes=[
+                    pltpu.VMEM((16, 2 * count), BF16),
+                    pltpu.VMEM((16, 3 * count), BF16),
+                    pltpu.VMEM((16, 2 * count), F32),
+                    pltpu.VMEM((16, 3 * count), F32),
+                ],
+            ),
+            out_shape=[f32(8, 4 * count)] * outs,
+            compiler_params=params(),
+            name="apply",
+        )(parity, *operands)
+
+    even, odd = reduce_all(part)
+    res, cur, part = apply(even, odd, full[8:], None, True, False)
+    even, odd = reduce_all(part)
+    res, cur = pl.pallas_call(
+        step_kernel,
+        out_shape=[f32(8, 4 * count)] * 2,
+        compiler_params=params(),
+        name="step",
+    )(even, odd, full, res, cur)
+
+    def from_planes(x):
+        return jnp.stack(
+            [
+                lax.ppermute(x, "row", [(z, (z + k) % ranks) for z in range(ranks)])
+                for k in range(1, ranks)
+            ]
+        )
+
+    far = from_planes(pack[:8])
+    far_cur = from_planes(cur[:, :count])
+    mine = jnp.arange(subs, dtype=jnp.int32) == plane
+    neighbours = jnp.sum(jnp.where(mine[:, None], adjacency, 0), axis=0)
+    lists = jnp.sum(jnp.where(mine[:, None, None], block_list, 0), axis=0)
+    counts = jnp.sum(jnp.where(mine[:, None], block_count, 0), axis=0)
+    source = (plane - neighbours + subs) % subs - 1
+    first_block = (place * (count // BLK)).astype(jnp.int32).reshape(1)
+    coupled = pl.pallas_call(
+        couple_kernel,
+        in_specs=[SMEM] * 4 + [pl.BlockSpec(memory_space=pltpu.VMEM)] * 3,
+        out_shape=f32(8, count),
+        compiler_params=params(),
+        name="couple",
+    )(source, lists, counts, first_block, pack, far, far_cur)
+    even = jnp.concatenate([coupled, send(coupled, 2)], axis=1)
+    odd = send(even, 1)
+
+    res, part = apply(even, odd, res, None, True, True)
+    even, odd = reduce_all(part)
+    res, cur, part = apply(even, odd, res, cur, True, False)
+    even, odd = reduce_all(part)
+    res, cur = pl.pallas_call(
+        step_kernel,
+        out_shape=[f32(8, 4 * count)] * 2,
+        compiler_params=params(),
+        name="step",
+    )(even, odd, full, res, cur)
+    out = jnp.concatenate([cur[:, :count], res[:, :count]], axis=0)
+    out = lax.ppermute(out, ("row", "sub"), swap)
+    return out[None, :8], out[None, 8:]
 
 
 def kernel_tile(near, far, area, scale):
@@ -29,7 +586,7 @@
     return jnp.sum(jnp.where(shaped, table, jnp.zeros_like(table)), axis=0)
 
 
-def on_device(positions, panel_area, self_term, excitation, adjacency, block_list, block_count):
+def on_rows(positions, panel_area, self_term, excitation, adjacency, block_list, block_count):
     width = excitation.shape[1]
     rows_here = excitation.shape[2]
     near = positions[0]
@@ -135,6 +692,15 @@
     return (currents[None], residual[None])
 
 
+def on_device(sizes, *arrays):
+    excitation, adjacency = arrays[3], arrays[4]
+    count = excitation.shape[2]
+    square = sizes["row"] == sizes["sub"] == adjacency.shape[0] == 4
+    if square and excitation.shape[1] == 8 and count % (2 * TILE) == 0:
+        return on_plane(*arrays)
+    return on_rows(*arrays)
+
+
 def solution(mesh):
     in_specs = (
         P(("body", "sub"), None, "row"),
@@ -146,6 +712,11 @@
         P("body", None),
     )
     out_specs = (P(("body", "sub"), None, "row"), P(("body", "sub"), None, "row"))
+    sizes = {name: mesh.shape[name] for name in ("row", "sub")}
     return jax.shard_map(
-        on_device, mesh=mesh, in_specs=in_specs, out_specs=out_specs, check_vma=False
+        functools.partial(on_device, sizes),
+        mesh=mesh,
+        in_specs=in_specs,
+        out_specs=out_specs,
+        check_vma=False,
     )

time: 976 us -> 246 us (0.25)
  other arithmetic: 426 us -> 0.79 us
  matrix products: 380 us -> 0 us
  Pallas kernels: 0 us -> 149 us
  blocking collectives: 123 us -> 0 us
  waiting for transfers between devices: 0 us -> 73.5 us
  local copies, waits for them, and re-layouts: 36.4 us -> 3.35 us
  starting transfers between devices: 0 us -> 17.9 us
    dynamic_update_slice x5 -> x0, other arithmetic: 421 us -> none  [build_step(): return lax.dynamic_update_slice_in_dim(stored, tile, offset, 1)]
    dot_general x6 -> x0, matrix products: 380 us -> none  [the longest x4 359 us: apply_self(): lax.dot_general(lax.all_gather(field[None], 'row', axis=2, tiled=True)[0]...]
    pallas_call x0 -> x12, Pallas kernels: none -> 149 us  [the longest x3 82.1 us: apply(): pl.pallas_call(functools.partial(apply_kernel, scale, first, with_low, co...]
    all_gather x9 -> x0, blocking collectives: 102 us -> none  [the longest x4 58.4 us: apply_self(): lax.all_gather(field[None], 'row', axis=2, tiled=True)[0]]
    ppermute x0 -> x24, waiting for transfers between devices: none -> 73.5 us  [the longest x16 43.9 us: send(): return lax.ppermute(x, 'sub', over(bit))]
    broadcast_in_dim x1 -> x2, local copies, waits for them, and re-layouts: 32.6 us -> 0.68 us  [the longest x1 0.67 us: on_plane(): return (out[None, :8], out[None, 8:])]
    psum x2 -> x0, blocking collectives: 20.8 us -> none  [on_device(): lax.psum((jnp.sum(residual * image, axis=1), jnp.sum(image * image, axis=...]
    ppermute x0 -> x24, starting transfers between devices: none -> 17.9 us  [the longest x6 7.98 us: from_planes(): lax.ppermute(x, 'row', [(z, (z + k) % ranks) for z in range(ranks)])]
  transfers between devices with their start and end apart: 0 -> 24, of which waited for: 0 -> 20; matrix products, arithmetic and copies ran while one was open for 0% -> 0% of each run, Pallas kernels for 0% -> 8%
where the time goes in v1:
time: 246 us
  Pallas kernels  149 us (61%)
  waiting for transfers between devices  73.5 us (30%)
  starting transfers between devices  17.9 us (7%)
  local copies, waits for them, and re-layouts  3.35 us (1%)
    pallas_call x3, Pallas kernels, apply(): pl.pallas_call(functools.partial(apply_kernel, scale, first, with_low, co...  82.1 us
    ppermute x16, waiting for transfers between devices, send(): return lax.ppermute(x, 'sub', over(bit))  43.9 us
    pallas_call x1, Pallas kernels, on_plane(): pl.pallas_call(build_oth_kernel, grid_spec=pltpu.PrefetchScalarGridSpec(n...  42.8 us
    pallas_call x1, Pallas kernels, on_plane(): pl.pallas_call(build_own_kernel, grid=(tiles,), in_specs=[whole((count, 1...  18.3 us
    ppermute x1, waiting for transfers between devices, on_plane(): out = lax.ppermute(out, ('row', 'sub'), swap)  11.6 us
    ppermute x1, waiting for transfers between devices, on_plane(): pack = lax.ppermute(pack, ('row', 'sub'), swap)  9.44 us
    ppermute x6, waiting for transfers between devices, from_planes(): lax.ppermute(x, 'row', [(z, (z + k) % ranks) for z in range(ranks)])  8.54 us
    ppermute x6, starting transfers between devices, from_planes(): lax.ppermute(x, 'row', [(z, (z + k) % ranks) for z in range(ranks)])  7.98 us
  transfers between devices with their start and end apart: 24, of which 20 were waited for; matrix products, arithmetic and copies ran while one was open for 0% of the time, Pallas kernels for 8%

profile of v1, /device:TPU:2, one launch (start us, length us, event | category | flops | bytes accessed | tf_op | source)
XLA Modules:
  0.0 245.5 jit_solution(2031121710813133811)
XLA Ops:
  0.6 0.8 copy.11
  1.4 1.7 concatenate.54
  3.1 4.5 %collective-permute-start = (f32[16,2560]{1,0:T(8,128)S(1)}, f32[16,2560]{1,0:T(8,128)S(1)}, u32[]{:S(2)}, u32[]{:S(2)}) collective-permute-start(f32[16,2560]{1,0:T(8,128)S(1)} %concatenate.54), channel_id=1, source_target_pairs={{0,0},{1,4},{2,8},{3,12},{4,1},{5,5},{6,9},{7,13},{8,2},{9,6},{10,... | collective-permute-start | bytes 491528 | tf_op jit(solution)/shard_map/ppermute | solution.py:390
  7.6 9.4 %collective-permute-done.pack_ref.near_ref = f32[16,2560]{1,0:T(8,128)S(1)} collective-permute-done((f32[16,2560]{1,0:T(8,128)S(1)}, f32[16,2560]{1,0:T(8,128)S(1)}, u32[]{:S(2)}, u32[]{:S(2)}) %collective-permute-start) | collective-permute-done | bytes 163872 | tf_op jit(solution)/shard_map/ppermute | solution.py:390
  17.0 5.3 %collective-permute-done.4.p = f32[16,2560]{1,0:T(8,128)S(1)} collective-permute-done((f32[16,2560]{1,0:T(8,128)S(1)}, f32[16,2560]{1,0:T(8,128)S(1)}, u32[]{:S(2)}, u32[]{:S(2)}) %collective-permute-start.4) | collective-permute-done | bytes 163872 | tf_op jit(solution)/shard_map/ppermute | solution.py:378
  22.5 0.3 prep_own.1
  22.8 18.3 %build_own.1 = (bf16[2560,1536]{1,0:T(8,128)(2,1)}, bf16[2560,1536]{1,0:T(8,128)(2,1)}, f32[16,5120]{1,0:T(8,128)S(1)}) custom-call(bf16[2560,128]{1,0:T(8,128)(2,1)S(1)} %get-tuple-element.29.left_ref, bf16[96,5120]{1,0:T(8,128)(2,1)S(1)} %get-tuple-element.37.right_ref, bf16[16,5120]{1,0:T(8,128)(2,1)S(1)} %get-tuple-element.33.field_ref.own_ref), custom_call_target="tpu_custom_call" | custom-call | flops 235929600 | bytes 15728640 | tf_op jit(solution)/shard_map/build_own/pallas_call | solution.py:407
  41.3 0.2 prep_oth.3
  41.7 42.8 %build_oth.1 = (bf16[2560,3840]{1,0:T(8,128)(2,1)}, bf16[2560,3840]{1,0:T(8,128)(2,1)}, f32[8,10240]{1,0:T(8,128)S(1)}) custom-call(s32[3]{0:T(128)S(1)} %add_convert_fusion.parity_ref.refs_0_, bf16[2560,128]{1,0:T(8,128)(2,1)S(1)} %get-tuple-element.29.left_ref, bf16[96,7680]{1,0:T(8,128)(2,1)S(1)} %pad_maximum_fusion.right_ref, ...), custom_call_target="tpu_custom_call" | custom-call | tf_op jit(solution)/shard_map/build_oth/pallas_call | solution.py:444
  84.6 0.5 collective-permute-start.6
  85.1 1.0 collective-permute-done.6
  86.2 6.4 %collective-permute-done.7 = f32[8,5120]{1,0:T(8,128)S(1)} collective-permute-done((f32[8,5120]{1,0:T(8,128)S(1)}, f32[8,5120]{1,0:T(8,128)S(1)}, u32[]{:S(2)}, u32[]{:S(2)}) %collective-permute-start.7) | collective-permute-done | bytes 163872 | tf_op jit(solution)/shard_map/ppermute | solution.py:378
  92.8 1.3 collective-permute-done.8.refs_2_
  94.2 27.4 %apply.3 = (f32[8,10240]{1,0:T(8,128)S(1)}, f32[8,10240]{1,0:T(8,128)S(1)}, f32[8,10240]{1,0:T(8,128)S(1)}) custom-call(s32[3]{0:T(128)S(1)} %add_convert_fusion.parity_ref.refs_0_, f32[8,5120]{1,0:T(8,128)S(1)} %maximum_add_fusion.1.refs_1_, f32[8,5120]{1,0:T(8,128)S(1)} %collective-permute-done.8.refs_2_, ...), custom_call_target="tpu_custom_call" | custom-call | tf_op jit(solution)/shard_map/apply/pallas_call | solution.py:505
  121.6 0.2 collective-permute-start.9
  121.8 1.3 collective-permute-done.9
  123.1 0.4 collective-permute-start.10
  123.6 5.8 %collective-permute-done.10 = f32[8,5120]{1,0:T(8,128)S(1)} collective-permute-done((f32[8,5120]{1,0:T(8,128)S(1)}, f32[8,5120]{1,0:T(8,128)S(1)}, u32[]{:S(2)}, u32[]{:S(2)}) %collective-permute-start.10) | collective-permute-done | bytes 163872 | tf_op jit(solution)/shard_map/ppermute | solution.py:378
  129.7 1.0 collective-permute-start.2
  130.6 2.8 %collective-permute-start.3 = (f32[8,2560]{1,0:T(8,128)S(1)}, f32[8,2560]{1,0:T(8,128)S(1)}, u32[]{:S(2)}, u32[]{:S(2)}) collective-permute-start(f32[8,2560]{1,0:T(8,128)S(1)} %slice.132), channel_id=1, source_target_pairs={{0,12},{4,0},{8,4},{12,8},{1,13},{5,1},{9,5},{13,9},{2,14},{6,2},{... | collective-permute-start | bytes 245768 | tf_op jit(solution)/shard_map/ppermute | solution.py:537
  133.5 0.2 step.2
  133.8 0.6 collective-permute-start.12
  134.4 1.5 collective-permute-start.13
  135.9 0.9 collective-permute-done.1
  136.8 1.9 collective-permute-start.14
  138.8 0.8 collective-permute-done.2
  139.6 2.5 %collective-permute-done.12 = f32[8,2560]{1,0:T(8,128)S(1)} collective-permute-done((f32[8,2560]{1,0:T(8,128)S(1)}, f32[8,2560]{1,0:T(8,128)S(1)}, u32[]{:S(2)}, u32[]{:S(2)}) %collective-permute-start.12) | collective-permute-done | bytes 81952 | tf_op jit(solution)/shard_map/ppermute | solution.py:537
  142.2 4.3 %collective-permute-done.13 = f32[8,2560]{1,0:T(8,128)S(1)} collective-permute-done((f32[8,2560]{1,0:T(8,128)S(1)}, f32[8,2560]{1,0:T(8,128)S(1)}, u32[]{:S(2)}, u32[]{:S(2)}) %collective-permute-start.13) | collective-permute-done | bytes 81952 | tf_op jit(solution)/shard_map/ppermute | solution.py:537
  146.5 4.6 %couple.1 = f32[8,2560]{1,0:T(8,128)S(1)} custom-call(s32[2]{0:T(128)S(1)} %fusion.source_ref, s32[2,32]{1,0:T(2,128)S(1)} %select_reduce_fusion.list_ref, s32[2]{0:T(128)S(1)} %get-tuple-element.56.count_ref, s32[1]{0:T(128)} %bitcast.3.first_ref, f32[16,2560]{1,0:T(8,128)S(1)} %collective-permute-done.pack_ref.near_ref, ...), custom_call_target="tpu_custom_call" | custom-call | tf_op jit(solution)/shard_map/couple/pallas_call | solution.py:550
  151.1 0.3 collective-permute-start.15
  151.4 4.2 %collective-permute-done.15 = f32[8,2560]{1,0:T(8,128)S(1)} collective-permute-done((f32[8,2560]{1,0:T(8,128)S(1)}, f32[8,2560]{1,0:T(8,128)S(1)}, u32[]{:S(2)}, u32[]{:S(2)}) %collective-permute-start.15) | collective-permute-done | bytes 81952 | tf_op jit(solution)/shard_map/ppermute | solution.py:378
  155.7 1.4 collective-permute-done.16.refs_2_
  157.0 27.3 %apply.4 = (f32[8,10240]{1,0:T(8,128)S(1)}, f32[8,10240]{1,0:T(8,128)S(1)}) custom-call(s32[3]{0:T(128)S(1)} %add_convert_fusion.parity_ref.refs_0_, f32[8,5120]{1,0:T(8,128)S(1)} %pad_maximum_fusion.8.refs_1_, f32[8,5120]{1,0:T(8,128)S(1)} %collective-permute-done.16.refs_2_, f32[16,10240]{1,0:T(8,128)S(1)} %pad_maximum_fusion.1.refs_3_.pack_ref, ...), custom_call_target="tpu_custom_call" | custom-call | tf_op jit(solution)/shard_map/apply/pallas_call | solution.py:505
  184.4 0.2 collective-permute-start.17
  184.6 1.3 collective-permute-done.17
  185.9 0.4 collective-permute-start.18
  186.2 6.0 %collective-permute-done.18 = f32[8,5120]{1,0:T(8,128)S(1)} collective-permute-done((f32[8,5120]{1,0:T(8,128)S(1)}, f32[8,5120]{1,0:T(8,128)S(1)}, u32[]{:S(2)}, u32[]{:S(2)}) %collective-permute-start.18) | collective-permute-done | bytes 163872 | tf_op jit(solution)/shard_map/ppermute | solution.py:378
  192.3 1.4 collective-permute-done.19.refs_2_
  193.7 27.4 %apply.5 = (f32[8,10240]{1,0:T(8,128)S(1)}, f32[8,10240]{1,0:T(8,128)S(1)}, f32[8,10240]{1,0:T(8,128)S(1)}) custom-call(s32[3]{0:T(128)S(1)} %add_convert_fusion.parity_ref.refs_0_, f32[8,5120]{1,0:T(8,128)S(1)} %maximum_add_fusion.5.refs_1_, f32[8,5120]{1,0:T(8,128)S(1)} %collective-permute-done.19.refs_2_, ...), custom_call_target="tpu_custom_call" | custom-call | tf_op jit(solution)/shard_map/apply/pallas_call | solution.py:505
  221.2 0.2 collective-permute-start.20
  221.4 1.3 collective-permute-done.20
  222.7 0.4 collective-permute-start.21
  223.0 6.0 %collective-permute-done.21 = f32[8,5120]{1,0:T(8,128)S(1)} collective-permute-done((f32[8,5120]{1,0:T(8,128)S(1)}, f32[8,5120]{1,0:T(8,128)S(1)}, u32[]{:S(2)}, u32[]{:S(2)}) %collective-permute-start.21) | collective-permute-done | bytes 163872 | tf_op jit(solution)/shard_map/ppermute | solution.py:378
  229.1 1.4 collective-permute-done.22.odd_ref
  230.5 0.2 step.3
  230.8 2.4 collective-permute-start.23
  233.2 11.6 %collective-permute-done.23 = f32[16,2560]{1,0:T(8,128)S(1)} collective-permute-done((f32[16,2560]{1,0:T(8,128)S(1)}, f32[16,2560]{1,0:T(8,128)S(1)}, u32[]{:S(2)}, u32[]{:S(2)}) %collective-permute-start.23) | collective-permute-done | bytes 163872 | tf_op jit(solution)/shard_map/ppermute | solution.py:571
  244.8 0.7 slice_bitcast_fusion.2
  (61 shorter events, 2.0 us)
Async XLA Ops:
  3.1 13.9 %collective-permute-start = (f32[16,2560]{1,0:T(8,128)S(1)}, f32[16,2560]{1,0:T(8,128)S(1)}, u32[]{:S(2)}, u32[]{:S(2)}) collective-permute-start(f32[16,2560]{1,0:T(8,128)S(1)} %concatenate.54), channel_id=1, source_target_pairs={{0,0},{1,4},{2,8},{3,12},{4,1},{5,5},{6,9},{7,13},{8,2},{9,6},{10,... | collective-permute-start | bytes 491528 | tf_op jit(solution)/shard_map/ppermute | solution.py:390
  17.0 5.3 %collective-permute-start.4 = (f32[16,2560]{1,0:T(8,128)S(1)}, f32[16,2560]{1,0:T(8,128)S(1)}, u32[]{:S(2)}, u32[]{:S(2)}) collective-permute-start(f32[16,2560]{1,0:T(8,128)S(1)} %collective-permute-done.pack_ref.near_ref), channel_id=1, source_target_pairs={{0,2},{1,3},{2,0},{3,1},{4,6},{5,7},{6,4},{7,5},{8,10},{9,11},{10,... | collective-permute-start | bytes 491528 | tf_op jit(solution)/shard_map/ppermute | solution.py:378
  22.3 18.9 %collective-permute-start.5 = (f32[2,16,2560]{2,1,0:T(8,128)S(1)}, f32[2,16,2560]{2,1,0:T(8,128)S(1)}, u32[]{:S(2)}, u32[]{:S(2)}) collective-permute-start(f32[2,16,2560]{2,1,0:T(8,128)S(1)} %pad_maximum_fusion.2), channel_id=1, source_target_pairs={{0,1},{1,0},{2,3},{3,2},{4,5},{5,4},{6,7},{7,6},{8,9},{9,8},{10,11... | collective-permute-start | bytes 983048 | tf_op jit(solution)/shard_map/ppermute | solution.py:378
  84.6 1.5 collective-permute-start.6
  86.1 6.5 %collective-permute-start.7 = (f32[8,5120]{1,0:T(8,128)S(1)}, f32[8,5120]{1,0:T(8,128)S(1)}, u32[]{:S(2)}, u32[]{:S(2)}) collective-permute-start(f32[8,5120]{1,0:T(8,128)S(1)} %maximum_add_fusion), channel_id=1, source_target_pairs={{0,2},{1,3},{2,0},{3,1},{4,6},{5,7},{6,4},{7,5},{8,10},{9,11},{10,... | collective-permute-start | bytes 491528 | tf_op jit(solution)/shard_map/ppermute | solution.py:378
  92.7 1.5 collective-permute-start.8
  94.1 29.3 %copy-start.1 = (s32[4,2]{0,1:T(2,128)S(1)}, s32[4,2]{0,1:T(2,128)}, u32[]{:S(2)}) copy-start(s32[4,2]{0,1:T(2,128)} %param.13) | copy-start | bytes 100
  94.2 29.3 %copy-start.2 = (s32[4,2]{0,1:T(2,128)S(1)}, s32[4,2]{0,1:T(2,128)}, u32[]{:S(2)}) copy-start(s32[4,2]{0,1:T(2,128)} %param.11) | copy-start | bytes 100
  94.2 39.3 %copy-start = (s32[4,2,32]{2,1,0:T(2,128)S(1)}, s32[4,2,32]{2,1,0:T(2,128)}, u32[]{:S(2)}) copy-start(s32[4,2,32]{2,1,0:T(2,128)} %param.12) | copy-start | bytes 3076
  121.6 1.5 collective-permute-start.9
  123.1 6.3 %collective-permute-start.10 = (f32[8,5120]{1,0:T(8,128)S(1)}, f32[8,5120]{1,0:T(8,128)S(1)}, u32[]{:S(2)}, u32[]{:S(2)}) collective-permute-start(f32[8,5120]{1,0:T(8,128)S(1)} %maximum_add_fusion.2), channel_id=1, source_target_pairs={{0,2},{1,3},{2,0},{3,1},{4,6},{5,7},{6,4},{7,5},{8,10},{9,11},{10,... | collective-permute-start | bytes 491528 | tf_op jit(solution)/shard_map/ppermute | solution.py:378
  129.5 4.1 %collective-permute-start.11 = (f32[8,5120]{1,0:T(8,128)S(1)}, f32[8,5120]{1,0:T(8,128)S(1)}, u32[]{:S(2)}, u32[]{:S(2)}) collective-permute-start(f32[8,5120]{1,0:T(8,128)S(1)} %maximum_add_fusion.3.even_ref), channel_id=1, source_target_pairs={{0,1},{1,0},{2,3},{3,2},{4,5},{5,4},{6,7},{7,6},{8,9},{9,8},{10,11... | collective-permute-start | bytes 491528 | tf_op jit(solution)/shard_map/ppermute | solution.py:378
  129.6 7.3 %collective-permute-start.1 = (f32[8,2560]{1,0:T(8,128)S(1)}, f32[8,2560]{1,0:T(8,128)S(1)}, u32[]{:S(2)}, u32[]{:S(2)}) collective-permute-start(f32[8,2560]{1,0:T(8,128)S(1)} %slice.132), channel_id=1, source_target_pairs={{0,4},{4,8},{8,12},{12,0},{1,5},{5,9},{9,13},{13,1},{2,6},{6,10},{... | collective-permute-start | bytes 245768 | tf_op jit(solution)/shard_map/ppermute | solution.py:537
  129.7 9.9 %collective-permute-start.2 = (f32[8,2560]{1,0:T(8,128)S(1)}, f32[8,2560]{1,0:T(8,128)S(1)}, u32[]{:S(2)}, u32[]{:S(2)}) collective-permute-start(f32[8,2560]{1,0:T(8,128)S(1)} %slice.132), channel_id=1, source_target_pairs={{0,8},{4,12},{8,0},{12,4},{1,9},{5,13},{9,1},{13,5},{2,10},{6,14},... | collective-permute-start | bytes 245768 | tf_op jit(solution)/shard_map/ppermute | solution.py:537
  130.6 9.0 %collective-permute-start.3 = (f32[8,2560]{1,0:T(8,128)S(1)}, f32[8,2560]{1,0:T(8,128)S(1)}, u32[]{:S(2)}, u32[]{:S(2)}) collective-permute-start(f32[8,2560]{1,0:T(8,128)S(1)} %slice.132), channel_id=1, source_target_pairs={{0,12},{4,0},{8,4},{12,8},{1,13},{5,1},{9,5},{13,9},{2,14},{6,2},{... | collective-permute-start | bytes 245768 | tf_op jit(solution)/shard_map/ppermute | solution.py:537
  133.8 8.4 %collective-permute-start.12 = (f32[8,2560]{1,0:T(8,128)S(1)}, f32[8,2560]{1,0:T(8,128)S(1)}, u32[]{:S(2)}, u32[]{:S(2)}) collective-permute-start(f32[8,2560]{1,0:T(8,128)S(1)} %slice.115), channel_id=1, source_target_pairs={{0,4},{4,8},{8,12},{12,0},{1,5},{5,9},{9,13},{13,1},{2,6},{6,10},{... | collective-permute-start | bytes 245768 | tf_op jit(solution)/shard_map/ppermute | solution.py:537
  134.4 12.1 %collective-permute-start.13 = (f32[8,2560]{1,0:T(8,128)S(1)}, f32[8,2560]{1,0:T(8,128)S(1)}, u32[]{:S(2)}, u32[]{:S(2)}) collective-permute-start(f32[8,2560]{1,0:T(8,128)S(1)} %slice.115), channel_id=1, source_target_pairs={{0,8},{4,12},{8,0},{12,4},{1,9},{5,13},{9,1},{13,5},{2,10},{6,14},... | collective-permute-start | bytes 245768 | tf_op jit(solution)/shard_map/ppermute | solution.py:537
  136.8 9.6 %collective-permute-start.14 = (f32[8,2560]{1,0:T(8,128)S(1)}, f32[8,2560]{1,0:T(8,128)S(1)}, u32[]{:S(2)}, u32[]{:S(2)}) collective-permute-start(f32[8,2560]{1,0:T(8,128)S(1)} %slice.115), channel_id=1, source_target_pairs={{0,12},{4,0},{8,4},{12,8},{1,13},{5,1},{9,5},{13,9},{2,14},{6,2},{... | collective-permute-start | bytes 245768 | tf_op jit(solution)/shard_map/ppermute | solution.py:537
  151.1 4.4 %collective-permute-start.15 = (f32[8,2560]{1,0:T(8,128)S(1)}, f32[8,2560]{1,0:T(8,128)S(1)}, u32[]{:S(2)}, u32[]{:S(2)}) collective-permute-start(f32[8,2560]{1,0:T(8,128)S(1)} %couple.1), channel_id=1, source_target_pairs={{0,2},{1,3},{2,0},{3,1},{4,6},{5,7},{6,4},{7,5},{8,10},{9,11},{10,... | collective-permute-start | bytes 245768 | tf_op jit(solution)/shard_map/ppermute | solution.py:378
  155.6 1.5 collective-permute-start.16
  184.4 1.5 collective-permute-start.17
  185.9 6.3 %collective-permute-start.18 = (f32[8,5120]{1,0:T(8,128)S(1)}, f32[8,5120]{1,0:T(8,128)S(1)}, u32[]{:S(2)}, u32[]{:S(2)}) collective-permute-start(f32[8,5120]{1,0:T(8,128)S(1)} %maximum_add_fusion.4), channel_id=1, source_target_pairs={{0,2},{1,3},{2,0},{3,1},{4,6},{5,7},{6,4},{7,5},{8,10},{9,11},{10,... | collective-permute-start | bytes 491528 | tf_op jit(solution)/shard_map/ppermute | solution.py:378
  192.2 1.5 collective-permute-start.19
  221.2 1.5 collective-permute-start.20
  222.7 6.3 %collective-permute-start.21 = (f32[8,5120]{1,0:T(8,128)S(1)}, f32[8,5120]{1,0:T(8,128)S(1)}, u32[]{:S(2)}, u32[]{:S(2)}) collective-permute-start(f32[8,5120]{1,0:T(8,128)S(1)} %maximum_add_fusion.6), channel_id=1, source_target_pairs={{0,2},{1,3},{2,0},{3,1},{4,6},{5,7},{6,4},{7,5},{8,10},{9,11},{10,... | collective-permute-start | bytes 491528 | tf_op jit(solution)/shard_map/ppermute | solution.py:378
  229.0 1.5 collective-permute-start.22
  230.8 14.1 %collective-permute-start.23 = (f32[16,2560]{1,0:T(8,128)S(1)}, f32[16,2560]{1,0:T(8,128)S(1)}, u32[]{:S(2)}, u32[]{:S(2)}) collective-permute-start(f32[16,2560]{1,0:T(8,128)S(1)} %pad_maximum_fusion.11), channel_id=1, source_target_pairs={{0,0},{1,4},{2,8},{3,12},{4,1},{5,5},{6,9},{7,13},{8,2},{9,6},{10,... | collective-permute-start | bytes 491528 | tf_op jit(solution)/shard_map/ppermute | solution.py:571

commit v2 on v1

--- a/solution.py
+++ b/solution.py
@@ -23,14 +23,15 @@
 FEATURES = 96
 WAVE = KAPPA / (2.0 * math.pi)
 ROUNDER = 12582912.0
-COSINE = (
-    0.999999210782322,
-    -19.738980355764046,
-    64.92865742103419,
-    -85.27162153430582,
-    58.790492120148535,
-    -21.07110562765538,
+HALF_COSINE = (
+    0.9999982896004456,
+    -4.934458936893249,
+    4.048771939331772,
+    -1.2478000348360374,
 )
+LIFT = 65536.0
+FP8 = jnp.float8_e4m3fn
+FP8_PEAK = 224.0
 
 
 def to_grid(x, step):
@@ -38,24 +39,21 @@
     return (x + shift) - shift
 
 
-def cos_turns(turns):
-    u = turns - to_grid(turns, 1.0)
+def cos_and_one(turns, amplitude):
+    u = turns - jnp.round(turns)
     s = u * u
-    value = jnp.full_like(s, COSINE[-1])
-    for coefficient in COSINE[-2::-1]:
-        value = value * s + coefficient
-    return value
+    factor = math.sqrt(2.0 * amplitude)
+    value = HALF_COSINE[-1] * factor
+    for coefficient in HALF_COSINE[-2::-1]:
+        value = value * s + coefficient * factor
+    return value * value
 
 
 def green(squared_turns):
     y = jnp.maximum(squared_turns, 1e-12)
     turns = y * lax.rsqrt(y)
-    u = turns - to_grid(turns, 1.0)
-    s = u * u
-    value = COSINE[-1] * WAVE
-    for coefficient in COSINE[-2::-1]:
-        value = value * s + coefficient * WAVE
-    return value / (turns + WAVE)
+    amplitude = WAVE * LIFT
+    return (cos_and_one(turns, amplitude) - amplitude) / (turns + WAVE)
 
 
 def features(points):
@@ -89,6 +87,11 @@
     return jnp.concatenate([high, x - high], axis=0).astype(BF16)
 
 
+def fp8_piece(x):
+    peak = jnp.maximum(jnp.max(jnp.abs(x), axis=1, keepdims=True), 1e-30)
+    return (x * (FP8_PEAK / peak)).astype(FP8), peak * (1.0 / FP8_PEAK)
+
+
 def nn(left, right):
     return lax.dot_general(left, right, (((1,), (0,)), ((), ())), preferred_element_type=F32)
 
@@ -97,16 +100,20 @@
     return lax.dot_general(left, right, (((1,), (1,)), ((), ())), preferred_element_type=F32)
 
 
-def prep_kernel(scale, doubled, pack_ref, left_ref, right_ref, field_ref):
+def prep_kernel(scale, doubled, pack_ref, left_ref, right_ref, field_ref, small_ref, undo_ref):
     pack = pack_ref[...]
     count = pack.shape[1]
     left, right = features(pack[:8])
     right = jnp.concatenate(right, axis=0).astype(BF16)
-    field = two_pieces(pack[8:] * (pack[3:4] * scale))
+    weighted = pack[8:] * (pack[3:4] * (scale / LIFT))
+    field = two_pieces(weighted)
+    small, undo = fp8_piece(weighted)
+    undo_ref[...] = jnp.broadcast_to(undo, undo_ref.shape)
     if doubled:
         for k in range(2):
             right_ref[:, k * count : (k + 1) * count] = right
             field_ref[:, k * count : (k + 1) * count] = field
+            small_ref[:, k * count : (k + 1) * count] = small
         left = jnp.concatenate(left + (jnp.zeros((128 - FEATURES, count), F32),), axis=0)
         for k in range(count // TILE):
             left_ref[k * TILE : (k + 1) * TILE, :] = left[:, k * TILE : (k + 1) * TILE].T.astype(BF16)
@@ -116,6 +123,7 @@
             to = (k % 2) * half + (k // 2) * TILE
             right_ref[:, to : to + TILE] = right[:, k * TILE : (k + 1) * TILE]
             field_ref[:, to : to + TILE] = field[:, k * TILE : (k + 1) * TILE]
+            small_ref[:, to : to + TILE] = small[:, k * TILE : (k + 1) * TILE]
 
 
 def fill_tile(source, at, target_high, target_low, to):
@@ -124,10 +132,16 @@
         g = green(source[rows, at : at + TILE])
         high = g.astype(BF16)
         target_high[rows, to : to + TILE] = high
-        target_low[rows, to : to + TILE] = (g - high.astype(F32)).astype(BF16)
-
-
-def build_own_kernel(left_ref, right_ref, field_ref, high_ref, low_ref, acc_ref, dist):
+        target_low[rows, to : to + TILE] = (g - high.astype(F32)).astype(FP8)
+
+
+def fold_pieces(x):
+    return x[:8] + x[8:]
+
+
+def build_own_kernel(
+    left_ref, right_ref, field_ref, small_ref, undo_ref, high_ref, low_ref, acc_ref, dist
+):
     i = pl.program_id(0)
     width = high_ref.shape[1]
     tiles = width // TILE
@@ -141,36 +155,34 @@
         left_ref[pl.ds(here, TILE), :FEATURES], right_ref[:, pl.ds(here, width)]
     )
     mine = field_ref[:, pl.ds(here, TILE)]
-    total = jnp.zeros((16, TILE), F32)
+    mine_small = small_ref[:, pl.ds(here, TILE)]
+    undo = undo_ref[:, :1]
+    total = jnp.zeros((8, TILE), F32)
     for k in range(tiles):
         fill_tile(dist, k * TILE, high_ref, low_ref, k * TILE)
         there = pl.ds(pl.multiple_of(here + k * TILE, TILE), TILE)
         high = high_ref[:, k * TILE : (k + 1) * TILE]
         low = low_ref[:, k * TILE : (k + 1) * TILE]
-        other = field_ref[:, there]
-        total = total + nt(other, high) + nt(other, low)
+        total += fold_pieces(nt(field_ref[:, there], high)) + nt(small_ref[:, there], low) * undo
         if 0 < k < tiles - 1:
-            acc_ref[:, there] += nn(mine, high) + nn(mine, low)
+            acc_ref[:, there] += fold_pieces(nn(mine, high)) + nn(mine_small, low) * undo
     acc_ref[:, pl.ds(here, TILE)] += total
-
-
-def fold_pieces(x):
-    return x[:8] + x[8:]
 
 
 def write_partial(part_ref, acc_own, acc_oth):
     count = acc_own.shape[1] // 2
     half = count // 2
-    part_ref[:, :count] = fold_pieces(acc_own[:, :count] + acc_own[:, count:])
+    part_ref[:, :count] = acc_own[:, :count] + acc_own[:, count:]
     for b in range(3):
         for k in range(count // TILE):
             at = b * count + (k % 2) * half + (k // 2) * TILE
             to = (b + 1) * count + k * TILE
-            part_ref[:, to : to + TILE] = fold_pieces(acc_oth[:, at : at + TILE])
+            part_ref[:, to : to + TILE] = acc_oth[:, at : at + TILE]
 
 
 def build_oth_kernel(
-    parity_ref, left_ref, right_ref, own_ref, field_ref, acc_in_ref,
+    parity_ref, left_ref, right_ref, own_ref, own_small_ref, own_undo_ref,
+    field_ref, small_ref, undo_ref, acc_in_ref,
     high_ref, low_ref, part_ref, dist, acc_own, acc_oth,
 ):
     i = pl.program_id(0)
@@ -189,20 +201,22 @@
     ]
     left = left_ref[pl.ds(here, TILE), :FEATURES]
     mine = own_ref[:, pl.ds(here, TILE)]
-    total = jnp.zeros((16, TILE), F32)
+    mine_small = own_small_ref[:, pl.ds(here, TILE)]
+    mine_undo = own_undo_ref[:, :1]
+    total = jnp.zeros((8, TILE), F32)
     dist[0] = nn(left, right_ref[:, pl.ds(offsets[0], half)])
     for b in range(3):
         if b < 2:
             dist[(b + 1) % 2] = nn(left, right_ref[:, pl.ds(offsets[b + 1], half)])
+        undo = undo_ref[:, b * 128 : b * 128 + 1]
         for k in range(tiles):
             to = b * half + k * TILE
             fill_tile(dist.at[b % 2], k * TILE, high_ref, low_ref, to)
             there = pl.ds(pl.multiple_of(offsets[b] + k * TILE, TILE), TILE)
             high = high_ref[:, to : to + TILE]
             low = low_ref[:, to : to + TILE]
-            other = field_ref[:, there]
-            total = total + nt(other, high) + nt(other, low)
-            acc_oth[:, there] += nn(mine, high) + nn(mine, low)
+            total += fold_pieces(nt(field_ref[:, there], high)) + nt(small_ref[:, there], low) * undo
+            acc_oth[:, there] += fold_pieces(nn(mine, high)) + nn(mine_small, low) * mine_undo
     acc_own[:, pl.ds(here, TILE)] += total
 
     @pl.when(i == pl.num_programs(0) - 1)
@@ -239,21 +253,17 @@
     mr_step(even_ref, odd_ref, pack_ref, res_ref, cur_ref, new_res_ref, new_cur_ref)
 
 
-def apply_kernel(scale, first, with_low, couple, *refs):
+def apply_kernel(scale, first, couple, *refs):
     refs = list(refs)
     parity_ref = refs.pop(0)
     even_ref, odd_ref, pack_ref, res_ref = refs[:4]
     refs = refs[4:]
     cur_ref = None if first or couple else refs.pop(0)
-    own_high, oth_high = refs[:2]
-    refs = refs[2:]
-    pieces = [(own_high, oth_high)]
-    if with_low:
-        pieces.append((refs[0], refs[1]))
-        refs = refs[2:]
+    own_high, own_low, oth_high, oth_low = refs[:4]
+    refs = refs[4:]
     new_res_ref = refs.pop(0)
     new_cur_ref = None if couple else refs.pop(0)
-    part_ref, own_field, oth_field, acc_own, acc_oth = refs
+    part_ref, own_field, oth_field, own_small, oth_small, undos, acc_own, acc_oth = refs
 
     i = pl.program_id(0)
     count = even_ref.shape[1] // 2
@@ -274,32 +284,42 @@
         else:
             mr_step(even_ref, odd_ref, pack_ref, res_ref, cur_ref, new_res_ref, new_cur_ref)
         for b in range(4):
+            cols = slice(b * count, (b + 1) * count)
+            weighted = new_res_ref[:, cols] * (pack_ref[3:4, cols] * (scale / LIFT))
+            field = two_pieces(weighted)
+            small, undo = fp8_piece(weighted)
+            undos[:, b * 128 : (b + 1) * 128] = jnp.broadcast_to(undo, (8, 128))
+            if b == 0:
+                for k in range(2):
+                    own_field[:, k * count : (k + 1) * count] = field
+                    own_small[:, k * count : (k + 1) * count] = small
+                continue
             for k in range(count // TILE):
-                cols = slice(b * count + k * TILE, b * count + (k + 1) * TILE)
-                field = two_pieces(new_res_ref[:, cols] * (pack_ref[3:4, cols] * scale))
-                if b == 0:
-                    own_field[:, k * TILE : (k + 1) * TILE] = field
-                    own_field[:, count + k * TILE : count + (k + 1) * TILE] = field
-                else:
-                    to = (b - 1) * count + (k % 2) * half + (k // 2) * TILE
-                    oth_field[:, to : to + TILE] = field
+                to = (b - 1) * count + (k % 2) * half + (k // 2) * TILE
+                oth_field[:, to : to + TILE] = field[:, k * TILE : (k + 1) * TILE]
+                oth_small[:, to : to + TILE] = small[:, k * TILE : (k + 1) * TILE]
 
     width = own_high.shape[1]
     mine = own_field[:, pl.ds(here, TILE)]
+    mine_small = own_small[:, pl.ds(here, TILE)]
+    undo = undos[:, :1]
     span = pl.ds(here, width)
     inner = pl.ds(pl.multiple_of(here + TILE, TILE), width - 2 * TILE)
-    total = jnp.zeros((16, TILE), F32)
-    for own_ref, _ in pieces:
-        total = total + nt(own_field[:, span], own_ref[...])
-        acc_own[:, inner] += nn(mine, own_ref[:, TILE : width - TILE])
+    total = fold_pieces(nt(own_field[:, span], own_high[...]))
+    total += nt(own_small[:, span], own_low[...]) * undo
+    acc_own[:, inner] += (
+        fold_pieces(nn(mine, own_high[:, TILE : width - TILE]))
+        + nn(mine_small, own_low[:, TILE : width - TILE]) * undo
+    )
     for b in range(3):
         there = pl.ds(
             pl.multiple_of(b * count + ((i + parity_ref[b]) & 1) * half, TILE), half
         )
-        for _, oth_ref in pieces:
-            block = oth_ref[:, b * half : (b + 1) * half]
-            total = total + nt(oth_field[:, there], block)
-            acc_oth[:, there] += nn(mine, block)
+        high = oth_high[:, b * half : (b + 1) * half]
+        low = oth_low[:, b * half : (b + 1) * half]
+        total += fold_pieces(nt(oth_field[:, there], high))
+        total += nt(oth_small[:, there], low) * undos[:, (b + 1) * 128 : (b + 1) * 128 + 1]
+        acc_oth[:, there] += fold_pieces(nn(mine, high)) + nn(mine_small, low) * undo
     acc_own[:, pl.ds(here, TILE)] += total
 
     @pl.when(i == pl.num_programs(0) - 1)
@@ -334,7 +354,7 @@
                 squared = squared + gap * gap
             safe = jnp.maximum(squared, 1e-30)
             radius = safe * lax.rsqrt(safe)
-            tile = cos_turns(radius * WAVE) / (1.0 + radius)
+            tile = (cos_and_one(radius * WAVE, 1.0) - 1.0) / (1.0 + radius)
             tile = jnp.where(same, tile, 0.0)
             field = cur_ref[source_ref[slot], :, cols] * (far[3:4, :] * (COUPLE / math.sqrt(BLK)))
             high = tile.astype(BF16)
@@ -391,10 +411,17 @@
 
     f32 = lambda *s: jax.ShapeDtypeStruct(s, F32)
     b16 = lambda *s: jax.ShapeDtypeStruct(s, BF16)
-
-    left, right_own, field_own = pl.pallas_call(
+    fp8 = lambda *s: jax.ShapeDtypeStruct(s, FP8)
+
+    left, right_own, field_own, small_own, undo_own = pl.pallas_call(
         functools.partial(prep_kernel, scale, True),
-        out_shape=(b16(count, 128), b16(FEATURES, 2 * count), b16(16, 2 * count)),
+        out_shape=(
+            b16(count, 128),
+            b16(FEATURES, 2 * count),
+            b16(16, 2 * count),
+            fp8(8, 2 * count),
+            f32(8, 128),
+        ),
         compiler_params=params(),
         name="prep_own",
     )(pack)
@@ -411,33 +438,36 @@
             whole((count, 128)),
             whole((FEATURES, 2 * count)),
             whole((16, 2 * count)),
+            whole((8, 2 * count)),
+            whole((8, 128)),
         ],
         out_specs=(
             pl.BlockSpec((TILE, own_width), lambda i: (i, 0)),
             pl.BlockSpec((TILE, own_width), lambda i: (i, 0)),
-            whole((16, 2 * count)),
+            whole((8, 2 * count)),
         ),
-        out_shape=(b16(count, own_width), b16(count, own_width), f32(16, 2 * count)),
+        out_shape=(b16(count, own_width), fp8(count, own_width), f32(8, 2 * count)),
         scratch_shapes=[pltpu.VMEM((TILE, own_width), F32)],
         compiler_params=params(),
         cost_estimate=pl.CostEstimate(
             flops=60 * count * own_width, bytes_accessed=4 * count * own_width, transcendentals=0
         ),
         name="build_own",
-    )(left, right_own, field_own)
-
-    right_oth, field_oth = [], []
+    )(left, right_own, field_own, small_own, undo_own)
+
+    others = []
     for b in range(1, 4):
-        r, f = pl.pallas_call(
-            lambda p, r, f: prep_kernel(scale, False, p, None, r, f),
-            out_shape=(b16(FEATURES, count), b16(16, count)),
-            compiler_params=params(),
-            name="prep_oth",
-        )(full[:, b * count : (b + 1) * count])
-        right_oth.append(r)
-        field_oth.append(f)
-    right_oth = jnp.concatenate(right_oth, axis=1)
-    field_oth = jnp.concatenate(field_oth, axis=1)
+        others.append(
+            pl.pallas_call(
+                lambda p, *outs: prep_kernel(scale, False, p, None, *outs),
+                out_shape=(b16(FEATURES, count), b16(16, count), fp8(8, count), f32(8, 128)),
+                compiler_params=params(),
+                name="prep_oth",
+            )(full[:, b * count : (b + 1) * count])
+        )
+    right_oth, field_oth, small_oth, undo_oth = (
+        jnp.concatenate(parts, axis=1) for parts in zip(*others)
+    )
 
     parity = jnp.stack([(place > (place ^ b)).astype(jnp.int32) for b in range(1, 4)])
 
@@ -450,8 +480,12 @@
                 whole((count, 128)),
                 whole((FEATURES, 3 * count)),
                 whole((16, 2 * count)),
+                whole((8, 2 * count)),
+                whole((8, 128)),
                 whole((16, 3 * count)),
-                whole((16, 2 * count)),
+                whole((8, 3 * count)),
+                whole((8, 3 * 128)),
+                whole((8, 2 * count)),
             ],
             out_specs=(
                 pl.BlockSpec((TILE, 3 * half), lambda i, *_: (i, 0)),
@@ -460,14 +494,17 @@
             ),
             scratch_shapes=[
                 pltpu.VMEM((2, TILE, half), F32),
-                pltpu.VMEM((16, 2 * count), F32),
-                pltpu.VMEM((16, 3 * count), F32),
+                pltpu.VMEM((8, 2 * count), F32),
+                pltpu.VMEM((8, 3 * count), F32),
             ],
         ),
-        out_shape=(b16(count, 3 * half), b16(count, 3 * half), f32(8, 4 * count)),
+        out_shape=(b16(count, 3 * half), fp8(count, 3 * half), f32(8, 4 * count)),
         compiler_params=params(),
         name="build_oth",
-    )(parity, left, right_oth, field_own, field_oth, acc)
+    )(
+        parity, left, right_oth, field_own, small_own, undo_own,
+        field_oth, small_oth, undo_oth, acc,
+    )
 
     def pair(x, a, b):
         return jnp.concatenate(
@@ -482,7 +519,7 @@
         odd = send(even, 1)
         return even, odd
 
-    def apply(even, odd, res, cur, with_low, couple):
+    def apply(even, odd, res, cur, couple):
         first = cur is None and not couple
         operands = [even, odd, full, res]
         specs = [
@@ -496,14 +533,11 @@
             specs.append(whole((8, 4 * count)))
         own_spec = pl.BlockSpec((TILE, own_width), lambda i, *_: (i, 0))
         oth_spec = pl.BlockSpec((TILE, 3 * half), lambda i, *_: (i, 0))
-        operands += [own_high, oth_high]
-        specs += [own_spec, oth_spec]
-        if with_low:
-            operands += [own_low, oth_low]
-            specs += [own_spec, oth_spec]
+        operands += [own_high, own_low, oth_high, oth_low]
+        specs += [own_spec, own_spec, oth_spec, oth_spec]
         outs = 2 if couple else 3
         return pl.pallas_call(
-            functools.partial(apply_kernel, scale, first, with_low, couple),
+            functools.partial(apply_kernel, scale, first, couple),
             grid_spec=pltpu.PrefetchScalarGridSpec(
                 num_scalar_prefetch=1,
                 grid=(tiles,),
@@ -512,8 +546,11 @@
                 scratch_shapes=[
                     pltpu.VMEM((16, 2 * count), BF16),
                     pltpu.VMEM((16, 3 * count), BF16),
-                    pltpu.VMEM((16, 2 * count), F32),
-                    pltpu.VMEM((16, 3 * count), F32),
+                    pltpu.VMEM((8, 2 * count), FP8),
+                    pltpu.VMEM((8, 3 * count), FP8),
+                    pltpu.VMEM((8, 4 * 128), F32),
+                    pltpu.VMEM((8, 2 * count), F32),
+                    pltpu.VMEM((8, 3 * count), F32),
                 ],
             ),
             out_shape=[f32(8, 4 * count)] * outs,
@@ -522,7 +559,7 @@
         )(parity, *operands)
 
     even, odd = reduce_all(part)
-    res, cur, part = apply(even, odd, full[8:], None, True, False)
+    res, cur, part = apply(even, odd, full[8:], None, False)
     even, odd = reduce_all(part)
     res, cur = pl.pallas_call(
         step_kernel,
@@ -557,9 +594,9 @@
     even = jnp.concatenate([coupled, send(coupled, 2)], axis=1)
     odd = send(even, 1)
 
-    res, part = apply(even, odd, res, None, True, True)
+    res, part = apply(even, odd, res, None, True)
     even, odd = reduce_all(part)
-    res, cur, part = apply(even, odd, res, cur, True, False)
+    res, cur, part = apply(even, odd, res, cur, False)
     even, odd = reduce_all(part)
     res, cur = pl.pallas_call(
         step_kernel,

time: 246 us -> 230 us (0.935)
  Pallas kernels: 149 us -> 131 us
    pallas_call x6, Pallas kernels: 82.6 us -> 66.5 us  [the longest x3 65.8 us: apply(): pl.pallas_call(functools.partial(apply_kernel, scale, first, couple), gri...]
where the time goes in v2:
time: 230 us; the launch traced here: 229 us
  Pallas kernels  131 us (57%)
  waiting for transfers between devices  73.5 us (32%)
  starting transfers between devices  17.9 us (8%)
  local copies, waits for them, and re-layouts  5.22 us (2%)
    pallas_call x3, Pallas kernels, apply(): pl.pallas_call(functools.partial(apply_kernel, scale, first, couple), gri...  65.8 us
    ppermute x16, waiting for transfers between devices, send(): return lax.ppermute(x, 'sub', over(bit))  43.9 us
    pallas_call x1, Pallas kernels, on_plane(): pl.pallas_call(build_oth_kernel, grid_spec=pltpu.PrefetchScalarGridSpec(n...  42.1 us
    pallas_call x1, Pallas kernels, on_plane(): pl.pallas_call(build_own_kernel, grid=(tiles,), in_specs=[whole((count, 1...  17.1 us
    ppermute x1, waiting for transfers between devices, on_plane(): out = lax.ppermute(out, ('row', 'sub'), swap)  11.6 us
    ppermute x1, waiting for transfers between devices, on_plane(): pack = lax.ppermute(pack, ('row', 'sub'), swap)  9.44 us
    ppermute x6, waiting for transfers between devices, from_planes(): lax.ppermute(x, 'row', [(z, (z + k) % ranks) for z in range(ranks)])  8.54 us
    ppermute x6, starting transfers between devices, from_planes(): lax.ppermute(x, 'row', [(z, (z + k) % ranks) for z in range(ranks)])  7.98 us
  transfers between devices with their start and end apart: 24, of which 20 were waited for; matrix products, arithmetic and copies ran while one was open for 0% of the time, Pallas kernels for 8%

profile of v2, /device:TPU:2, one launch (start us, length us, event | category | flops | bytes accessed | tf_op | source)
XLA Modules:
  0.0 229.4 jit_solution(1400838121310281633)
XLA Ops:
  0.6 0.8 copy.11
  1.4 1.7 concatenate.60
  3.1 4.5 %collective-permute-start = (f32[16,2560]{1,0:T(8,128)S(1)}, f32[16,2560]{1,0:T(8,128)S(1)}, u32[]{:S(2)}, u32[]{:S(2)}) collective-permute-start(f32[16,2560]{1,0:T(8,128)S(1)} %concatenate.60), channel_id=1, source_target_pairs={{0,0},{1,4},{2,8},{3,12},{4,1},{5,5},{6,9},{7,13},{8,2},{9,6},{10,... | collective-permute-start | bytes 491528 | tf_op jit(solution)/shard_map/ppermute | solution.py:410
  7.6 9.4 %collective-permute-done.pack_ref.near_ref = f32[16,2560]{1,0:T(8,128)S(1)} collective-permute-done((f32[16,2560]{1,0:T(8,128)S(1)}, f32[16,2560]{1,0:T(8,128)S(1)}, u32[]{:S(2)}, u32[]{:S(2)}) %collective-permute-start) | collective-permute-done | bytes 163872 | tf_op jit(solution)/shard_map/ppermute | solution.py:410
  17.0 5.3 %collective-permute-done.4.p = f32[16,2560]{1,0:T(8,128)S(1)} collective-permute-done((f32[16,2560]{1,0:T(8,128)S(1)}, f32[16,2560]{1,0:T(8,128)S(1)}, u32[]{:S(2)}, u32[]{:S(2)}) %collective-permute-start.4) | collective-permute-done | bytes 163872 | tf_op jit(solution)/shard_map/ppermute | solution.py:398
  22.5 0.3 prep_own.1
  22.8 17.1 %build_own.1 = (bf16[2560,1536]{1,0:T(8,128)(2,1)}, f8e4m3fn[2560,1536]{1,0:T(32,128)(4,1)S(1)}, f32[8,5120]{1,0:T(8,128)S(1)}) custom-call(bf16[2560,128]{1,0:T(8,128)(2,1)S(1)} %get-tuple-element.37.left_ref, bf16[96,5120]{1,0:T(8,128)(2,1)S(1)} %get-tuple-element.53.right_ref, bf16[16,5120]{1,0:T(8,128)(2,1)S(1)} %get-tuple-element.41.field_ref.own_ref, ...), custom_call_target="tpu_custom_call" | custom-call | flops 235929600 | bytes 15728640 | tf_op jit(solution)/shard_map/build_own/pallas_call | solution.py:434
  40.0 1.9 copy-done
  41.9 0.2 prep_oth.4
  42.1 0.2 prep_oth.3
  42.3 0.2 prep_oth.5
  42.8 42.1 %build_oth.1 = (bf16[2560,3840]{1,0:T(8,128)(2,1)}, f8e4m3fn[2560,3840]{1,0:T(32,128)(4,1)}, f32[8,10240]{1,0:T(8,128)S(1)}) custom-call(s32[3]{0:T(128)S(1)} %add_convert_fusion.parity_ref.refs_0_, bf16[2560,128]{1,0:T(8,128)(2,1)S(1)} %get-tuple-element.37.left_ref, bf16[96,7680]{1,0:T(8,128)(2,1)S(1)} %pad_maximum_fusion.right_ref, ...), custom_call_target="tpu_custom_call" | custom-call | tf_op jit(solution)/shard_map/build_oth/pallas_call | solution.py:474
  84.9 0.6 collective-permute-start.6
  85.4 1.0 collective-permute-done.6
  86.6 6.5 %collective-permute-done.7 = f32[8,5120]{1,0:T(8,128)S(1)} collective-permute-done((f32[8,5120]{1,0:T(8,128)S(1)}, f32[8,5120]{1,0:T(8,128)S(1)}, u32[]{:S(2)}, u32[]{:S(2)}) %collective-permute-start.7) | collective-permute-done | bytes 163872 | tf_op jit(solution)/shard_map/ppermute | solution.py:398
  93.2 1.3 collective-permute-done.8.refs_2_
  94.5 22.2 %apply.3 = (f32[8,10240]{1,0:T(8,128)S(1)}, f32[8,10240]{1,0:T(8,128)S(1)}, f32[8,10240]{1,0:T(8,128)S(1)}) custom-call(s32[3]{0:T(128)S(1)} %add_convert_fusion.parity_ref.refs_0_, f32[8,5120]{1,0:T(8,128)S(1)} %maximum_add_fusion.1.refs_1_, f32[8,5120]{1,0:T(8,128)S(1)} %collective-permute-done.8.refs_2_, ...), custom_call_target="tpu_custom_call" | custom-call | tf_op jit(solution)/shard_map/apply/pallas_call | solution.py:539
  117.0 1.3 collective-permute-done.9
  118.3 0.4 collective-permute-start.10
  118.8 5.8 %collective-permute-done.10 = f32[8,5120]{1,0:T(8,128)S(1)} collective-permute-done((f32[8,5120]{1,0:T(8,128)S(1)}, f32[8,5120]{1,0:T(8,128)S(1)}, u32[]{:S(2)}, u32[]{:S(2)}) %collective-permute-start.10) | collective-permute-done | bytes 163872 | tf_op jit(solution)/shard_map/ppermute | solution.py:398
  124.9 1.0 collective-permute-start.2
  125.8 2.8 %collective-permute-start.3 = (f32[8,2560]{1,0:T(8,128)S(1)}, f32[8,2560]{1,0:T(8,128)S(1)}, u32[]{:S(2)}, u32[]{:S(2)}) collective-permute-start(f32[8,2560]{1,0:T(8,128)S(1)} %slice.132), channel_id=1, source_target_pairs={{0,12},{4,0},{8,4},{12,8},{1,13},{5,1},{9,5},{13,9},{2,14},{6,2},{... | collective-permute-start | bytes 245768 | tf_op jit(solution)/shard_map/ppermute | solution.py:574
  128.8 0.2 step.2
  129.0 0.6 collective-permute-start.12
  129.6 1.5 collective-permute-start.13
  131.2 0.9 collective-permute-done.1
  132.1 2.0 collective-permute-start.14
  134.0 0.8 collective-permute-done.2
  134.8 2.5 %collective-permute-done.12 = f32[8,2560]{1,0:T(8,128)S(1)} collective-permute-done((f32[8,2560]{1,0:T(8,128)S(1)}, f32[8,2560]{1,0:T(8,128)S(1)}, u32[]{:S(2)}, u32[]{:S(2)}) %collective-permute-start.12) | collective-permute-done | bytes 81952 | tf_op jit(solution)/shard_map/ppermute | solution.py:574
  137.4 4.3 %collective-permute-done.13 = f32[8,2560]{1,0:T(8,128)S(1)} collective-permute-done((f32[8,2560]{1,0:T(8,128)S(1)}, f32[8,2560]{1,0:T(8,128)S(1)}, u32[]{:S(2)}, u32[]{:S(2)}) %collective-permute-start.13) | collective-permute-done | bytes 81952 | tf_op jit(solution)/shard_map/ppermute | solution.py:574
  141.7 4.4 %couple.1 = f32[8,2560]{1,0:T(8,128)S(1)} custom-call(s32[2]{0:T(128)S(1)} %fusion.source_ref, s32[2,32]{1,0:T(2,128)S(1)} %select_reduce_fusion.list_ref, s32[2]{0:T(128)S(1)} %get-tuple-element.72.count_ref, s32[1]{0:T(128)} %bitcast.3.first_ref, f32[16,2560]{1,0:T(8,128)S(1)} %collective-permute-done.pack_ref.near_ref, ...), custom_call_target="tpu_custom_call" | custom-call | tf_op jit(solution)/shard_map/couple/pallas_call | solution.py:587
  146.1 0.3 collective-permute-start.15
  146.4 4.2 %collective-permute-done.15 = f32[8,2560]{1,0:T(8,128)S(1)} collective-permute-done((f32[8,2560]{1,0:T(8,128)S(1)}, f32[8,2560]{1,0:T(8,128)S(1)}, u32[]{:S(2)}, u32[]{:S(2)}) %collective-permute-start.15) | collective-permute-done | bytes 81952 | tf_op jit(solution)/shard_map/ppermute | solution.py:398
  150.6 1.4 collective-permute-done.16.refs_2_
  152.0 21.4 %apply.4 = (f32[8,10240]{1,0:T(8,128)S(1)}, f32[8,10240]{1,0:T(8,128)S(1)}) custom-call(s32[3]{0:T(128)S(1)} %add_convert_fusion.parity_ref.refs_0_, f32[8,5120]{1,0:T(8,128)S(1)} %pad_maximum_fusion.8.refs_1_, f32[8,5120]{1,0:T(8,128)S(1)} %collective-permute-done.16.refs_2_, f32[16,10240]{1,0:T(8,128)S(1)} %pad_maximum_fusion.1.refs_3_.pack_ref, ...), custom_call_target="tpu_custom_call" | custom-call | tf_op jit(solution)/shard_map/apply/pallas_call | solution.py:539
  173.6 1.3 collective-permute-done.17
  174.9 0.4 collective-permute-start.18
  175.3 6.0 %collective-permute-done.18 = f32[8,5120]{1,0:T(8,128)S(1)} collective-permute-done((f32[8,5120]{1,0:T(8,128)S(1)}, f32[8,5120]{1,0:T(8,128)S(1)}, u32[]{:S(2)}, u32[]{:S(2)}) %collective-permute-start.18) | collective-permute-done | bytes 163872 | tf_op jit(solution)/shard_map/ppermute | solution.py:398
  181.3 1.4 collective-permute-done.19.refs_2_
  182.7 22.3 %apply.5 = (f32[8,10240]{1,0:T(8,128)S(1)}, f32[8,10240]{1,0:T(8,128)S(1)}, f32[8,10240]{1,0:T(8,128)S(1)}) custom-call(s32[3]{0:T(128)S(1)} %add_convert_fusion.parity_ref.refs_0_, f32[8,5120]{1,0:T(8,128)S(1)} %maximum_add_fusion.5.refs_1_, f32[8,5120]{1,0:T(8,128)S(1)} %collective-permute-done.19.refs_2_, ...), custom_call_target="tpu_custom_call" | custom-call | tf_op jit(solution)/shard_map/apply/pallas_call | solution.py:539
  205.3 1.3 collective-permute-done.20
  206.5 0.4 collective-permute-start.21
  206.9 6.0 %collective-permute-done.21 = f32[8,5120]{1,0:T(8,128)S(1)} collective-permute-done((f32[8,5120]{1,0:T(8,128)S(1)}, f32[8,5120]{1,0:T(8,128)S(1)}, u32[]{:S(2)}, u32[]{:S(2)}) %collective-permute-start.21) | collective-permute-done | bytes 163872 | tf_op jit(solution)/shard_map/ppermute | solution.py:398
  213.0 1.4 collective-permute-done.22.odd_ref
  214.4 0.2 step.3
  214.6 2.4 %collective-permute-start.23 = (f32[16,2560]{1,0:T(8,128)S(1)}, f32[16,2560]{1,0:T(8,128)S(1)}, u32[]{:S(2)}, u32[]{:S(2)}) collective-permute-start(f32[16,2560]{1,0:T(8,128)S(1)} %pad_maximum_fusion.11), channel_id=1, source_target_pairs={{0,0},{1,4},{2,8},{3,12},{4,1},{5,5},{6,9},{7,13},{8,2},{9,6},{10,... | collective-permute-start | bytes 491528 | tf_op jit(solution)/shard_map/ppermute | solution.py:608
  217.1 11.6 %collective-permute-done.23 = f32[16,2560]{1,0:T(8,128)S(1)} collective-permute-done((f32[16,2560]{1,0:T(8,128)S(1)}, f32[16,2560]{1,0:T(8,128)S(1)}, u32[]{:S(2)}, u32[]{:S(2)}) %collective-permute-start.23) | collective-permute-done | bytes 163872 | tf_op jit(solution)/shard_map/ppermute | solution.py:608
  228.7 0.7 slice_bitcast_fusion.2
  (67 shorter events, 2.3 us)
Async XLA Ops:
  3.1 13.9 %collective-permute-start = (f32[16,2560]{1,0:T(8,128)S(1)}, f32[16,2560]{1,0:T(8,128)S(1)}, u32[]{:S(2)}, u32[]{:S(2)}) collective-permute-start(f32[16,2560]{1,0:T(8,128)S(1)} %concatenate.60), channel_id=1, source_target_pairs={{0,0},{1,4},{2,8},{3,12},{4,1},{5,5},{6,9},{7,13},{8,2},{9,6},{10,... | collective-permute-start | bytes 491528 | tf_op jit(solution)/shard_map/ppermute | solution.py:410
  17.0 5.3 %collective-permute-start.4 = (f32[16,2560]{1,0:T(8,128)S(1)}, f32[16,2560]{1,0:T(8,128)S(1)}, u32[]{:S(2)}, u32[]{:S(2)}) collective-permute-start(f32[16,2560]{1,0:T(8,128)S(1)} %collective-permute-done.pack_ref.near_ref), channel_id=1, source_target_pairs={{0,2},{1,3},{2,0},{3,1},{4,6},{5,7},{6,4},{7,5},{8,10},{9,11},{10,... | collective-permute-start | bytes 491528 | tf_op jit(solution)/shard_map/ppermute | solution.py:398
  22.3 19.7 %collective-permute-start.5 = (f32[2,16,2560]{2,1,0:T(8,128)S(1)}, f32[2,16,2560]{2,1,0:T(8,128)S(1)}, u32[]{:S(2)}, u32[]{:S(2)}) collective-permute-start(f32[2,16,2560]{2,1,0:T(8,128)S(1)} %pad_maximum_fusion.2), channel_id=1, source_target_pairs={{0,1},{1,0},{2,3},{3,2},{4,5},{5,4},{6,7},{7,6},{8,9},{9,8},{10,11... | collective-permute-start | bytes 983048 | tf_op jit(solution)/shard_map/ppermute | solution.py:398
  40.0 1.9 copy-start
  84.9 1.6 collective-permute-start.6
  86.5 6.5 %collective-permute-start.7 = (f32[8,5120]{1,0:T(8,128)S(1)}, f32[8,5120]{1,0:T(8,128)S(1)}, u32[]{:S(2)}, u32[]{:S(2)}) collective-permute-start(f32[8,5120]{1,0:T(8,128)S(1)} %maximum_add_fusion), channel_id=1, source_target_pairs={{0,2},{1,3},{2,0},{3,1},{4,6},{5,7},{6,4},{7,5},{8,10},{9,11},{10,... | collective-permute-start | bytes 491528 | tf_op jit(solution)/shard_map/ppermute | solution.py:398
  93.1 1.5 collective-permute-start.8
  94.5 24.1 %copy-start.3 = (s32[4,2]{0,1:T(2,128)S(1)}, s32[4,2]{0,1:T(2,128)}, u32[]{:S(2)}) copy-start(s32[4,2]{0,1:T(2,128)} %param.13) | copy-start | bytes 100
  94.5 24.1 %copy-start.4 = (s32[4,2]{0,1:T(2,128)S(1)}, s32[4,2]{0,1:T(2,128)}, u32[]{:S(2)}) copy-start(s32[4,2]{0,1:T(2,128)} %param.11) | copy-start | bytes 100
  94.5 34.1 %copy-start.2 = (s32[4,2,32]{2,1,0:T(2,128)S(1)}, s32[4,2,32]{2,1,0:T(2,128)}, u32[]{:S(2)}) copy-start(s32[4,2,32]{2,1,0:T(2,128)} %param.12) | copy-start | bytes 3076
  116.8 1.5 collective-permute-start.9
  118.3 6.3 %collective-permute-start.10 = (f32[8,5120]{1,0:T(8,128)S(1)}, f32[8,5120]{1,0:T(8,128)S(1)}, u32[]{:S(2)}, u32[]{:S(2)}) collective-permute-start(f32[8,5120]{1,0:T(8,128)S(1)} %maximum_add_fusion.2), channel_id=1, source_target_pairs={{0,2},{1,3},{2,0},{3,1},{4,6},{5,7},{6,4},{7,5},{8,10},{9,11},{10,... | collective-permute-start | bytes 491528 | tf_op jit(solution)/shard_map/ppermute | solution.py:398
  124.7 4.1 %collective-permute-start.11 = (f32[8,5120]{1,0:T(8,128)S(1)}, f32[8,5120]{1,0:T(8,128)S(1)}, u32[]{:S(2)}, u32[]{:S(2)}) collective-permute-start(f32[8,5120]{1,0:T(8,128)S(1)} %maximum_add_fusion.3.even_ref), channel_id=1, source_target_pairs={{0,1},{1,0},{2,3},{3,2},{4,5},{5,4},{6,7},{7,6},{8,9},{9,8},{10,11... | collective-permute-start | bytes 491528 | tf_op jit(solution)/shard_map/ppermute | solution.py:398
  124.8 27.2 %copy-start.1 = (f8e4m3fn[2560,1536]{1,0:T(32,128)(4,1)S(1)}, f8e4m3fn[2560,1536]{1,0:T(32,128)(4,1)}, u32[]{:S(2)}) copy-start(f8e4m3fn[2560,1536]{1,0:T(32,128)(4,1)} %copy-done) | copy-start | bytes 11796484
  124.8 7.3 %collective-permute-start.1 = (f32[8,2560]{1,0:T(8,128)S(1)}, f32[8,2560]{1,0:T(8,128)S(1)}, u32[]{:S(2)}, u32[]{:S(2)}) collective-permute-start(f32[8,2560]{1,0:T(8,128)S(1)} %slice.132), channel_id=1, source_target_pairs={{0,4},{4,8},{8,12},{12,0},{1,5},{5,9},{9,13},{13,1},{2,6},{6,10},{... | collective-permute-start | bytes 245768 | tf_op jit(solution)/shard_map/ppermute | solution.py:574
  124.9 9.9 %collective-permute-start.2 = (f32[8,2560]{1,0:T(8,128)S(1)}, f32[8,2560]{1,0:T(8,128)S(1)}, u32[]{:S(2)}, u32[]{:S(2)}) collective-permute-start(f32[8,2560]{1,0:T(8,128)S(1)} %slice.132), channel_id=1, source_target_pairs={{0,8},{4,12},{8,0},{12,4},{1,9},{5,13},{9,1},{13,5},{2,10},{6,14},... | collective-permute-start | bytes 245768 | tf_op jit(solution)/shard_map/ppermute | solution.py:574
  125.8 9.0 %collective-permute-start.3 = (f32[8,2560]{1,0:T(8,128)S(1)}, f32[8,2560]{1,0:T(8,128)S(1)}, u32[]{:S(2)}, u32[]{:S(2)}) collective-permute-start(f32[8,2560]{1,0:T(8,128)S(1)} %slice.132), channel_id=1, source_target_pairs={{0,12},{4,0},{8,4},{12,8},{1,13},{5,1},{9,5},{13,9},{2,14},{6,2},{... | collective-permute-start | bytes 245768 | tf_op jit(solution)/shard_map/ppermute | solution.py:574
  129.0 8.4 %collective-permute-start.12 = (f32[8,2560]{1,0:T(8,128)S(1)}, f32[8,2560]{1,0:T(8,128)S(1)}, u32[]{:S(2)}, u32[]{:S(2)}) collective-permute-start(f32[8,2560]{1,0:T(8,128)S(1)} %slice.115), channel_id=1, source_target_pairs={{0,4},{4,8},{8,12},{12,0},{1,5},{5,9},{9,13},{13,1},{2,6},{6,10},{... | collective-permute-start | bytes 245768 | tf_op jit(solution)/shard_map/ppermute | solution.py:574
  129.6 12.0 %collective-permute-start.13 = (f32[8,2560]{1,0:T(8,128)S(1)}, f32[8,2560]{1,0:T(8,128)S(1)}, u32[]{:S(2)}, u32[]{:S(2)}) collective-permute-start(f32[8,2560]{1,0:T(8,128)S(1)} %slice.115), channel_id=1, source_target_pairs={{0,8},{4,12},{8,0},{12,4},{1,9},{5,13},{9,1},{13,5},{2,10},{6,14},... | collective-permute-start | bytes 245768 | tf_op jit(solution)/shard_map/ppermute | solution.py:574
  132.1 9.6 %collective-permute-start.14 = (f32[8,2560]{1,0:T(8,128)S(1)}, f32[8,2560]{1,0:T(8,128)S(1)}, u32[]{:S(2)}, u32[]{:S(2)}) collective-permute-start(f32[8,2560]{1,0:T(8,128)S(1)} %slice.115), channel_id=1, source_target_pairs={{0,12},{4,0},{8,4},{12,8},{1,13},{5,1},{9,5},{13,9},{2,14},{6,2},{... | collective-permute-start | bytes 245768 | tf_op jit(solution)/shard_map/ppermute | solution.py:574
  146.1 4.4 %collective-permute-start.15 = (f32[8,2560]{1,0:T(8,128)S(1)}, f32[8,2560]{1,0:T(8,128)S(1)}, u32[]{:S(2)}, u32[]{:S(2)}) collective-permute-start(f32[8,2560]{1,0:T(8,128)S(1)} %couple.1), channel_id=1, source_target_pairs={{0,2},{1,3},{2,0},{3,1},{4,6},{5,7},{6,4},{7,5},{8,10},{9,11},{10,... | collective-permute-start | bytes 245768 | tf_op jit(solution)/shard_map/ppermute | solution.py:398
  150.5 1.5 collective-permute-start.16
  173.4 1.5 collective-permute-start.17
  174.9 6.3 %collective-permute-start.18 = (f32[8,5120]{1,0:T(8,128)S(1)}, f32[8,5120]{1,0:T(8,128)S(1)}, u32[]{:S(2)}, u32[]{:S(2)}) collective-permute-start(f32[8,5120]{1,0:T(8,128)S(1)} %maximum_add_fusion.4), channel_id=1, source_target_pairs={{0,2},{1,3},{2,0},{3,1},{4,6},{5,7},{6,4},{7,5},{8,10},{9,11},{10,... | collective-permute-start | bytes 491528 | tf_op jit(solution)/shard_map/ppermute | solution.py:398
  181.3 1.5 collective-permute-start.19
  205.1 1.5 collective-permute-start.20
  206.5 6.3 %collective-permute-start.21 = (f32[8,5120]{1,0:T(8,128)S(1)}, f32[8,5120]{1,0:T(8,128)S(1)}, u32[]{:S(2)}, u32[]{:S(2)}) collective-permute-start(f32[8,5120]{1,0:T(8,128)S(1)} %maximum_add_fusion.6), channel_id=1, source_target_pairs={{0,2},{1,3},{2,0},{3,1},{4,6},{5,7},{6,4},{7,5},{8,10},{9,11},{10,... | collective-permute-start | bytes 491528 | tf_op jit(solution)/shard_map/ppermute | solution.py:398
  212.9 1.5 collective-permute-start.22
  214.6 14.1 %collective-permute-start.23 = (f32[16,2560]{1,0:T(8,128)S(1)}, f32[16,2560]{1,0:T(8,128)S(1)}, u32[]{:S(2)}, u32[]{:S(2)}) collective-permute-start(f32[16,2560]{1,0:T(8,128)S(1)} %pad_maximum_fusion.11), channel_id=1, source_target_pairs={{0,0},{1,4},{2,8},{3,12},{4,1},{5,5},{6,9},{7,13},{8,2},{9,6},{10,... | collective-permute-start | bytes 491528 | tf_op jit(solution)/shard_map/ppermute | solution.py:608

commit v3 on v2

--- a/solution.py
+++ b/solution.py
@@ -7,6 +7,7 @@
 from jax.experimental import pallas as pl
 from jax.experimental.pallas import tpu as pltpu
 from jax.sharding import PartitionSpec as P
+
 
 BLK = 32
 OUTER = 2
@@ -182,7 +183,7 @@
 
 def build_oth_kernel(
     parity_ref, left_ref, right_ref, own_ref, own_small_ref, own_undo_ref,
-    field_ref, small_ref, undo_ref, acc_in_ref,
+    field_ref, small_ref, undo_ref, acc_in_ref, far_ref,
     high_ref, low_ref, part_ref, dist, acc_own, acc_oth,
 ):
     i = pl.program_id(0)
@@ -224,9 +225,10 @@
         write_partial(part_ref, acc_own, acc_oth)
 
 
-def mr_step(even_ref, odd_ref, pack_ref, res_ref, cur_ref, new_res_ref, new_cur_ref):
+def step_kernel(even_ref, odd_ref, pack_ref, res_ref, *refs):
+    cur_ref = refs[0] if len(refs) == 4 else None
+    new_res_ref, new_cur_ref, alpha_ref = refs[-3:]
     count = even_ref.shape[1] // 2
-    image = []
     numerator = 0.0
     denominator = 0.0
     for b in range(4):
@@ -239,6 +241,7 @@
         numerator = numerator + jnp.sum(res * img, axis=1, keepdims=True)
         denominator = denominator + jnp.sum(img * img, axis=1, keepdims=True)
     alpha = numerator / (denominator + EPS)
+    alpha_ref[...] = jnp.broadcast_to(alpha, alpha_ref.shape)
     for b in range(4):
         cols = slice(b * count, (b + 1) * count)
         res = res_ref[:, cols]
@@ -249,24 +252,12 @@
         new_res_ref[:, cols] = res - alpha * new_res_ref[:, cols]
 
 
-def step_kernel(even_ref, odd_ref, pack_ref, res_ref, cur_ref, new_res_ref, new_cur_ref):
-    mr_step(even_ref, odd_ref, pack_ref, res_ref, cur_ref, new_res_ref, new_cur_ref)
-
-
-def apply_kernel(scale, first, couple, *refs):
-    refs = list(refs)
-    parity_ref = refs.pop(0)
-    even_ref, odd_ref, pack_ref, res_ref = refs[:4]
-    refs = refs[4:]
-    cur_ref = None if first or couple else refs.pop(0)
-    own_high, own_low, oth_high, oth_low = refs[:4]
-    refs = refs[4:]
-    new_res_ref = refs.pop(0)
-    new_cur_ref = None if couple else refs.pop(0)
-    part_ref, own_field, oth_field, own_small, oth_small, undos, acc_own, acc_oth = refs
-
+def apply_kernel(
+    scale, parity_ref, pack_ref, res_ref, own_high, own_low, oth_high, oth_low,
+    part_ref, own_field, oth_field, own_small, oth_small, undos, acc_own, acc_oth,
+):
     i = pl.program_id(0)
-    count = even_ref.shape[1] // 2
+    count = res_ref.shape[1] // 4
     half = count // 2
     here = pl.multiple_of(i * TILE, TILE)
 
@@ -274,18 +265,9 @@
     def _():
         acc_own[...] = jnp.zeros_like(acc_own)
         acc_oth[...] = jnp.zeros_like(acc_oth)
-        if couple:
-            for b in range(4):
-                source = odd_ref if b % 2 else even_ref
-                cols = slice(b * count, (b + 1) * count)
-                new_res_ref[:, cols] = (
-                    res_ref[:, cols] - source[:, (b // 2) * count : (b // 2 + 1) * count]
-                )
-        else:
-            mr_step(even_ref, odd_ref, pack_ref, res_ref, cur_ref, new_res_ref, new_cur_ref)
         for b in range(4):
             cols = slice(b * count, (b + 1) * count)
-            weighted = new_res_ref[:, cols] * (pack_ref[3:4, cols] * (scale / LIFT))
+            weighted = res_ref[:, cols] * (pack_ref[3:4, cols] * (scale / LIFT))
             field = two_pieces(weighted)
             small, undo = fp8_piece(weighted)
             undos[:, b * 128 : (b + 1) * 128] = jnp.broadcast_to(undo, (8, 128))
@@ -327,26 +309,32 @@
         write_partial(part_ref, acc_own, acc_oth)
 
 
-def couple_kernel(source_ref, list_ref, count_ref, first_ref, near_ref, far_ref, cur_ref, out_ref):
+def interface_product(field, high, low):
+    pieces = two_pieces(field)
+    return fold_pieces(nt(pieces, high) + nt(pieces, low))
+
+
+def couple_kernel(
+    source_ref, list_ref, count_ref, first_ref, near_ref, far_ref,
+    high_ref, low_ref, weight_ref, out_ref,
+):
     count = near_ref.shape[1]
+    slots = count_ref.shape[0]
     lane = lax.broadcasted_iota(jnp.int32, (1, count), 1)
     ident = first_ref[0] + lane // BLK
     row = lax.broadcasted_iota(jnp.int32, (128, 128), 0) // BLK
     col = lax.broadcasted_iota(jnp.int32, (128, 128), 1) // BLK
     same = row == col
-    total = None
-    weights = []
-    for slot in range(count_ref.shape[0]):
+    for slot in range(slots):
         hits = jnp.zeros((1, count), F32)
         for k in range(list_ref.shape[1]):
             hit = (ident == list_ref[slot, k]) & (k < count_ref[slot])
             hits = hits + jnp.where(hit, 1.0, 0.0)
-        weights.append(hits)
+        weight_ref[slot * 8 : slot * 8 + 8, :] = jnp.broadcast_to(hits, (8, count))
     for g in range(count // 128):
         cols = slice(g * 128, (g + 1) * 128)
         near = near_ref[:8, cols].T
-        total = jnp.zeros((8, 128), F32)
-        for slot in range(count_ref.shape[0]):
+        for slot in range(slots):
             far = far_ref[source_ref[slot], :, cols]
             squared = jnp.zeros((128, 128), F32)
             for x in range(3):
@@ -355,14 +343,32 @@
             safe = jnp.maximum(squared, 1e-30)
             radius = safe * lax.rsqrt(safe)
             tile = (cos_and_one(radius * WAVE, 1.0) - 1.0) / (1.0 + radius)
-            tile = jnp.where(same, tile, 0.0)
-            field = cur_ref[source_ref[slot], :, cols] * (far[3:4, :] * (COUPLE / math.sqrt(BLK)))
+            tile = jnp.where(same, tile * (far[3:4, :] * (COUPLE / math.sqrt(BLK))), 0.0)
             high = tile.astype(BF16)
             low = (tile - high.astype(F32)).astype(BF16)
-            pieces = two_pieces(field)
-            product = nt(pieces, high) + nt(pieces, low)
-            total = total + fold_pieces(product) * weights[slot][:, cols]
-        out_ref[:, cols] = total
+            high_ref[slot, cols, :] = high
+            low_ref[slot, cols, :] = low
+            rows = slice(slot * 8, slot * 8 + 8)
+            out_ref[rows, cols] = interface_product(far[8:], high, low) * weight_ref[rows, cols]
+
+
+def couple_again_kernel(source_ref, high_ref, low_ref, weight_ref, far_ref, out_ref):
+    for g in range(out_ref.shape[1] // 128):
+        cols = slice(g * 128, (g + 1) * 128)
+        for slot in range(source_ref.shape[0]):
+            rows = slice(slot * 8, slot * 8 + 8)
+            far = far_ref[source_ref[slot], :, cols]
+            product = interface_product(far, high_ref[slot, cols, :], low_ref[slot, cols, :])
+            out_ref[rows, cols] = product * weight_ref[rows, cols]
+
+
+def combine_kernel(source_ref, alpha_ref, first_ref, second_ref, out_ref):
+    total = 0.0
+    for slot in range(source_ref.shape[0]):
+        rows = slice(slot * 8, slot * 8 + 8)
+        alpha = alpha_ref[source_ref[slot]]
+        total = total + alpha[:8, :1] * first_ref[rows, :] + alpha[8:, :1] * second_ref[rows, :]
+    out_ref[...] = total
 
 
 def whole(shape):
@@ -371,6 +377,12 @@
 
 SMEM = pl.BlockSpec(memory_space=pltpu.SMEM)
 VMEM_LIMIT = 48 * 1024 * 1024
+
+
+def cost(microseconds):
+    return pl.CostEstimate(
+        flops=int(microseconds * 1e9), bytes_accessed=1000, transcendentals=0
+    )
 
 
 def params(**kw):
@@ -408,6 +420,22 @@
         axis=0,
     )
     pack = lax.ppermute(pack, ("row", "sub"), swap)
+
+    mine = jnp.arange(subs, dtype=jnp.int32) == plane
+    neighbours = jnp.sum(jnp.where(mine[:, None], adjacency, 0), axis=0)
+    lists = jnp.sum(jnp.where(mine[:, None, None], block_list, 0), axis=0)
+    counts = jnp.sum(jnp.where(mine[:, None], block_count, 0), axis=0)
+    source = jnp.maximum((plane - neighbours + subs) % subs - 1, 0)
+    first_block = (place * (count // BLK)).astype(jnp.int32).reshape(1)
+
+    def from_planes(x):
+        got = []
+        for k in range(1, ranks):
+            shift = [(z, (z + k) % ranks) for z in range(ranks)]
+            got.append(lax.ppermute(x, "row", shift))
+        return jnp.stack(got)
+
+    far = from_planes(pack)
 
     f32 = lambda *s: jax.ShapeDtypeStruct(s, F32)
     b16 = lambda *s: jax.ShapeDtypeStruct(s, BF16)
@@ -431,7 +459,7 @@
     packs_odd = send(packs, 1)
     full = jnp.concatenate([pack, packs_odd[0], pack2, packs_odd[1]], axis=1)
 
-    own_high, own_low, acc = pl.pallas_call(
+    build_own = pl.pallas_call(
         build_own_kernel,
         grid=(tiles,),
         in_specs=[
@@ -449,11 +477,10 @@
         out_shape=(b16(count, own_width), fp8(count, own_width), f32(8, 2 * count)),
         scratch_shapes=[pltpu.VMEM((TILE, own_width), F32)],
         compiler_params=params(),
-        cost_estimate=pl.CostEstimate(
-            flops=60 * count * own_width, bytes_accessed=4 * count * own_width, transcendentals=0
-        ),
+        cost_estimate=cost(17),
         name="build_own",
-    )(left, right_own, field_own, small_own, undo_own)
+    )
+    own_high, own_low, acc = build_own(left, right_own, field_own, small_own, undo_own)
 
     others = []
     for b in range(1, 4):
@@ -486,6 +513,7 @@
                 whole((8, 3 * count)),
                 whole((8, 3 * 128)),
                 whole((8, 2 * count)),
+                pl.BlockSpec(memory_space=pl.ANY),
             ],
             out_specs=(
                 pl.BlockSpec((TILE, 3 * half), lambda i, *_: (i, 0)),
@@ -500,10 +528,11 @@
         ),
         out_shape=(b16(count, 3 * half), fp8(count, 3 * half), f32(8, 4 * count)),
         compiler_params=params(),
+        cost_estimate=cost(42),
         name="build_oth",
     )(
         parity, left, right_oth, field_own, small_own, undo_own,
-        field_oth, small_oth, undo_oth, acc,
+        field_oth, small_oth, undo_oth, acc, far,
     )
 
     def pair(x, a, b):
@@ -519,30 +548,23 @@
         odd = send(even, 1)
         return even, odd
 
-    def apply(even, odd, res, cur, couple):
-        first = cur is None and not couple
-        operands = [even, odd, full, res]
-        specs = [
-            whole((8, 2 * count)),
-            whole((8, 2 * count)),
-            whole((16, 4 * count)),
-            whole((8, 4 * count)),
-        ]
-        if not first and not couple:
-            operands.append(cur)
-            specs.append(whole((8, 4 * count)))
+    def apply(res):
         own_spec = pl.BlockSpec((TILE, own_width), lambda i, *_: (i, 0))
         oth_spec = pl.BlockSpec((TILE, 3 * half), lambda i, *_: (i, 0))
-        operands += [own_high, own_low, oth_high, oth_low]
-        specs += [own_spec, own_spec, oth_spec, oth_spec]
-        outs = 2 if couple else 3
         return pl.pallas_call(
-            functools.partial(apply_kernel, scale, first, couple),
+            functools.partial(apply_kernel, scale),
             grid_spec=pltpu.PrefetchScalarGridSpec(
                 num_scalar_prefetch=1,
                 grid=(tiles,),
-                in_specs=specs,
-                out_specs=[whole((8, 4 * count))] * outs,
+                in_specs=[
+                    whole((16, 4 * count)),
+                    whole((8, 4 * count)),
+                    own_spec,
+                    own_spec,
+                    oth_spec,
+                    oth_spec,
+                ],
+                out_specs=whole((8, 4 * count)),
                 scratch_shapes=[
                     pltpu.VMEM((16, 2 * count), BF16),
                     pltpu.VMEM((16, 3 * count), BF16),
@@ -553,57 +575,69 @@
                     pltpu.VMEM((8, 3 * count), F32),
                 ],
             ),
-            out_shape=[f32(8, 4 * count)] * outs,
+            out_shape=f32(8, 4 * count),
             compiler_params=params(),
+            cost_estimate=cost(22),
             name="apply",
-        )(parity, *operands)
-
-    even, odd = reduce_all(part)
-    res, cur, part = apply(even, odd, full[8:], None, False)
-    even, odd = reduce_all(part)
-    res, cur = pl.pallas_call(
-        step_kernel,
-        out_shape=[f32(8, 4 * count)] * 2,
+        )(parity, full, res, own_high, own_low, oth_high, oth_low)
+
+    def step(part, res, *cur):
+        even, odd = reduce_all(part)
+        return pl.pallas_call(
+            step_kernel,
+            out_shape=[f32(8, 4 * count)] * 2 + [f32(8, 128)],
+            compiler_params=params(),
+            name="step",
+        )(even, odd, full, res, *cur)
+
+    slots = adjacency.shape[1]
+    vmem = pl.BlockSpec(memory_space=pltpu.VMEM)
+    tile_high, tile_low, weight, first_part = pl.pallas_call(
+        couple_kernel,
+        in_specs=[SMEM] * 4 + [vmem] * 2,
+        out_shape=(
+            b16(slots, count, 128),
+            b16(slots, count, 128),
+            f32(8 * slots, count),
+            f32(8 * slots, count),
+        ),
         compiler_params=params(),
-        name="step",
-    )(even, odd, full, res, cur)
-
-    def from_planes(x):
-        return jnp.stack(
-            [
-                lax.ppermute(x, "row", [(z, (z + k) % ranks) for z in range(ranks)])
-                for k in range(1, ranks)
-            ]
-        )
-
-    far = from_planes(pack[:8])
-    far_cur = from_planes(cur[:, :count])
-    mine = jnp.arange(subs, dtype=jnp.int32) == plane
-    neighbours = jnp.sum(jnp.where(mine[:, None], adjacency, 0), axis=0)
-    lists = jnp.sum(jnp.where(mine[:, None, None], block_list, 0), axis=0)
-    counts = jnp.sum(jnp.where(mine[:, None], block_count, 0), axis=0)
-    source = (plane - neighbours + subs) % subs - 1
-    first_block = (place * (count // BLK)).astype(jnp.int32).reshape(1)
+        cost_estimate=cost(4),
+        name="couple",
+    )(source, lists, counts, first_block, pack, far)
+
+    res, cur, alpha_first = step(part, full[8:])
+    far_res = from_planes(res[:, :count])
+    part = apply(res)
+    second_part = pl.pallas_call(
+        couple_again_kernel,
+        in_specs=[SMEM] + [vmem] * 4,
+        out_shape=f32(8 * slots, count),
+        compiler_params=params(),
+        cost_estimate=cost(1),
+        name="couple_again",
+    )(source, tile_high, tile_low, weight, far_res)
+    res, cur, alpha_second = step(part, res, cur)
     coupled = pl.pallas_call(
-        couple_kernel,
-        in_specs=[SMEM] * 4 + [pl.BlockSpec(memory_space=pltpu.VMEM)] * 3,
+        combine_kernel,
+        in_specs=[SMEM] + [vmem] * 3,
         out_shape=f32(8, count),
         compiler_params=params(),
-        name="couple",
-    )(source, lists, counts, first_block, pack, far, far_cur)
-    even = jnp.concatenate([coupled, send(coupled, 2)], axis=1)
-    odd = send(even, 1)
-
-    res, part = apply(even, odd, res, None, True)
-    even, odd = reduce_all(part)
-    res, cur, part = apply(even, odd, res, cur, False)
-    even, odd = reduce_all(part)
-    res, cur = pl.pallas_call(
-        step_kernel,
-        out_shape=[f32(8, 4 * count)] * 2,
-        compiler_params=params(),
-        name="step",
-    )(even, odd, full, res, cur)
+        name="combine",
+    )(
+        source,
+        from_planes(jnp.concatenate([alpha_first, alpha_second], axis=0)),
+        first_part,
+        second_part,
+    )
+    coupled_across = send(coupled, 2)
+    odd = send(jnp.concatenate([coupled, coupled_across], axis=1), 1)
+    res = res - jnp.concatenate(
+        [coupled, odd[:, :count], coupled_across, odd[:, count:]], axis=1
+    )
+
+    res, cur, _ = step(apply(res), res, cur)
+    res, cur, _ = step(apply(res), res, cur)
     out = jnp.concatenate([cur[:, :count], res[:, :count]], axis=0)
     out = lax.ppermute(out, ("row", "sub"), swap)
     return out[None, :8], out[None, 8:]
@@ -750,10 +784,13 @@
     )
     out_specs = (P(("body", "sub"), None, "row"), P(("body", "sub"), None, "row"))
     sizes = {name: mesh.shape[name] for name in ("row", "sub")}
-    return jax.shard_map(
+    step = jax.shard_map(
         functools.partial(on_device, sizes),
         mesh=mesh,
         in_specs=in_specs,
         out_specs=out_specs,
         check_vma=False,
     )
+    if sizes["row"] != sizes["sub"]:
+        return step
+    return step

time: 230 us -> 234 us (1.017)
  starting transfers between devices: 17.9 us -> 25.6 us
  waiting for transfers between devices: 73.5 us -> 67.9 us
    ppermute x16, waiting for transfers between devices: 43.9 us -> 29 us  [send(): return lax.ppermute(x, 'sub', over(bit))]
    ppermute x6 -> x9, waiting for transfers between devices: 8.54 us -> 19.7 us  [from_planes(): got.append(lax.ppermute(x, 'row', shift))]
    ppermute x16, starting transfers between devices: 3.03 us -> 7.57 us  [send(): return lax.ppermute(x, 'sub', over(bit))]
    pallas_call x7 -> x11, Pallas kernels: 87.8 us -> 90.1 us  [the longest x3 64 us: apply(): pl.pallas_call(functools.partial(apply_kernel, scale), grid_spec=pltpu.Pr...]
    ppermute x6 -> x9, starting transfers between devices: 7.98 us -> 9.9 us  [from_planes(): got.append(lax.ppermute(x, 'row', shift))]
  transfers between devices with their start and end apart: 24 -> 27, of which waited for: 20 -> 21; matrix products, arithmetic and copies ran while one was open for 0% -> 0% of each run, Pallas kernels for 8% -> 10%
where the time goes in v3:
time: 234 us
  Pallas kernels  133 us (57%)
  waiting for transfers between devices  67.9 us (29%)
  starting transfers between devices  25.6 us (11%)
  local copies, waits for them, and re-layouts  5.25 us (2%)
    pallas_call x3, Pallas kernels, apply(): pl.pallas_call(functools.partial(apply_kernel, scale), grid_spec=pltpu.Pr...  64 us
    pallas_call x1, Pallas kernels, on_plane(): pl.pallas_call(build_oth_kernel, grid_spec=pltpu.PrefetchScalarGridSpec(n...  42.1 us
    ppermute x16, waiting for transfers between devices, send(): return lax.ppermute(x, 'sub', over(bit))  29 us
    ppermute x9, waiting for transfers between devices, from_planes(): got.append(lax.ppermute(x, 'row', shift))  19.7 us
    pallas_call x1, Pallas kernels, on_plane(): build_own(left, right_own, field_own, small_own, undo_own)  17 us
    ppermute x1, waiting for transfers between devices, on_plane(): out = lax.ppermute(out, ('row', 'sub'), swap)  9.95 us
    ppermute x9, starting transfers between devices, from_planes(): got.append(lax.ppermute(x, 'row', shift))  9.9 us
    ppermute x1, waiting for transfers between devices, on_plane(): pack = lax.ppermute(pack, ('row', 'sub'), swap)  9.28 us
  transfers between devices with their start and end apart: 27, of which 21 were waited for; matrix products, arithmetic and copies ran while one was open for 0% of the time, Pallas kernels for 10%

profile of v3, /device:TPU:2, one launch (start us, length us, event | category | flops | bytes accessed | tf_op | source)
XLA Modules:
  0.0 234.0 jit_solution(9277590728533431444)
XLA Ops:
  0.6 0.8 copy.11
  1.4 1.7 concatenate.66
  3.1 4.5 %collective-permute-start = (f32[16,2560]{1,0:T(8,128)S(1)}, f32[16,2560]{1,0:T(8,128)S(1)}, u32[]{:S(2)}, u32[]{:S(2)}) collective-permute-start(f32[16,2560]{1,0:T(8,128)S(1)} %concatenate.66), channel_id=1, source_target_pairs={{0,0},{1,4},{2,8},{3,12},{4,1},{5,5},{6,9},{7,13},{8,2},{9,6},{10,... | collective-permute-start | bytes 491528 | tf_op jit(solution)/shard_map/ppermute | solution.py:422
  7.6 9.3 %collective-permute-done.pack_ref.near_ref = f32[16,2560]{1,0:T(8,128)S(1)} collective-permute-done((f32[16,2560]{1,0:T(8,128)S(1)}, f32[16,2560]{1,0:T(8,128)S(1)}, u32[]{:S(2)}, u32[]{:S(2)}) %collective-permute-start) | collective-permute-done | bytes 163872 | tf_op jit(solution)/shard_map/ppermute | solution.py:422
  17.3 17.0 %build_own.1 = (bf16[2560,1536]{1,0:T(8,128)(2,1)}, f8e4m3fn[2560,1536]{1,0:T(32,128)(4,1)S(1)}, f32[8,5120]{1,0:T(8,128)S(1)}) custom-call(bf16[2560,128]{1,0:T(8,128)(2,1)S(1)} %get-tuple-element.39.left_ref, bf16[96,5120]{1,0:T(8,128)(2,1)S(1)} %get-tuple-element.55.right_ref, bf16[16,5120]{1,0:T(8,128)(2,1)S(1)} %get-tuple-element.43.field_ref.own_ref, ...), custom_call_target="tpu_custom_call" | custom-call | flops 16999999488 | bytes 1000 | tf_op jit(solution)/shard_map/build_own/pallas_call | solution.py:483
  34.4 1.9 copy-done
  36.2 1.0 collective-permute-start.5
  37.2 1.0 collective-permute-start.3
  39.0 2.5 %collective-permute-done.5 = f32[16,2560]{1,0:T(8,128)S(1)} collective-permute-done((f32[16,2560]{1,0:T(8,128)S(1)}, f32[16,2560]{1,0:T(8,128)S(1)}, u32[]{:S(2)}, u32[]{:S(2)}) %collective-permute-start.5) | collective-permute-done | bytes 163872 | tf_op jit(solution)/shard_map/ppermute | solution.py:435
  41.6 4.6 %collective-permute-done.3 = f32[16,2560]{1,0:T(8,128)S(1)} collective-permute-done((f32[16,2560]{1,0:T(8,128)S(1)}, f32[16,2560]{1,0:T(8,128)S(1)}, u32[]{:S(2)}, u32[]{:S(2)}) %collective-permute-start.3) | collective-permute-done | bytes 163872 | tf_op jit(solution)/shard_map/ppermute | solution.py:435
  46.2 6.3 %collective-permute-done.4 = f32[16,2560]{1,0:T(8,128)S(1)} collective-permute-done((f32[16,2560]{1,0:T(8,128)S(1)}, f32[16,2560]{1,0:T(8,128)S(1)}, u32[]{:S(2)}, u32[]{:S(2)}) %collective-permute-start.4) | collective-permute-done | bytes 163872 | tf_op jit(solution)/shard_map/ppermute | solution.py:435
  53.2 42.1 %build_oth.1 = (bf16[2560,3840]{1,0:T(8,128)(2,1)}, f8e4m3fn[2560,3840]{1,0:T(32,128)(4,1)}, f32[8,10240]{1,0:T(8,128)S(1)}) custom-call(s32[3]{0:T(128)S(1)} %add_convert_fusion.parity_ref, bf16[2560,128]{1,0:T(8,128)(2,1)S(1)} %get-tuple-element.39.left_ref, bf16[96,7680]{1,0:T(8,128)(2,1)S(1)} %pad_maximum_fusion.right_ref, ...), custom_call_target="tpu_custom_call" | custom-call | flops 41999998976 | bytes 1000 | tf_op jit(solution)/shard_map/build_oth/pallas_call | solution.py:501
  95.4 1.4 collective-permute-done.6
  96.8 1.2 collective-permute-start.7
  98.2 5.0 %collective-permute-done.7 = f32[8,5120]{1,0:T(8,128)S(1)} collective-permute-done((f32[8,5120]{1,0:T(8,128)S(1)}, f32[8,5120]{1,0:T(8,128)S(1)}, u32[]{:S(2)}, u32[]{:S(2)}) %collective-permute-start.7) | collective-permute-done | bytes 163872 | tf_op jit(solution)/shard_map/ppermute | solution.py:410
  103.3 1.3 collective-permute-done.8.odd_ref
  104.9 21.3 %apply.3 = f32[8,10240]{1,0:T(8,128)S(1)} custom-call(s32[3]{0:T(128)S(1)} %add_convert_fusion.parity_ref, f32[16,10240]{1,0:T(8,128)S(1)} %pad_maximum_fusion.1.pack_ref, f32[8,10240]{1,0:T(8,128)S(1)} %get-tuple-element.58.res_ref, bf16[2560,1536]{1,0:T(8,128)(2,1)} %get-tuple-element.59.own_high, f8e4m3fn[2560,1536]{1,0:T(32,128)(4,1)S(1)} %copy-done.1, ...), custom_call_target="tpu_custom_call" | custom-call | flops 22000001024 | bytes 1000 | tf_op jit(solution)/shard_map/apply/pallas_call | solution.py:554
  126.6 1.1 collective-permute-done.9
  127.7 1.2 collective-permute-start.10
  128.9 4.5 %couple.1 = (bf16[2,2560,128]{2,1,0:T(8,128)(2,1)S(1)}, bf16[2,2560,128]{2,1,0:T(8,128)(2,1)S(1)}, f32[16,2560]{1,0:T(8,128)S(1)}, f32[16,2560]{1,0:T(8,128)S(1)}) custom-call(s32[2]{0:T(128)S(1)} %fusion.1.source_ref, s32[2,32]{1,0:T(2,128)S(1)} %select_reduce_fusion.list_ref, s32[2]{0:T(128)S(1)} %get-tuple-element.76.count_ref, s32[1]{0:T(128)} %bitcast.14.first_ref, ...), custom_call_target="tpu_custom_call" | custom-call | flops 4000000000 | bytes 1000 | tf_op jit(solution)/shard_map/couple/pallas_call | solution.py:595
  133.5 2.7 %collective-permute-start.16 = (f32[8,2560]{1,0:T(8,128)S(1)}, f32[8,2560]{1,0:T(8,128)S(1)}, u32[]{:S(2)}, u32[]{:S(2)}) collective-permute-start(f32[8,2560]{1,0:T(8,128)S(1)} %slice.117), channel_id=1, source_target_pairs={{0,8},{4,12},{8,0},{12,4},{1,9},{5,13},{9,1},{13,5},{2,10},{6,14},... | collective-permute-start | bytes 245768 | tf_op jit(solution)/shard_map/ppermute | solution.py:435
  136.2 1.1 collective-permute-start.17
  137.4 3.2 %collective-permute-done.15 = f32[8,2560]{1,0:T(8,128)S(1)} collective-permute-done((f32[8,2560]{1,0:T(8,128)S(1)}, f32[8,2560]{1,0:T(8,128)S(1)}, u32[]{:S(2)}, u32[]{:S(2)}) %collective-permute-start.15) | collective-permute-done | bytes 81952 | tf_op jit(solution)/shard_map/ppermute | solution.py:435
  140.6 2.4 %collective-permute-done.16 = f32[8,2560]{1,0:T(8,128)S(1)} collective-permute-done((f32[8,2560]{1,0:T(8,128)S(1)}, f32[8,2560]{1,0:T(8,128)S(1)}, u32[]{:S(2)}, u32[]{:S(2)}) %collective-permute-start.16) | collective-permute-done | bytes 81952 | tf_op jit(solution)/shard_map/ppermute | solution.py:435
  143.3 1.5 collective-permute-start.12
  144.8 1.5 collective-permute-start.13
  146.3 1.0 collective-permute-start.14
  147.3 2.0 couple_again.1.second_ref
  149.4 0.6 collective-permute-done.14
  150.0 0.6 combine.1
  150.6 1.2 collective-permute-start.18
  151.8 3.3 %collective-permute-done.18 = f32[8,2560]{1,0:T(8,128)S(1)} collective-permute-done((f32[8,2560]{1,0:T(8,128)S(1)}, f32[8,2560]{1,0:T(8,128)S(1)}, u32[]{:S(2)}, u32[]{:S(2)}) %collective-permute-start.18) | collective-permute-done | bytes 81952 | tf_op jit(solution)/shard_map/ppermute | solution.py:410
  155.2 1.4 collective-permute-done.19
  156.7 21.3 %apply.4 = f32[8,10240]{1,0:T(8,128)S(1)} custom-call(s32[3]{0:T(128)S(1)} %add_convert_fusion.parity_ref, f32[16,10240]{1,0:T(8,128)S(1)} %pad_maximum_fusion.1.pack_ref, f32[8,10240]{1,0:T(8,128)S(1)} %maximum_subtract_fusion.res_ref, bf16[2560,1536]{1,0:T(8,128)(2,1)} %get-tuple-element.59.own_high, f8e4m3fn[2560,1536]{1,0:T(32,128)(4,1)S(1)} %copy-done.2, ...), custom_call_target="tpu_custom_call" | custom-call | flops 22000001024 | bytes 1000 | tf_op jit(solution)/shard_map/apply/pallas_call | solution.py:554
  178.3 1.3 collective-permute-done.20
  179.6 1.2 collective-permute-start.21
  180.7 5.1 %collective-permute-done.21 = f32[8,5120]{1,0:T(8,128)S(1)} collective-permute-done((f32[8,5120]{1,0:T(8,128)S(1)}, f32[8,5120]{1,0:T(8,128)S(1)}, u32[]{:S(2)}, u32[]{:S(2)}) %collective-permute-start.21) | collective-permute-done | bytes 163872 | tf_op jit(solution)/shard_map/ppermute | solution.py:410
  186.0 1.4 collective-permute-done.22.odd_ref
  187.4 0.8 step.6
  188.2 21.3 %apply.5 = f32[8,10240]{1,0:T(8,128)S(1)} custom-call(s32[3]{0:T(128)S(1)} %add_convert_fusion.parity_ref, f32[16,10240]{1,0:T(8,128)S(1)} %pad_maximum_fusion.1.pack_ref, f32[8,10240]{1,0:T(8,128)S(1)} %get-tuple-element.72.res_ref, bf16[2560,1536]{1,0:T(8,128)(2,1)} %get-tuple-element.59.own_high, f8e4m3fn[2560,1536]{1,0:T(32,128)(4,1)S(1)} %copy-done.2, ...), custom_call_target="tpu_custom_call" | custom-call | flops 22000001024 | bytes 1000 | tf_op jit(solution)/shard_map/apply/pallas_call | solution.py:554
  209.8 1.3 collective-permute-done.23
  211.0 1.2 collective-permute-start.24
  212.2 5.1 %collective-permute-done.24 = f32[8,5120]{1,0:T(8,128)S(1)} collective-permute-done((f32[8,5120]{1,0:T(8,128)S(1)}, f32[8,5120]{1,0:T(8,128)S(1)}, u32[]{:S(2)}, u32[]{:S(2)}) %collective-permute-start.24) | collective-permute-done | bytes 163872 | tf_op jit(solution)/shard_map/ppermute | solution.py:410
  217.5 1.4 collective-permute-done.25.odd_ref
  218.9 0.8 step.7
  219.7 3.7 %collective-permute-start.26 = (f32[16,2560]{1,0:T(8,128)S(1)}, f32[16,2560]{1,0:T(8,128)S(1)}, u32[]{:S(2)}, u32[]{:S(2)}) collective-permute-start(f32[16,2560]{1,0:T(8,128)S(1)} %pad_maximum_fusion.11), channel_id=1, source_target_pairs={{0,0},{1,4},{2,8},{3,12},{4,1},{5,5},{6,9},{7,13},{8,2},{9,6},{10,... | collective-permute-start | bytes 491528 | tf_op jit(solution)/shard_map/ppermute | solution.py:642
  223.4 9.9 %collective-permute-done.26 = f32[16,2560]{1,0:T(8,128)S(1)} collective-permute-done((f32[16,2560]{1,0:T(8,128)S(1)}, f32[16,2560]{1,0:T(8,128)S(1)}, u32[]{:S(2)}, u32[]{:S(2)}) %collective-permute-start.26) | collective-permute-done | bytes 163872 | tf_op jit(solution)/shard_map/ppermute | solution.py:642
  233.3 0.7 slice_bitcast_fusion.2
  (83 shorter events, 4.4 us)
Async XLA Ops:
  3.1 13.8 %collective-permute-start = (f32[16,2560]{1,0:T(8,128)S(1)}, f32[16,2560]{1,0:T(8,128)S(1)}, u32[]{:S(2)}, u32[]{:S(2)}) collective-permute-start(f32[16,2560]{1,0:T(8,128)S(1)} %concatenate.66), channel_id=1, source_target_pairs={{0,0},{1,4},{2,8},{3,12},{4,1},{5,5},{6,9},{7,13},{8,2},{9,6},{10,... | collective-permute-start | bytes 491528 | tf_op jit(solution)/shard_map/ppermute | solution.py:422
  17.2 21.0 %collective-permute-start.1 = (f32[16,2560]{1,0:T(8,128)S(1)}, f32[16,2560]{1,0:T(8,128)S(1)}, u32[]{:S(2)}, u32[]{:S(2)}) collective-permute-start(f32[16,2560]{1,0:T(8,128)S(1)} %collective-permute-done.pack_ref.near_ref), channel_id=1, source_target_pairs={{0,2},{1,3},{2,0},{3,1},{4,6},{5,7},{6,4},{7,5},{8,10},{9,11},{10,... | collective-permute-start | bytes 491528 | tf_op jit(solution)/shard_map/ppermute | solution.py:410
  34.4 1.9 copy-start
  36.2 5.3 %collective-permute-start.5 = (f32[16,2560]{1,0:T(8,128)S(1)}, f32[16,2560]{1,0:T(8,128)S(1)}, u32[]{:S(2)}, u32[]{:S(2)}) collective-permute-start(f32[16,2560]{1,0:T(8,128)S(1)} %collective-permute-done.pack_ref.near_ref), channel_id=1, source_target_pairs={{0,12},{4,0},{8,4},{12,8},{1,13},{5,1},{9,5},{13,9},{2,14},{6,2},{... | collective-permute-start | bytes 491528 | tf_op jit(solution)/shard_map/ppermute | solution.py:435
  37.2 9.0 %collective-permute-start.3 = (f32[16,2560]{1,0:T(8,128)S(1)}, f32[16,2560]{1,0:T(8,128)S(1)}, u32[]{:S(2)}, u32[]{:S(2)}) collective-permute-start(f32[16,2560]{1,0:T(8,128)S(1)} %collective-permute-done.pack_ref.near_ref), channel_id=1, source_target_pairs={{0,4},{4,8},{8,12},{12,0},{1,5},{5,9},{9,13},{13,1},{2,6},{6,10},{... | collective-permute-start | bytes 491528 | tf_op jit(solution)/shard_map/ppermute | solution.py:435
  38.3 14.2 %collective-permute-start.4 = (f32[16,2560]{1,0:T(8,128)S(1)}, f32[16,2560]{1,0:T(8,128)S(1)}, u32[]{:S(2)}, u32[]{:S(2)}) collective-permute-start(f32[16,2560]{1,0:T(8,128)S(1)} %collective-permute-done.pack_ref.near_ref), channel_id=1, source_target_pairs={{0,8},{4,12},{8,0},{12,4},{1,9},{5,13},{9,1},{13,5},{2,10},{6,14},... | collective-permute-start | bytes 491528 | tf_op jit(solution)/shard_map/ppermute | solution.py:435
  38.3 14.2 %collective-permute-start.2 = (f32[2,16,2560]{2,1,0:T(8,128)S(1)}, f32[2,16,2560]{2,1,0:T(8,128)S(1)}, u32[]{:S(2)}, u32[]{:S(2)}) collective-permute-start(f32[2,16,2560]{2,1,0:T(8,128)S(1)} %pad_maximum_fusion.3), channel_id=1, source_target_pairs={{0,1},{1,0},{2,3},{3,2},{4,5},{5,4},{6,7},{7,6},{8,9},{9,8},{10,11... | collective-permute-start | bytes 983048 | tf_op jit(solution)/shard_map/ppermute | solution.py:410
  53.2 44.8 %copy-start.4 = (s32[4,2]{0,1:T(2,128)S(1)}, s32[4,2]{0,1:T(2,128)}, u32[]{:S(2)}) copy-start(s32[4,2]{0,1:T(2,128)} %param.13) | copy-start | bytes 100
  53.2 44.8 %copy-start.5 = (s32[4,2]{0,1:T(2,128)S(1)}, s32[4,2]{0,1:T(2,128)}, u32[]{:S(2)}) copy-start(s32[4,2]{0,1:T(2,128)} %param.11) | copy-start | bytes 100
  95.3 1.5 collective-permute-start.6
  95.4 9.4 %copy-start.1 = (f8e4m3fn[2560,1536]{1,0:T(32,128)(4,1)S(1)}, f8e4m3fn[2560,1536]{1,0:T(32,128)(4,1)}, u32[]{:S(2)}) copy-start(f8e4m3fn[2560,1536]{1,0:T(32,128)(4,1)} %copy-done) | copy-start | bytes 11796484
  96.8 6.3 %collective-permute-start.7 = (f32[8,5120]{1,0:T(8,128)S(1)}, f32[8,5120]{1,0:T(8,128)S(1)}, u32[]{:S(2)}, u32[]{:S(2)}) collective-permute-start(f32[8,5120]{1,0:T(8,128)S(1)} %maximum_add_fusion), channel_id=1, source_target_pairs={{0,2},{1,3},{2,0},{3,1},{4,6},{5,7},{6,4},{7,5},{8,10},{9,11},{10,... | collective-permute-start | bytes 491528 | tf_op jit(solution)/shard_map/ppermute | solution.py:410
  103.2 1.5 collective-permute-start.8
  104.8 21.6 %copy-start.3 = (s32[4,2,32]{2,1,0:T(2,128)S(1)}, s32[4,2,32]{2,1,0:T(2,128)}, u32[]{:S(2)}) copy-start(s32[4,2,32]{2,1,0:T(2,128)} %param.12) | copy-start | bytes 3076
  126.3 1.5 collective-permute-start.9
  127.7 9.6 %collective-permute-start.10 = (f32[8,5120]{1,0:T(8,128)S(1)}, f32[8,5120]{1,0:T(8,128)S(1)}, u32[]{:S(2)}, u32[]{:S(2)}) collective-permute-start(f32[8,5120]{1,0:T(8,128)S(1)} %maximum_add_fusion.2), channel_id=1, source_target_pairs={{0,2},{1,3},{2,0},{3,1},{4,6},{5,7},{6,4},{7,5},{8,10},{9,11},{10,... | collective-permute-start | bytes 491528 | tf_op jit(solution)/shard_map/ppermute | solution.py:410
  133.4 7.2 %collective-permute-start.15 = (f32[8,2560]{1,0:T(8,128)S(1)}, f32[8,2560]{1,0:T(8,128)S(1)}, u32[]{:S(2)}, u32[]{:S(2)}) collective-permute-start(f32[8,2560]{1,0:T(8,128)S(1)} %slice.117), channel_id=1, source_target_pairs={{0,4},{4,8},{8,12},{12,0},{1,5},{5,9},{9,13},{13,1},{2,6},{6,10},{... | collective-permute-start | bytes 245768 | tf_op jit(solution)/shard_map/ppermute | solution.py:435
  133.5 9.5 %collective-permute-start.16 = (f32[8,2560]{1,0:T(8,128)S(1)}, f32[8,2560]{1,0:T(8,128)S(1)}, u32[]{:S(2)}, u32[]{:S(2)}) collective-permute-start(f32[8,2560]{1,0:T(8,128)S(1)} %slice.117), channel_id=1, source_target_pairs={{0,8},{4,12},{8,0},{12,4},{1,9},{5,13},{9,1},{13,5},{2,10},{6,14},... | collective-permute-start | bytes 245768 | tf_op jit(solution)/shard_map/ppermute | solution.py:435
  136.2 6.8 %collective-permute-start.17 = (f32[8,2560]{1,0:T(8,128)S(1)}, f32[8,2560]{1,0:T(8,128)S(1)}, u32[]{:S(2)}, u32[]{:S(2)}) collective-permute-start(f32[8,2560]{1,0:T(8,128)S(1)} %slice.117), channel_id=1, source_target_pairs={{0,12},{4,0},{8,4},{12,8},{1,13},{5,1},{9,5},{13,9},{2,14},{6,2},{... | collective-permute-start | bytes 245768 | tf_op jit(solution)/shard_map/ppermute | solution.py:435
  137.3 5.7 %collective-permute-start.11 = (f32[8,5120]{1,0:T(8,128)S(1)}, f32[8,5120]{1,0:T(8,128)S(1)}, u32[]{:S(2)}, u32[]{:S(2)}) collective-permute-start(f32[8,5120]{1,0:T(8,128)S(1)} %maximum_add_fusion.3.even_ref), channel_id=1, source_target_pairs={{0,1},{1,0},{2,3},{3,2},{4,5},{5,4},{6,7},{7,6},{8,9},{9,8},{10,11... | collective-permute-start | bytes 491528 | tf_op jit(solution)/shard_map/ppermute | solution.py:410
  143.3 13.4 %copy-start.2 = (f8e4m3fn[2560,1536]{1,0:T(32,128)(4,1)S(1)}, f8e4m3fn[2560,1536]{1,0:T(32,128)(4,1)}, u32[]{:S(2)}) copy-start(f8e4m3fn[2560,1536]{1,0:T(32,128)(4,1)} %copy-done) | copy-start | bytes 11796484
  143.3 6.0 %collective-permute-start.12 = (f32[16,128]{1,0:T(8,128)S(1)}, f32[16,128]{1,0:T(8,128)S(1)}, u32[]{:S(2)}, u32[]{:S(2)}) collective-permute-start(f32[16,128]{1,0:T(8,128)S(1)} %constant_dynamic-update-slice_fusion), channel_id=1, source_target_pairs={{0,4},{4,8},{8,12},{12,0},{1,5},{5,9},{9,13},{13,1},{2,6},{6,10},{... | collective-permute-start | bytes 24584 | tf_op jit(solution)/shard_map/ppermute | solution.py:435
  144.8 4.5 %collective-permute-start.13 = (f32[16,128]{1,0:T(8,128)S(1)}, f32[16,128]{1,0:T(8,128)S(1)}, u32[]{:S(2)}, u32[]{:S(2)}) collective-permute-start(f32[16,128]{1,0:T(8,128)S(1)} %constant_dynamic-update-slice_fusion), channel_id=1, source_target_pairs={{0,8},{4,12},{8,0},{12,4},{1,9},{5,13},{9,1},{13,5},{2,10},{6,14},... | collective-permute-start | bytes 24584 | tf_op jit(solution)/shard_map/ppermute | solution.py:435
  146.3 3.7 %collective-permute-start.14 = (f32[16,128]{1,0:T(8,128)S(1)}, f32[16,128]{1,0:T(8,128)S(1)}, u32[]{:S(2)}, u32[]{:S(2)}) collective-permute-start(f32[16,128]{1,0:T(8,128)S(1)} %constant_dynamic-update-slice_fusion), channel_id=1, source_target_pairs={{0,12},{4,0},{8,4},{12,8},{1,13},{5,1},{9,5},{13,9},{2,14},{6,2},{... | collective-permute-start | bytes 24584 | tf_op jit(solution)/shard_map/ppermute | solution.py:435
  150.6 4.5 %collective-permute-start.18 = (f32[8,2560]{1,0:T(8,128)S(1)}, f32[8,2560]{1,0:T(8,128)S(1)}, u32[]{:S(2)}, u32[]{:S(2)}) collective-permute-start(f32[8,2560]{1,0:T(8,128)S(1)} %combine.1), channel_id=1, source_target_pairs={{0,2},{1,3},{2,0},{3,1},{4,6},{5,7},{6,4},{7,5},{8,10},{9,11},{10,... | collective-permute-start | bytes 245768 | tf_op jit(solution)/shard_map/ppermute | solution.py:410
  155.1 1.5 collective-permute-start.19
  178.1 1.5 collective-permute-start.20
  179.6 6.3 %collective-permute-start.21 = (f32[8,5120]{1,0:T(8,128)S(1)}, f32[8,5120]{1,0:T(8,128)S(1)}, u32[]{:S(2)}, u32[]{:S(2)}) collective-permute-start(f32[8,5120]{1,0:T(8,128)S(1)} %maximum_add_fusion.4), channel_id=1, source_target_pairs={{0,2},{1,3},{2,0},{3,1},{4,6},{5,7},{6,4},{7,5},{8,10},{9,11},{10,... | collective-permute-start | bytes 491528 | tf_op jit(solution)/shard_map/ppermute | solution.py:410
  185.9 1.5 collective-permute-start.22
  209.6 1.5 collective-permute-start.23
  211.0 6.3 %collective-permute-start.24 = (f32[8,5120]{1,0:T(8,128)S(1)}, f32[8,5120]{1,0:T(8,128)S(1)}, u32[]{:S(2)}, u32[]{:S(2)}) collective-permute-start(f32[8,5120]{1,0:T(8,128)S(1)} %maximum_add_fusion.6), channel_id=1, source_target_pairs={{0,2},{1,3},{2,0},{3,1},{4,6},{5,7},{6,4},{7,5},{8,10},{9,11},{10,... | collective-permute-start | bytes 491528 | tf_op jit(solution)/shard_map/ppermute | solution.py:410
  217.4 1.5 collective-permute-start.25
  219.7 13.7 %collective-permute-start.26 = (f32[16,2560]{1,0:T(8,128)S(1)}, f32[16,2560]{1,0:T(8,128)S(1)}, u32[]{:S(2)}, u32[]{:S(2)}) collective-permute-start(f32[16,2560]{1,0:T(8,128)S(1)} %pad_maximum_fusion.11), channel_id=1, source_target_pairs={{0,0},{1,4},{2,8},{3,12},{4,1},{5,5},{6,9},{7,13},{8,2},{9,6},{10,... | collective-permute-start | bytes 491528 | tf_op jit(solution)/shard_map/ppermute | solution.py:642

commit v4 on v3

--- a/solution.py
+++ b/solution.py
@@ -101,6 +101,14 @@
     return lax.dot_general(left, right, (((1,), (1,)), ((), ())), preferred_element_type=F32)
 
 
+def pack_kernel(positions_ref, area_ref, term_ref, excitation_ref, pack_ref):
+    pack_ref[0:3, :] = positions_ref[0]
+    pack_ref[3:4, :] = area_ref[...]
+    pack_ref[4:5, :] = term_ref[...]
+    pack_ref[5:8, :] = jnp.zeros((3, pack_ref.shape[1]), F32)
+    pack_ref[8:16, :] = excitation_ref[0]
+
+
 def prep_kernel(scale, doubled, pack_ref, left_ref, right_ref, field_ref, small_ref, undo_ref):
     pack = pack_ref[...]
     count = pack.shape[1]
@@ -183,7 +191,7 @@
 
 def build_oth_kernel(
     parity_ref, left_ref, right_ref, own_ref, own_small_ref, own_undo_ref,
-    field_ref, small_ref, undo_ref, acc_in_ref, far_ref,
+    field_ref, small_ref, undo_ref, acc_in_ref,
     high_ref, low_ref, part_ref, dist, acc_own, acc_oth,
 ):
     i = pl.program_id(0)
@@ -409,16 +417,12 @@
     def send(x, bit):
         return lax.ppermute(x, "sub", over(bit))
 
-    pack = jnp.concatenate(
-        [
-            positions[0],
-            panel_area,
-            self_term,
-            jnp.zeros((3, count), F32),
-            excitation[0],
-        ],
-        axis=0,
-    )
+    pack = pl.pallas_call(
+        pack_kernel,
+        out_shape=jax.ShapeDtypeStruct((16, count), F32),
+        compiler_params=params(),
+        name="pack",
+    )(positions, panel_area, self_term, excitation)
     pack = lax.ppermute(pack, ("row", "sub"), swap)
 
     mine = jnp.arange(subs, dtype=jnp.int32) == plane
@@ -454,10 +458,10 @@
         name="prep_own",
     )(pack)
 
-    pack2 = send(pack, 2)
-    packs = jnp.stack([pack, pack2])
-    packs_odd = send(packs, 1)
-    full = jnp.concatenate([pack, packs_odd[0], pack2, packs_odd[1]], axis=1)
+    blocks = [pack]
+    for bit in range(1, subs):
+        blocks.append(send(pack, bit))
+    full = jnp.concatenate(blocks, axis=1)
 
     build_own = pl.pallas_call(
         build_own_kernel,
@@ -490,7 +494,7 @@
                 out_shape=(b16(FEATURES, count), b16(16, count), fp8(8, count), f32(8, 128)),
                 compiler_params=params(),
                 name="prep_oth",
-            )(full[:, b * count : (b + 1) * count])
+            )(blocks[b])
         )
     right_oth, field_oth, small_oth, undo_oth = (
         jnp.concatenate(parts, axis=1) for parts in zip(*others)
@@ -498,7 +502,7 @@
 
     parity = jnp.stack([(place > (place ^ b)).astype(jnp.int32) for b in range(1, 4)])
 
-    oth_high, oth_low, part = pl.pallas_call(
+    build_oth = pl.pallas_call(
         build_oth_kernel,
         grid_spec=pltpu.PrefetchScalarGridSpec(
             num_scalar_prefetch=1,
@@ -513,7 +517,6 @@
                 whole((8, 3 * count)),
                 whole((8, 3 * 128)),
                 whole((8, 2 * count)),
-                pl.BlockSpec(memory_space=pl.ANY),
             ],
             out_specs=(
                 pl.BlockSpec((TILE, 3 * half), lambda i, *_: (i, 0)),
@@ -530,9 +533,10 @@
         compiler_params=params(),
         cost_estimate=cost(42),
         name="build_oth",
-    )(
+    )
+    oth_high, oth_low, part = build_oth(
         parity, left, right_oth, field_own, small_own, undo_own,
-        field_oth, small_oth, undo_oth, acc, far,
+        field_oth, small_oth, undo_oth, acc,
     )
 
     def pair(x, a, b):
@@ -592,7 +596,7 @@
 
     slots = adjacency.shape[1]
     vmem = pl.BlockSpec(memory_space=pltpu.VMEM)
-    tile_high, tile_low, weight, first_part = pl.pallas_call(
+    interface = pl.pallas_call(
         couple_kernel,
         in_specs=[SMEM] * 4 + [vmem] * 2,
         out_shape=(
@@ -604,7 +608,10 @@
         compiler_params=params(),
         cost_estimate=cost(4),
         name="couple",
-    )(source, lists, counts, first_block, pack, far)
+    )
+    tile_high, tile_low, weight, first_part = interface(
+        source, lists, counts, first_block, pack, far
+    )
 
     res, cur, alpha_first = step(part, full[8:])
     far_res = from_planes(res[:, :count])

time: 234 us -> 226 us (0.966)
  waiting for transfers between devices: 67.9 us -> 54.5 us
  starting transfers between devices: 25.6 us -> 30.4 us
    ppermute x9, waiting for transfers between devices: 19.7 us -> 5.93 us  [from_planes(): got.append(lax.ppermute(x, 'row', shift))]
    ppermute x16 -> x17, waiting for transfers between devices: 29 us -> 31.9 us  [send(): return lax.ppermute(x, 'sub', over(bit))]
    ppermute x16 -> x17, starting transfers between devices: 7.57 us -> 9.32 us  [send(): return lax.ppermute(x, 'sub', over(bit))]
    pallas_call x2 -> x3, Pallas kernels: 46.5 us -> 46.5 us  [the longest x1 42 us: on_plane(): build_oth(parity, left, right_oth, field_own, small_own, undo_own, field_...]
  transfers between devices with their start and end apart: 27 -> 28, of which waited for: 21 -> 20; matrix products, arithmetic and copies ran while one was open for 0% -> 1% of each run, Pallas kernels for 10% -> 31%
where the time goes in v4:
time: 226 us; the launch traced here: 225 us
  Pallas kernels  133 us (59%)
  waiting for transfers between devices  54.5 us (24%)
  starting transfers between devices  30.4 us (13%)
  local copies, waits for them, and re-layouts  3.97 us (2%)
    pallas_call x3, Pallas kernels, apply(): pl.pallas_call(functools.partial(apply_kernel, scale), grid_spec=pltpu.Pr...  64 us
    pallas_call x1, Pallas kernels, on_plane(): build_oth(parity, left, right_oth, field_own, small_own, undo_own, field_...  42 us
    ppermute x17, waiting for transfers between devices, send(): return lax.ppermute(x, 'sub', over(bit))  31.9 us
    pallas_call x1, Pallas kernels, on_plane(): build_own(left, right_own, field_own, small_own, undo_own)  17 us
    ppermute x9, starting transfers between devices, from_planes(): got.append(lax.ppermute(x, 'row', shift))  11.7 us
    ppermute x17, starting transfers between devices, send(): return lax.ppermute(x, 'sub', over(bit))  9.32 us
    ppermute x1, waiting for transfers between devices, on_plane(): out = lax.ppermute(out, ('row', 'sub'), swap)  9.14 us
    ppermute x1, waiting for transfers between devices, on_plane(): pack = lax.ppermute(pack, ('row', 'sub'), swap)  7.59 us
  transfers between devices with their start and end apart: 28, of which 20 were waited for; matrix products, arithmetic and copies ran while one was open for 1% of the time, Pallas kernels for 31%

profile of v4, /device:TPU:2, one launch (start us, length us, event | category | flops | bytes accessed | tf_op | source)
XLA Modules:
  0.0 225.3 jit_solution(8375744871788120449)
XLA Ops:
  0.6 0.8 copy.9.positions_ref
  1.4 0.9 copy-done
  2.3 0.7 copy-done.1
  3.0 0.7 copy-done.2
  3.7 4.5 %collective-permute-start = (f32[16,2560]{1,0:T(8,128)S(1)}, f32[16,2560]{1,0:T(8,128)S(1)}, u32[]{:S(2)}, u32[]{:S(2)}) collective-permute-start(f32[16,2560]{1,0:T(8,128)S(1)} %pack.1), channel_id=1, source_target_pairs={{0,0},{1,4},{2,8},{3,12},{4,1},{5,5},{6,9},{7,13},{8,2},{9,6},{10,... | collective-permute-start | bytes 491528 | tf_op jit(solution)/shard_map/ppermute | solution.py:426
  8.2 0.8 select_reduce_fusion.1
  9.2 0.8 select_reduce_fusion.list_ref
  9.9 7.6 %collective-permute-done.pack_ref.near_ref = f32[16,2560]{1,0:T(8,128)S(1)} collective-permute-done((f32[16,2560]{1,0:T(8,128)S(1)}, f32[16,2560]{1,0:T(8,128)S(1)}, u32[]{:S(2)}, u32[]{:S(2)}) %collective-permute-start) | collective-permute-done | bytes 163872 | tf_op jit(solution)/shard_map/ppermute | solution.py:426
  17.9 17.0 %build_own.1 = (bf16[2560,1536]{1,0:T(8,128)(2,1)}, f8e4m3fn[2560,1536]{1,0:T(32,128)(4,1)S(1)}, f32[8,5120]{1,0:T(8,128)S(1)}) custom-call(bf16[2560,128]{1,0:T(8,128)(2,1)S(1)} %get-tuple-element.39.left_ref, bf16[96,5120]{1,0:T(8,128)(2,1)S(1)} %get-tuple-element.55.right_ref, bf16[16,5120]{1,0:T(8,128)(2,1)S(1)} %get-tuple-element.43.field_ref.own_ref, ...), custom_call_target="tpu_custom_call" | custom-call | flops 16999999488 | bytes 1000 | tf_op jit(solution)/shard_map/build_own/pallas_call | solution.py:487
  34.9 1.9 collective-permute-start.3
  36.9 1.4 collective-permute-start.14
  38.4 2.3 %collective-permute-start.15 = (f32[16,2560]{1,0:T(8,128)S(1)}, f32[16,2560]{1,0:T(8,128)S(1)}, u32[]{:S(2)}, u32[]{:S(2)}) collective-permute-start(f32[16,2560]{1,0:T(8,128)S(1)} %collective-permute-done.pack_ref.near_ref), channel_id=1, source_target_pairs={{0,12},{4,0},{8,4},{12,8},{1,13},{5,1},{9,5},{13,9},{2,14},{6,2},{... | collective-permute-start | bytes 491528 | tf_op jit(solution)/shard_map/ppermute | solution.py:439
  40.9 1.1 collective-permute-done.2.p
  42.2 2.4 %collective-permute-done.3.p = f32[16,2560]{1,0:T(8,128)S(1)} collective-permute-done((f32[16,2560]{1,0:T(8,128)S(1)}, f32[16,2560]{1,0:T(8,128)S(1)}, u32[]{:S(2)}, u32[]{:S(2)}) %collective-permute-start.3) | collective-permute-done | bytes 163872 | tf_op jit(solution)/shard_map/ppermute | solution.py:418
  45.0 42.0 %build_oth.1 = (bf16[2560,3840]{1,0:T(8,128)(2,1)}, f8e4m3fn[2560,3840]{1,0:T(32,128)(4,1)}, f32[8,10240]{1,0:T(8,128)S(1)}) custom-call(s32[3]{0:T(128)S(1)} %add_convert_fusion.parity_ref, bf16[2560,128]{1,0:T(8,128)(2,1)S(1)} %get-tuple-element.39.left_ref, bf16[96,7680]{1,0:T(8,128)(2,1)S(1)} %pad_maximum_fusion.right_ref, ...), custom_call_target="tpu_custom_call" | custom-call | flops 41999998976 | bytes 1000 | tf_op jit(solution)/shard_map/build_oth/pallas_call | solution.py:537
  87.0 0.7 collective-permute-start.4
  87.7 1.0 collective-permute-done.4
  89.2 6.1 %collective-permute-done.5 = f32[8,5120]{1,0:T(8,128)S(1)} collective-permute-done((f32[8,5120]{1,0:T(8,128)S(1)}, f32[8,5120]{1,0:T(8,128)S(1)}, u32[]{:S(2)}, u32[]{:S(2)}) %collective-permute-start.5) | collective-permute-done | bytes 163872 | tf_op jit(solution)/shard_map/ppermute | solution.py:418
  95.5 1.3 collective-permute-done.6.odd_ref
  97.0 21.3 %apply.3 = f32[8,10240]{1,0:T(8,128)S(1)} custom-call(s32[3]{0:T(128)S(1)} %add_convert_fusion.parity_ref, f32[16,10240]{1,0:T(8,128)S(1)} %constant_dynamic-update-slice_fusion.pack_ref, f32[8,10240]{1,0:T(8,128)S(1)} %get-tuple-element.58.res_ref, bf16[2560,1536]{1,0:T(8,128)(2,1)} %get-tuple-element.59.own_high, ...), custom_call_target="tpu_custom_call" | custom-call | flops 22000001024 | bytes 1000 | tf_op jit(solution)/shard_map/apply/pallas_call | solution.py:558
  118.7 1.2 collective-permute-done.7
  120.2 4.5 %couple.1 = (bf16[2,2560,128]{2,1,0:T(8,128)(2,1)S(1)}, bf16[2,2560,128]{2,1,0:T(8,128)(2,1)S(1)}, f32[16,2560]{1,0:T(8,128)S(1)}, f32[16,2560]{1,0:T(8,128)S(1)}) custom-call(s32[2]{0:T(128)S(1)} %fusion.1.source_ref, s32[2,32]{1,0:T(2,128)S(1)} %select_reduce_fusion.list_ref, s32[2]{0:T(128)S(1)} %get-tuple-element.76.count_ref, s32[1]{0:T(128)} %bitcast.6.first_ref, ...), custom_call_target="tpu_custom_call" | custom-call | flops 4000000000 | bytes 1000 | tf_op jit(solution)/shard_map/couple/pallas_call | solution.py:612
  124.8 2.3 %collective-permute-start.17 = (f32[8,2560]{1,0:T(8,128)S(1)}, f32[8,2560]{1,0:T(8,128)S(1)}, u32[]{:S(2)}, u32[]{:S(2)}) collective-permute-start(f32[8,2560]{1,0:T(8,128)S(1)} %slice.109), channel_id=1, source_target_pairs={{0,8},{4,12},{8,0},{12,4},{1,9},{5,13},{9,1},{13,5},{2,10},{6,14},... | collective-permute-start | bytes 245768 | tf_op jit(solution)/shard_map/ppermute | solution.py:439
  127.0 1.6 collective-permute-start.18
  128.7 3.2 %collective-permute-done.16 = f32[8,2560]{1,0:T(8,128)S(1)} collective-permute-done((f32[8,2560]{1,0:T(8,128)S(1)}, f32[8,2560]{1,0:T(8,128)S(1)}, u32[]{:S(2)}, u32[]{:S(2)}) %collective-permute-start.16) | collective-permute-done | bytes 81952 | tf_op jit(solution)/shard_map/ppermute | solution.py:439
  131.9 2.4 %collective-permute-done.17 = f32[8,2560]{1,0:T(8,128)S(1)} collective-permute-done((f32[8,2560]{1,0:T(8,128)S(1)}, f32[8,2560]{1,0:T(8,128)S(1)}, u32[]{:S(2)}, u32[]{:S(2)}) %collective-permute-start.17) | collective-permute-done | bytes 81952 | tf_op jit(solution)/shard_map/ppermute | solution.py:439
  134.6 1.5 collective-permute-start.10
  136.1 1.1 collective-permute-start.11
  137.2 1.3 collective-permute-start.12
  138.6 2.0 couple_again.1.second_ref
  141.5 1.7 collective-permute-start.19
  143.2 2.8 %collective-permute-done.19 = f32[8,2560]{1,0:T(8,128)S(1)} collective-permute-done((f32[8,2560]{1,0:T(8,128)S(1)}, f32[8,2560]{1,0:T(8,128)S(1)}, u32[]{:S(2)}, u32[]{:S(2)}) %collective-permute-start.19) | collective-permute-done | bytes 81952 | tf_op jit(solution)/shard_map/ppermute | solution.py:418
  146.1 1.4 collective-permute-done.20
  147.6 21.3 %apply.4 = f32[8,10240]{1,0:T(8,128)S(1)} custom-call(s32[3]{0:T(128)S(1)} %add_convert_fusion.parity_ref, f32[16,10240]{1,0:T(8,128)S(1)} %constant_dynamic-update-slice_fusion.pack_ref, f32[8,10240]{1,0:T(8,128)S(1)} %maximum_subtract_fusion.res_ref, bf16[2560,1536]{1,0:T(8,128)(2,1)} %get-tuple-element.59.own_high, ...), custom_call_target="tpu_custom_call" | custom-call | flops 22000001024 | bytes 1000 | tf_op jit(solution)/shard_map/apply/pallas_call | solution.py:558
  169.2 1.3 collective-permute-done.21
  170.4 1.7 collective-permute-start.22
  172.1 4.6 %collective-permute-done.22 = f32[8,5120]{1,0:T(8,128)S(1)} collective-permute-done((f32[8,5120]{1,0:T(8,128)S(1)}, f32[8,5120]{1,0:T(8,128)S(1)}, u32[]{:S(2)}, u32[]{:S(2)}) %collective-permute-start.22) | collective-permute-done | bytes 163872 | tf_op jit(solution)/shard_map/ppermute | solution.py:418
  176.9 1.4 collective-permute-done.23.odd_ref
  178.3 0.8 step.6
  179.0 21.3 %apply.5 = f32[8,10240]{1,0:T(8,128)S(1)} custom-call(s32[3]{0:T(128)S(1)} %add_convert_fusion.parity_ref, f32[16,10240]{1,0:T(8,128)S(1)} %constant_dynamic-update-slice_fusion.pack_ref, f32[8,10240]{1,0:T(8,128)S(1)} %get-tuple-element.72.res_ref, bf16[2560,1536]{1,0:T(8,128)(2,1)} %get-tuple-element.59.own_high, ...), custom_call_target="tpu_custom_call" | custom-call | flops 22000001024 | bytes 1000 | tf_op jit(solution)/shard_map/apply/pallas_call | solution.py:558
  200.6 1.3 collective-permute-done.24
  201.9 1.7 collective-permute-start.25
  203.6 4.6 %collective-permute-done.25 = f32[8,5120]{1,0:T(8,128)S(1)} collective-permute-done((f32[8,5120]{1,0:T(8,128)S(1)}, f32[8,5120]{1,0:T(8,128)S(1)}, u32[]{:S(2)}, u32[]{:S(2)}) %collective-permute-start.25) | collective-permute-done | bytes 163872 | tf_op jit(solution)/shard_map/ppermute | solution.py:418
  208.3 1.4 collective-permute-done.26.odd_ref
  209.7 0.8 step.7
  210.5 4.9 %collective-permute-start.27 = (f32[16,2560]{1,0:T(8,128)S(1)}, f32[16,2560]{1,0:T(8,128)S(1)}, u32[]{:S(2)}, u32[]{:S(2)}) collective-permute-start(f32[16,2560]{1,0:T(8,128)S(1)} %pad_maximum_fusion.9), channel_id=1, source_target_pairs={{0,0},{1,4},{2,8},{3,12},{4,1},{5,5},{6,9},{7,13},{8,2},{9,6},{10,... | collective-permute-start | bytes 491528 | tf_op jit(solution)/shard_map/ppermute | solution.py:649
  215.4 9.1 %collective-permute-done.27 = f32[16,2560]{1,0:T(8,128)S(1)} collective-permute-done((f32[16,2560]{1,0:T(8,128)S(1)}, f32[16,2560]{1,0:T(8,128)S(1)}, u32[]{:S(2)}, u32[]{:S(2)}) %collective-permute-start.27) | collective-permute-done | bytes 163872 | tf_op jit(solution)/shard_map/ppermute | solution.py:649
  224.6 0.7 slice_bitcast_fusion
  (79 shorter events, 5.2 us)
Async XLA Ops:
  1.4 0.9 copy-start
  2.3 0.7 copy-start.1
  3.0 0.7 copy-start.2
  3.7 13.8 %collective-permute-start = (f32[16,2560]{1,0:T(8,128)S(1)}, f32[16,2560]{1,0:T(8,128)S(1)}, u32[]{:S(2)}, u32[]{:S(2)}) collective-permute-start(f32[16,2560]{1,0:T(8,128)S(1)} %pack.1), channel_id=1, source_target_pairs={{0,0},{1,4},{2,8},{3,12},{4,1},{5,5},{6,9},{7,13},{8,2},{9,6},{10,... | collective-permute-start | bytes 491528 | tf_op jit(solution)/shard_map/ppermute | solution.py:426
  34.9 3.5 %collective-permute-start.1 = (f32[16,2560]{1,0:T(8,128)S(1)}, f32[16,2560]{1,0:T(8,128)S(1)}, u32[]{:S(2)}, u32[]{:S(2)}) collective-permute-start(f32[16,2560]{1,0:T(8,128)S(1)} %collective-permute-done.pack_ref.near_ref), channel_id=1, source_target_pairs={{0,1},{1,0},{2,3},{3,2},{4,5},{5,4},{6,7},{7,6},{8,9},{9,8},{10,11... | collective-permute-start | bytes 491528 | tf_op jit(solution)/shard_map/ppermute | solution.py:418
  34.9 7.1 %collective-permute-start.2 = (f32[16,2560]{1,0:T(8,128)S(1)}, f32[16,2560]{1,0:T(8,128)S(1)}, u32[]{:S(2)}, u32[]{:S(2)}) collective-permute-start(f32[16,2560]{1,0:T(8,128)S(1)} %collective-permute-done.pack_ref.near_ref), channel_id=1, source_target_pairs={{0,2},{1,3},{2,0},{3,1},{4,6},{5,7},{6,4},{7,5},{8,10},{9,11},{10,... | collective-permute-start | bytes 491528 | tf_op jit(solution)/shard_map/ppermute | solution.py:418
  34.9 9.7 %collective-permute-start.3 = (f32[16,2560]{1,0:T(8,128)S(1)}, f32[16,2560]{1,0:T(8,128)S(1)}, u32[]{:S(2)}, u32[]{:S(2)}) collective-permute-start(f32[16,2560]{1,0:T(8,128)S(1)} %collective-permute-done.pack_ref.near_ref), channel_id=1, source_target_pairs={{0,3},{1,2},{2,1},{3,0},{4,7},{5,6},{6,5},{7,4},{8,11},{9,10},{10,... | collective-permute-start | bytes 491528 | tf_op jit(solution)/shard_map/ppermute | solution.py:418
  36.8 81.8 %collective-permute-start.13 = (f32[16,2560]{1,0:T(8,128)S(1)}, f32[16,2560]{1,0:T(8,128)S(1)}, u32[]{:S(2)}, u32[]{:S(2)}) collective-permute-start(f32[16,2560]{1,0:T(8,128)S(1)} %collective-permute-done.pack_ref.near_ref), channel_id=1, source_target_pairs={{0,4},{4,8},{8,12},{12,0},{1,5},{5,9},{9,13},{13,1},{2,6},{6,10},{... | collective-permute-start | bytes 491528 | tf_op jit(solution)/shard_map/ppermute | solution.py:439
  36.9 81.7 %collective-permute-start.14 = (f32[16,2560]{1,0:T(8,128)S(1)}, f32[16,2560]{1,0:T(8,128)S(1)}, u32[]{:S(2)}, u32[]{:S(2)}) collective-permute-start(f32[16,2560]{1,0:T(8,128)S(1)} %collective-permute-done.pack_ref.near_ref), channel_id=1, source_target_pairs={{0,8},{4,12},{8,0},{12,4},{1,9},{5,13},{9,1},{13,5},{2,10},{6,14},... | collective-permute-start | bytes 491528 | tf_op jit(solution)/shard_map/ppermute | solution.py:439
  38.4 80.3 %collective-permute-start.15 = (f32[16,2560]{1,0:T(8,128)S(1)}, f32[16,2560]{1,0:T(8,128)S(1)}, u32[]{:S(2)}, u32[]{:S(2)}) collective-permute-start(f32[16,2560]{1,0:T(8,128)S(1)} %collective-permute-done.pack_ref.near_ref), channel_id=1, source_target_pairs={{0,12},{4,0},{8,4},{12,8},{1,13},{5,1},{9,5},{13,9},{2,14},{6,2},{... | collective-permute-start | bytes 491528 | tf_op jit(solution)/shard_map/ppermute | solution.py:439
  87.0 1.7 collective-permute-start.4
  88.8 6.5 %collective-permute-start.5 = (f32[8,5120]{1,0:T(8,128)S(1)}, f32[8,5120]{1,0:T(8,128)S(1)}, u32[]{:S(2)}, u32[]{:S(2)}) collective-permute-start(f32[8,5120]{1,0:T(8,128)S(1)} %maximum_add_fusion), channel_id=1, source_target_pairs={{0,2},{1,3},{2,0},{3,1},{4,6},{5,7},{6,4},{7,5},{8,10},{9,11},{10,... | collective-permute-start | bytes 491528 | tf_op jit(solution)/shard_map/ppermute | solution.py:418
  95.3 1.5 collective-permute-start.6
  118.4 1.5 collective-permute-start.7
  119.9 8.7 %collective-permute-start.8 = (f32[8,5120]{1,0:T(8,128)S(1)}, f32[8,5120]{1,0:T(8,128)S(1)}, u32[]{:S(2)}, u32[]{:S(2)}) collective-permute-start(f32[8,5120]{1,0:T(8,128)S(1)} %maximum_add_fusion.2), channel_id=1, source_target_pairs={{0,2},{1,3},{2,0},{3,1},{4,6},{5,7},{6,4},{7,5},{8,10},{9,11},{10,... | collective-permute-start | bytes 491528 | tf_op jit(solution)/shard_map/ppermute | solution.py:418
  124.7 7.2 %collective-permute-start.16 = (f32[8,2560]{1,0:T(8,128)S(1)}, f32[8,2560]{1,0:T(8,128)S(1)}, u32[]{:S(2)}, u32[]{:S(2)}) collective-permute-start(f32[8,2560]{1,0:T(8,128)S(1)} %slice.109), channel_id=1, source_target_pairs={{0,4},{4,8},{8,12},{12,0},{1,5},{5,9},{9,13},{13,1},{2,6},{6,10},{... | collective-permute-start | bytes 245768 | tf_op jit(solution)/shard_map/ppermute | solution.py:439
  124.8 9.5 %collective-permute-start.17 = (f32[8,2560]{1,0:T(8,128)S(1)}, f32[8,2560]{1,0:T(8,128)S(1)}, u32[]{:S(2)}, u32[]{:S(2)}) collective-permute-start(f32[8,2560]{1,0:T(8,128)S(1)} %slice.109), channel_id=1, source_target_pairs={{0,8},{4,12},{8,0},{12,4},{1,9},{5,13},{9,1},{13,5},{2,10},{6,14},... | collective-permute-start | bytes 245768 | tf_op jit(solution)/shard_map/ppermute | solution.py:439
  127.0 7.3 %collective-permute-start.18 = (f32[8,2560]{1,0:T(8,128)S(1)}, f32[8,2560]{1,0:T(8,128)S(1)}, u32[]{:S(2)}, u32[]{:S(2)}) collective-permute-start(f32[8,2560]{1,0:T(8,128)S(1)} %slice.109), channel_id=1, source_target_pairs={{0,12},{4,0},{8,4},{12,8},{1,13},{5,1},{9,5},{13,9},{2,14},{6,2},{... | collective-permute-start | bytes 245768 | tf_op jit(solution)/shard_map/ppermute | solution.py:439
  128.6 5.7 %collective-permute-start.9 = (f32[8,5120]{1,0:T(8,128)S(1)}, f32[8,5120]{1,0:T(8,128)S(1)}, u32[]{:S(2)}, u32[]{:S(2)}) collective-permute-start(f32[8,5120]{1,0:T(8,128)S(1)} %maximum_add_fusion.3.even_ref), channel_id=1, source_target_pairs={{0,1},{1,0},{2,3},{3,2},{4,5},{5,4},{6,7},{7,6},{8,9},{9,8},{10,11... | collective-permute-start | bytes 491528 | tf_op jit(solution)/shard_map/ppermute | solution.py:418
  134.6 6.0 %collective-permute-start.10 = (f32[16,128]{1,0:T(8,128)S(1)}, f32[16,128]{1,0:T(8,128)S(1)}, u32[]{:S(2)}, u32[]{:S(2)}) collective-permute-start(f32[16,128]{1,0:T(8,128)S(1)} %constant_dynamic-update-slice_fusion.4), channel_id=1, source_target_pairs={{0,4},{4,8},{8,12},{12,0},{1,5},{5,9},{9,13},{13,1},{2,6},{6,10},{... | collective-permute-start | bytes 24584 | tf_op jit(solution)/shard_map/ppermute | solution.py:439
  136.1 4.5 %collective-permute-start.11 = (f32[16,128]{1,0:T(8,128)S(1)}, f32[16,128]{1,0:T(8,128)S(1)}, u32[]{:S(2)}, u32[]{:S(2)}) collective-permute-start(f32[16,128]{1,0:T(8,128)S(1)} %constant_dynamic-update-slice_fusion.4), channel_id=1, source_target_pairs={{0,8},{4,12},{8,0},{12,4},{1,9},{5,13},{9,1},{13,5},{2,10},{6,14},... | collective-permute-start | bytes 24584 | tf_op jit(solution)/shard_map/ppermute | solution.py:439
  137.2 3.7 %collective-permute-start.12 = (f32[16,128]{1,0:T(8,128)S(1)}, f32[16,128]{1,0:T(8,128)S(1)}, u32[]{:S(2)}, u32[]{:S(2)}) collective-permute-start(f32[16,128]{1,0:T(8,128)S(1)} %constant_dynamic-update-slice_fusion.4), channel_id=1, source_target_pairs={{0,12},{4,0},{8,4},{12,8},{1,13},{5,1},{9,5},{13,9},{2,14},{6,2},{... | collective-permute-start | bytes 24584 | tf_op jit(solution)/shard_map/ppermute | solution.py:439
  141.5 4.5 %collective-permute-start.19 = (f32[8,2560]{1,0:T(8,128)S(1)}, f32[8,2560]{1,0:T(8,128)S(1)}, u32[]{:S(2)}, u32[]{:S(2)}) collective-permute-start(f32[8,2560]{1,0:T(8,128)S(1)} %combine.1), channel_id=1, source_target_pairs={{0,2},{1,3},{2,0},{3,1},{4,6},{5,7},{6,4},{7,5},{8,10},{9,11},{10,... | collective-permute-start | bytes 245768 | tf_op jit(solution)/shard_map/ppermute | solution.py:418
  146.1 1.5 collective-permute-start.20
  169.0 1.5 collective-permute-start.21
  170.4 6.3 %collective-permute-start.22 = (f32[8,5120]{1,0:T(8,128)S(1)}, f32[8,5120]{1,0:T(8,128)S(1)}, u32[]{:S(2)}, u32[]{:S(2)}) collective-permute-start(f32[8,5120]{1,0:T(8,128)S(1)} %maximum_add_fusion.4), channel_id=1, source_target_pairs={{0,2},{1,3},{2,0},{3,1},{4,6},{5,7},{6,4},{7,5},{8,10},{9,11},{10,... | collective-permute-start | bytes 491528 | tf_op jit(solution)/shard_map/ppermute | solution.py:418
  176.8 1.5 collective-permute-start.23
  200.4 1.5 collective-permute-start.24
  201.9 6.3 %collective-permute-start.25 = (f32[8,5120]{1,0:T(8,128)S(1)}, f32[8,5120]{1,0:T(8,128)S(1)}, u32[]{:S(2)}, u32[]{:S(2)}) collective-permute-start(f32[8,5120]{1,0:T(8,128)S(1)} %maximum_add_fusion.6), channel_id=1, source_target_pairs={{0,2},{1,3},{2,0},{3,1},{4,6},{5,7},{6,4},{7,5},{8,10},{9,11},{10,... | collective-permute-start | bytes 491528 | tf_op jit(solution)/shard_map/ppermute | solution.py:418
  208.3 1.5 collective-permute-start.26
  210.5 14.0 %collective-permute-start.27 = (f32[16,2560]{1,0:T(8,128)S(1)}, f32[16,2560]{1,0:T(8,128)S(1)}, u32[]{:S(2)}, u32[]{:S(2)}) collective-permute-start(f32[16,2560]{1,0:T(8,128)S(1)} %pad_maximum_fusion.9), channel_id=1, source_target_pairs={{0,0},{1,4},{2,8},{3,12},{4,1},{5,5},{6,9},{7,13},{8,2},{9,6},{10,... | collective-permute-start | bytes 491528 | tf_op jit(solution)/shard_map/ppermute | solution.py:649

commit v5 on v4

--- a/solution.py
+++ b/solution.py
@@ -21,6 +21,7 @@
 BF16 = jnp.bfloat16
 TILE = 256
 CHUNK = 32
+ROWS = 2
 FEATURES = 96
 WAVE = KAPPA / (2.0 * math.pi)
 ROUNDER = 12582912.0
@@ -30,7 +31,7 @@
     4.048771939331772,
     -1.2478000348360374,
 )
-LIFT = 65536.0
+LIFT = 256.0
 FP8 = jnp.float8_e4m3fn
 FP8_PEAK = 224.0
 
@@ -101,14 +102,6 @@
     return lax.dot_general(left, right, (((1,), (1,)), ((), ())), preferred_element_type=F32)
 
 
-def pack_kernel(positions_ref, area_ref, term_ref, excitation_ref, pack_ref):
-    pack_ref[0:3, :] = positions_ref[0]
-    pack_ref[3:4, :] = area_ref[...]
-    pack_ref[4:5, :] = term_ref[...]
-    pack_ref[5:8, :] = jnp.zeros((3, pack_ref.shape[1]), F32)
-    pack_ref[8:16, :] = excitation_ref[0]
-
-
 def prep_kernel(scale, doubled, pack_ref, left_ref, right_ref, field_ref, small_ref, undo_ref):
     pack = pack_ref[...]
     count = pack.shape[1]
@@ -139,9 +132,9 @@
     for c in range(TILE // CHUNK):
         rows = slice(c * CHUNK, (c + 1) * CHUNK)
         g = green(source[rows, at : at + TILE])
-        high = g.astype(BF16)
-        target_high[rows, to : to + TILE] = high
-        target_low[rows, to : to + TILE] = (g - high.astype(F32)).astype(FP8)
+        high = jnp.round(g)
+        target_high[rows, to : to + TILE] = high.astype(BF16)
+        target_low[rows, to : to + TILE] = (g - high).astype(FP8)
 
 
 def fold_pieces(x):
@@ -267,7 +260,6 @@
     i = pl.program_id(0)
     count = res_ref.shape[1] // 4
     half = count // 2
-    here = pl.multiple_of(i * TILE, TILE)
 
     @pl.when(i == 0)
     def _():
@@ -290,27 +282,31 @@
                 oth_small[:, to : to + TILE] = small[:, k * TILE : (k + 1) * TILE]
 
     width = own_high.shape[1]
-    mine = own_field[:, pl.ds(here, TILE)]
-    mine_small = own_small[:, pl.ds(here, TILE)]
-    undo = undos[:, :1]
-    span = pl.ds(here, width)
-    inner = pl.ds(pl.multiple_of(here + TILE, TILE), width - 2 * TILE)
-    total = fold_pieces(nt(own_field[:, span], own_high[...]))
-    total += nt(own_small[:, span], own_low[...]) * undo
-    acc_own[:, inner] += (
-        fold_pieces(nn(mine, own_high[:, TILE : width - TILE]))
-        + nn(mine_small, own_low[:, TILE : width - TILE]) * undo
-    )
-    for b in range(3):
-        there = pl.ds(
-            pl.multiple_of(b * count + ((i + parity_ref[b]) & 1) * half, TILE), half
+    for j in range(ROWS):
+        index = i * ROWS + j
+        rows = slice(j * TILE, (j + 1) * TILE)
+        here = pl.multiple_of(index * TILE, TILE)
+        mine = own_field[:, pl.ds(here, TILE)]
+        mine_small = own_small[:, pl.ds(here, TILE)]
+        undo = undos[:, :1]
+        span = pl.ds(here, width)
+        inner = pl.ds(pl.multiple_of(here + TILE, TILE), width - 2 * TILE)
+        total = fold_pieces(nt(own_field[:, span], own_high[rows, :]))
+        total += nt(own_small[:, span], own_low[rows, :]) * undo
+        acc_own[:, inner] += (
+            fold_pieces(nn(mine, own_high[rows, TILE : width - TILE]))
+            + nn(mine_small, own_low[rows, TILE : width - TILE]) * undo
         )
-        high = oth_high[:, b * half : (b + 1) * half]
-        low = oth_low[:, b * half : (b + 1) * half]
-        total += fold_pieces(nt(oth_field[:, there], high))
-        total += nt(oth_small[:, there], low) * undos[:, (b + 1) * 128 : (b + 1) * 128 + 1]
-        acc_oth[:, there] += fold_pieces(nn(mine, high)) + nn(mine_small, low) * undo
-    acc_own[:, pl.ds(here, TILE)] += total
+        for b in range(3):
+            there = pl.ds(
+                pl.multiple_of(b * count + ((index + parity_ref[b]) & 1) * half, TILE), half
+            )
+            high = oth_high[rows, b * half : (b + 1) * half]
+            low = oth_low[rows, b * half : (b + 1) * half]
+            total += fold_pieces(nt(oth_field[:, there], high))
+            total += nt(oth_small[:, there], low) * undos[:, (b + 1) * 128 : (b + 1) * 128 + 1]
+            acc_oth[:, there] += fold_pieces(nn(mine, high)) + nn(mine_small, low) * undo
+        acc_own[:, pl.ds(here, TILE)] += total
 
     @pl.when(i == pl.num_programs(0) - 1)
     def _():
@@ -417,12 +413,10 @@
     def send(x, bit):
         return lax.ppermute(x, "sub", over(bit))
 
-    pack = pl.pallas_call(
-        pack_kernel,
-        out_shape=jax.ShapeDtypeStruct((16, count), F32),
-        compiler_params=params(),
-        name="pack",
-    )(positions, panel_area, self_term, excitation)
+    pack = jnp.concatenate(
+        [positions[0], panel_area, self_term, jnp.zeros((3, count), F32), excitation[0]],
+        axis=0,
+    )
     pack = lax.ppermute(pack, ("row", "sub"), swap)
 
     mine = jnp.arange(subs, dtype=jnp.int32) == plane
@@ -553,13 +547,13 @@
         return even, odd
 
     def apply(res):
-        own_spec = pl.BlockSpec((TILE, own_width), lambda i, *_: (i, 0))
-        oth_spec = pl.BlockSpec((TILE, 3 * half), lambda i, *_: (i, 0))
+        own_spec = pl.BlockSpec((ROWS * TILE, own_width), lambda i, *_: (i, 0))
+        oth_spec = pl.BlockSpec((ROWS * TILE, 3 * half), lambda i, *_: (i, 0))
         return pl.pallas_call(
             functools.partial(apply_kernel, scale),
             grid_spec=pltpu.PrefetchScalarGridSpec(
                 num_scalar_prefetch=1,
-                grid=(tiles,),
+                grid=(tiles // ROWS,),
                 in_specs=[
                     whole((16, 4 * count)),
                     whole((8, 4 * count)),
@@ -637,10 +631,8 @@
         first_part,
         second_part,
     )
-    coupled_across = send(coupled, 2)
-    odd = send(jnp.concatenate([coupled, coupled_across], axis=1), 1)
     res = res - jnp.concatenate(
-        [coupled, odd[:, :count], coupled_across, odd[:, count:]], axis=1
+        [coupled] + [send(coupled, bit) for bit in range(1, subs)], axis=1
     )
 
     res, cur, _ = step(apply(res), res, cur)

time: 226 us -> 221 us (0.978)
  Pallas kernels: 133 us -> 129 us
  waiting for transfers between devices: 54.5 us -> 57.3 us
  starting transfers between devices: 30.4 us -> 28 us
    pallas_call x3, Pallas kernels: 64 us -> 60.8 us  [apply(): pl.pallas_call(functools.partial(apply_kernel, scale), grid_spec=pltpu.Pr...]
    ppermute x17 -> x18, waiting for transfers between devices: 31.9 us -> 34.3 us  [send(): return lax.ppermute(x, 'sub', over(bit))]
    unnamed x11 -> x5, local copies, waits for them, and re-layouts: 3.09 us -> 0.8 us
    ppermute x17 -> x18, starting transfers between devices: 9.32 us -> 8.99 us  [send(): return lax.ppermute(x, 'sub', over(bit))]
  transfers between devices with their start and end apart: 28 -> 29, of which waited for: 20 -> 20; matrix products, arithmetic and copies ran while one was open for 1% -> 1% of each run, Pallas kernels for 31% -> 31%
where the time goes in v5:
time: 221 us
  Pallas kernels  129 us (58%)
  waiting for transfers between devices  57.3 us (26%)
  starting transfers between devices  28 us (13%)
  local copies, waits for them, and re-layouts  3.36 us (2%)
  other arithmetic  2.21 us (1%)
    pallas_call x3, Pallas kernels, apply(): pl.pallas_call(functools.partial(apply_kernel, scale), grid_spec=pltpu.Pr...  60.8 us
    pallas_call x1, Pallas kernels, on_plane(): build_oth(parity, left, right_oth, field_own, small_own, undo_own, field_...  41.2 us
    ppermute x18, waiting for transfers between devices, send(): return lax.ppermute(x, 'sub', over(bit))  34.3 us
    pallas_call x1, Pallas kernels, on_plane(): build_own(left, right_own, field_own, small_own, undo_own)  16.8 us
    ppermute x9, starting transfers between devices, from_planes(): got.append(lax.ppermute(x, 'row', shift))  9.93 us
    ppermute x1, waiting for transfers between devices, on_plane(): out = lax.ppermute(out, ('row', 'sub'), swap)  9.18 us
    ppermute x18, starting transfers between devices, send(): return lax.ppermute(x, 'sub', over(bit))  8.99 us
    ppermute x1, waiting for transfers between devices, on_plane(): pack = lax.ppermute(pack, ('row', 'sub'), swap)  7.6 us
  transfers between devices with their start and end apart: 29, of which 20 were waited for; matrix products, arithmetic and copies ran while one was open for 1% of the time, Pallas kernels for 31%

profile of v5, /device:TPU:2, one launch (start us, length us, event | category | flops | bytes accessed | tf_op | source)
XLA Modules:
  0.0 220.8 jit_solution(17923224399940666376)
XLA Ops:
  0.6 0.8 copy.11
  1.4 1.7 concatenate.63
  3.1 4.5 %collective-permute-start = (f32[16,2560]{1,0:T(8,128)S(1)}, f32[16,2560]{1,0:T(8,128)S(1)}, u32[]{:S(2)}, u32[]{:S(2)}) collective-permute-start(f32[16,2560]{1,0:T(8,128)S(1)} %concatenate.63), channel_id=1, source_target_pairs={{0,0},{1,4},{2,8},{3,12},{4,1},{5,5},{6,9},{7,13},{8,2},{9,6},{10,... | collective-permute-start | bytes 491528 | tf_op jit(solution)/shard_map/ppermute | solution.py:420
  7.6 0.8 select_reduce_fusion.1
  8.5 0.8 select_reduce_fusion.list_ref
  9.3 7.6 %collective-permute-done.pack_ref.near_ref = f32[16,2560]{1,0:T(8,128)S(1)} collective-permute-done((f32[16,2560]{1,0:T(8,128)S(1)}, f32[16,2560]{1,0:T(8,128)S(1)}, u32[]{:S(2)}, u32[]{:S(2)}) %collective-permute-start) | collective-permute-done | bytes 163872 | tf_op jit(solution)/shard_map/ppermute | solution.py:420
  17.2 16.8 %build_own.1 = (bf16[2560,1536]{1,0:T(8,128)(2,1)}, f8e4m3fn[2560,1536]{1,0:T(32,128)(4,1)S(1)}, f32[8,5120]{1,0:T(8,128)S(1)}) custom-call(bf16[2560,128]{1,0:T(8,128)(2,1)S(1)} %get-tuple-element.39.left_ref, bf16[96,5120]{1,0:T(8,128)(2,1)S(1)} %get-tuple-element.55.right_ref, bf16[16,5120]{1,0:T(8,128)(2,1)S(1)} %get-tuple-element.43.field_ref.own_ref, ...), custom_call_target="tpu_custom_call" | custom-call | flops 16999999488 | bytes 1000 | tf_op jit(solution)/shard_map/build_own/pallas_call | solution.py:481
  34.0 1.9 collective-permute-start.3
  35.9 1.0 collective-permute-start.15
  37.0 1.0 collective-permute-start.13
  38.2 2.9 %collective-permute-done.2.p = f32[16,2560]{1,0:T(8,128)S(1)} collective-permute-done((f32[16,2560]{1,0:T(8,128)S(1)}, f32[16,2560]{1,0:T(8,128)S(1)}, u32[]{:S(2)}, u32[]{:S(2)}) %collective-permute-start.2) | collective-permute-done | bytes 163872 | tf_op jit(solution)/shard_map/ppermute | solution.py:414
  41.3 2.4 %collective-permute-done.3.p = f32[16,2560]{1,0:T(8,128)S(1)} collective-permute-done((f32[16,2560]{1,0:T(8,128)S(1)}, f32[16,2560]{1,0:T(8,128)S(1)}, u32[]{:S(2)}, u32[]{:S(2)}) %collective-permute-start.3) | collective-permute-done | bytes 163872 | tf_op jit(solution)/shard_map/ppermute | solution.py:414
  44.1 41.2 %build_oth.1 = (bf16[2560,3840]{1,0:T(8,128)(2,1)}, f8e4m3fn[2560,3840]{1,0:T(32,128)(4,1)}, f32[8,10240]{1,0:T(8,128)S(1)}) custom-call(s32[3]{0:T(128)S(1)} %add_convert_fusion.parity_ref, bf16[2560,128]{1,0:T(8,128)(2,1)S(1)} %get-tuple-element.39.left_ref, bf16[96,7680]{1,0:T(8,128)(2,1)S(1)} %pad_maximum_fusion.right_ref, ...), custom_call_target="tpu_custom_call" | custom-call | flops 41999998976 | bytes 1000 | tf_op jit(solution)/shard_map/build_oth/pallas_call | solution.py:531
  85.4 0.6 collective-permute-start.4
  86.0 1.0 collective-permute-done.4
  87.5 6.1 %collective-permute-done.5 = f32[8,5120]{1,0:T(8,128)S(1)} collective-permute-done((f32[8,5120]{1,0:T(8,128)S(1)}, f32[8,5120]{1,0:T(8,128)S(1)}, u32[]{:S(2)}, u32[]{:S(2)}) %collective-permute-start.5) | collective-permute-done | bytes 163872 | tf_op jit(solution)/shard_map/ppermute | solution.py:414
  93.8 1.3 collective-permute-done.6.odd_ref
  95.3 20.3 %apply.3 = f32[8,10240]{1,0:T(8,128)S(1)} custom-call(s32[3]{0:T(128)S(1)} %add_convert_fusion.parity_ref, f32[16,10240]{1,0:T(8,128)S(1)} %constant_dynamic-update-slice_fusion.pack_ref, f32[8,10240]{1,0:T(8,128)S(1)} %get-tuple-element.58.res_ref, bf16[2560,1536]{1,0:T(8,128)(2,1)} %get-tuple-element.59.own_high, ...), custom_call_target="tpu_custom_call" | custom-call | flops 22000001024 | bytes 1000 | tf_op jit(solution)/shard_map/apply/pallas_call | solution.py:552
  115.9 1.2 collective-permute-done.7
  117.5 4.5 %couple.1 = (bf16[2,2560,128]{2,1,0:T(8,128)(2,1)S(1)}, bf16[2,2560,128]{2,1,0:T(8,128)(2,1)S(1)}, f32[16,2560]{1,0:T(8,128)S(1)}, f32[16,2560]{1,0:T(8,128)S(1)}) custom-call(s32[2]{0:T(128)S(1)} %fusion.1.source_ref, s32[2,32]{1,0:T(2,128)S(1)} %select_reduce_fusion.list_ref, s32[2]{0:T(128)S(1)} %get-tuple-element.76.count_ref, s32[1]{0:T(128)} %bitcast.7.first_ref, ...), custom_call_target="tpu_custom_call" | custom-call | flops 4000000000 | bytes 1000 | tf_op jit(solution)/shard_map/couple/pallas_call | solution.py:606
  122.1 2.5 %collective-permute-start.17 = (f32[8,2560]{1,0:T(8,128)S(1)}, f32[8,2560]{1,0:T(8,128)S(1)}, u32[]{:S(2)}, u32[]{:S(2)}) collective-permute-start(f32[8,2560]{1,0:T(8,128)S(1)} %slice.103), channel_id=1, source_target_pairs={{0,8},{4,12},{8,0},{12,4},{1,9},{5,13},{9,1},{13,5},{2,10},{6,14},... | collective-permute-start | bytes 245768 | tf_op jit(solution)/shard_map/ppermute | solution.py:433
  124.6 1.2 collective-permute-start.18
  126.0 3.2 %collective-permute-done.16 = f32[8,2560]{1,0:T(8,128)S(1)} collective-permute-done((f32[8,2560]{1,0:T(8,128)S(1)}, f32[8,2560]{1,0:T(8,128)S(1)}, u32[]{:S(2)}, u32[]{:S(2)}) %collective-permute-start.16) | collective-permute-done | bytes 81952 | tf_op jit(solution)/shard_map/ppermute | solution.py:433
  129.2 2.4 %collective-permute-done.17 = f32[8,2560]{1,0:T(8,128)S(1)} collective-permute-done((f32[8,2560]{1,0:T(8,128)S(1)}, f32[8,2560]{1,0:T(8,128)S(1)}, u32[]{:S(2)}, u32[]{:S(2)}) %collective-permute-start.17) | collective-permute-done | bytes 81952 | tf_op jit(solution)/shard_map/ppermute | solution.py:433
  131.9 1.5 collective-permute-start.10
  133.4 1.4 collective-permute-start.11
  134.8 1.0 collective-permute-start.12
  135.8 2.0 couple_again.1.second_ref
  137.9 0.5 collective-permute-done.12
  138.4 0.6 combine.1
  139.2 1.4 collective-permute-start.20
  141.0 3.5 %collective-permute-done.20 = f32[8,2560]{1,0:T(8,128)S(1)} collective-permute-done((f32[8,2560]{1,0:T(8,128)S(1)}, f32[8,2560]{1,0:T(8,128)S(1)}, u32[]{:S(2)}, u32[]{:S(2)}) %collective-permute-start.20) | collective-permute-done | bytes 81952 | tf_op jit(solution)/shard_map/ppermute | solution.py:414
  144.5 0.8 collective-permute-done.21
  145.3 20.3 %apply.4 = f32[8,10240]{1,0:T(8,128)S(1)} custom-call(s32[3]{0:T(128)S(1)} %add_convert_fusion.parity_ref, f32[16,10240]{1,0:T(8,128)S(1)} %constant_dynamic-update-slice_fusion.pack_ref, f32[8,10240]{1,0:T(8,128)S(1)} %maximum_subtract_fusion.res_ref, bf16[2560,1536]{1,0:T(8,128)(2,1)} %get-tuple-element.59.own_high, ...), custom_call_target="tpu_custom_call" | custom-call | flops 22000001024 | bytes 1000 | tf_op jit(solution)/shard_map/apply/pallas_call | solution.py:552
  166.0 1.1 collective-permute-done.22
  167.1 1.3 collective-permute-start.23
  168.5 5.1 %collective-permute-done.23 = f32[8,5120]{1,0:T(8,128)S(1)} collective-permute-done((f32[8,5120]{1,0:T(8,128)S(1)}, f32[8,5120]{1,0:T(8,128)S(1)}, u32[]{:S(2)}, u32[]{:S(2)}) %collective-permute-start.23) | collective-permute-done | bytes 163872 | tf_op jit(solution)/shard_map/ppermute | solution.py:414
  173.7 1.4 collective-permute-done.24.odd_ref
  175.1 0.8 step.6
  175.9 20.3 %apply.5 = f32[8,10240]{1,0:T(8,128)S(1)} custom-call(s32[3]{0:T(128)S(1)} %add_convert_fusion.parity_ref, f32[16,10240]{1,0:T(8,128)S(1)} %constant_dynamic-update-slice_fusion.pack_ref, f32[8,10240]{1,0:T(8,128)S(1)} %get-tuple-element.72.res_ref, bf16[2560,1536]{1,0:T(8,128)(2,1)} %get-tuple-element.59.own_high, ...), custom_call_target="tpu_custom_call" | custom-call | flops 22000001024 | bytes 1000 | tf_op jit(solution)/shard_map/apply/pallas_call | solution.py:552
  196.4 1.3 collective-permute-done.25
  197.7 1.4 collective-permute-start.26
  199.1 4.9 %collective-permute-done.26 = f32[8,5120]{1,0:T(8,128)S(1)} collective-permute-done((f32[8,5120]{1,0:T(8,128)S(1)}, f32[8,5120]{1,0:T(8,128)S(1)}, u32[]{:S(2)}, u32[]{:S(2)}) %collective-permute-start.26) | collective-permute-done | bytes 163872 | tf_op jit(solution)/shard_map/ppermute | solution.py:414
  204.1 1.4 collective-permute-done.27.odd_ref
  205.5 0.8 step.7
  206.3 4.6 %collective-permute-start.28 = (f32[16,2560]{1,0:T(8,128)S(1)}, f32[16,2560]{1,0:T(8,128)S(1)}, u32[]{:S(2)}, u32[]{:S(2)}) collective-permute-start(f32[16,2560]{1,0:T(8,128)S(1)} %pad_maximum_fusion.8), channel_id=1, source_target_pairs={{0,0},{1,4},{2,8},{3,12},{4,1},{5,5},{6,9},{7,13},{8,2},{9,6},{10,... | collective-permute-start | bytes 491528 | tf_op jit(solution)/shard_map/ppermute | solution.py:641
  211.0 9.2 %collective-permute-done.28 = f32[16,2560]{1,0:T(8,128)S(1)} collective-permute-done((f32[16,2560]{1,0:T(8,128)S(1)}, f32[16,2560]{1,0:T(8,128)S(1)}, u32[]{:S(2)}, u32[]{:S(2)}) %collective-permute-start.28) | collective-permute-done | bytes 163872 | tf_op jit(solution)/shard_map/ppermute | solution.py:641
  220.1 0.7 slice_bitcast_fusion
  (74 shorter events, 5.0 us)
Async XLA Ops:
  3.1 13.8 %collective-permute-start = (f32[16,2560]{1,0:T(8,128)S(1)}, f32[16,2560]{1,0:T(8,128)S(1)}, u32[]{:S(2)}, u32[]{:S(2)}) collective-permute-start(f32[16,2560]{1,0:T(8,128)S(1)} %concatenate.63), channel_id=1, source_target_pairs={{0,0},{1,4},{2,8},{3,12},{4,1},{5,5},{6,9},{7,13},{8,2},{9,6},{10,... | collective-permute-start | bytes 491528 | tf_op jit(solution)/shard_map/ppermute | solution.py:420
  34.0 4.0 %collective-permute-start.1 = (f32[16,2560]{1,0:T(8,128)S(1)}, f32[16,2560]{1,0:T(8,128)S(1)}, u32[]{:S(2)}, u32[]{:S(2)}) collective-permute-start(f32[16,2560]{1,0:T(8,128)S(1)} %collective-permute-done.pack_ref.near_ref), channel_id=1, source_target_pairs={{0,1},{1,0},{2,3},{3,2},{4,5},{5,4},{6,7},{7,6},{8,9},{9,8},{10,11... | collective-permute-start | bytes 491528 | tf_op jit(solution)/shard_map/ppermute | solution.py:414
  34.0 7.1 %collective-permute-start.2 = (f32[16,2560]{1,0:T(8,128)S(1)}, f32[16,2560]{1,0:T(8,128)S(1)}, u32[]{:S(2)}, u32[]{:S(2)}) collective-permute-start(f32[16,2560]{1,0:T(8,128)S(1)} %collective-permute-done.pack_ref.near_ref), channel_id=1, source_target_pairs={{0,2},{1,3},{2,0},{3,1},{4,6},{5,7},{6,4},{7,5},{8,10},{9,11},{10,... | collective-permute-start | bytes 491528 | tf_op jit(solution)/shard_map/ppermute | solution.py:414
  34.0 9.7 %collective-permute-start.3 = (f32[16,2560]{1,0:T(8,128)S(1)}, f32[16,2560]{1,0:T(8,128)S(1)}, u32[]{:S(2)}, u32[]{:S(2)}) collective-permute-start(f32[16,2560]{1,0:T(8,128)S(1)} %collective-permute-done.pack_ref.near_ref), channel_id=1, source_target_pairs={{0,3},{1,2},{2,1},{3,0},{4,7},{5,6},{6,5},{7,4},{8,11},{9,10},{10,... | collective-permute-start | bytes 491528 | tf_op jit(solution)/shard_map/ppermute | solution.py:414
  35.9 80.0 %collective-permute-start.15 = (f32[16,2560]{1,0:T(8,128)S(1)}, f32[16,2560]{1,0:T(8,128)S(1)}, u32[]{:S(2)}, u32[]{:S(2)}) collective-permute-start(f32[16,2560]{1,0:T(8,128)S(1)} %collective-permute-done.pack_ref.near_ref), channel_id=1, source_target_pairs={{0,12},{4,0},{8,4},{12,8},{1,13},{5,1},{9,5},{13,9},{2,14},{6,2},{... | collective-permute-start | bytes 491528 | tf_op jit(solution)/shard_map/ppermute | solution.py:433
  37.0 78.9 %collective-permute-start.13 = (f32[16,2560]{1,0:T(8,128)S(1)}, f32[16,2560]{1,0:T(8,128)S(1)}, u32[]{:S(2)}, u32[]{:S(2)}) collective-permute-start(f32[16,2560]{1,0:T(8,128)S(1)} %collective-permute-done.pack_ref.near_ref), channel_id=1, source_target_pairs={{0,4},{4,8},{8,12},{12,0},{1,5},{5,9},{9,13},{13,1},{2,6},{6,10},{... | collective-permute-start | bytes 491528 | tf_op jit(solution)/shard_map/ppermute | solution.py:433
  38.0 77.9 %collective-permute-start.14 = (f32[16,2560]{1,0:T(8,128)S(1)}, f32[16,2560]{1,0:T(8,128)S(1)}, u32[]{:S(2)}, u32[]{:S(2)}) collective-permute-start(f32[16,2560]{1,0:T(8,128)S(1)} %collective-permute-done.pack_ref.near_ref), channel_id=1, source_target_pairs={{0,8},{4,12},{8,0},{12,4},{1,9},{5,13},{9,1},{13,5},{2,10},{6,14},... | collective-permute-start | bytes 491528 | tf_op jit(solution)/shard_map/ppermute | solution.py:433
  85.4 1.7 collective-permute-start.4
  87.1 6.5 %collective-permute-start.5 = (f32[8,5120]{1,0:T(8,128)S(1)}, f32[8,5120]{1,0:T(8,128)S(1)}, u32[]{:S(2)}, u32[]{:S(2)}) collective-permute-start(f32[8,5120]{1,0:T(8,128)S(1)} %maximum_add_fusion), channel_id=1, source_target_pairs={{0,2},{1,3},{2,0},{3,1},{4,6},{5,7},{6,4},{7,5},{8,10},{9,11},{10,... | collective-permute-start | bytes 491528 | tf_op jit(solution)/shard_map/ppermute | solution.py:414
  93.7 1.5 collective-permute-start.6
  115.7 1.5 collective-permute-start.7
  117.1 8.7 %collective-permute-start.8 = (f32[8,5120]{1,0:T(8,128)S(1)}, f32[8,5120]{1,0:T(8,128)S(1)}, u32[]{:S(2)}, u32[]{:S(2)}) collective-permute-start(f32[8,5120]{1,0:T(8,128)S(1)} %maximum_add_fusion.2), channel_id=1, source_target_pairs={{0,2},{1,3},{2,0},{3,1},{4,6},{5,7},{6,4},{7,5},{8,10},{9,11},{10,... | collective-permute-start | bytes 491528 | tf_op jit(solution)/shard_map/ppermute | solution.py:414
  122.0 7.2 %collective-permute-start.16 = (f32[8,2560]{1,0:T(8,128)S(1)}, f32[8,2560]{1,0:T(8,128)S(1)}, u32[]{:S(2)}, u32[]{:S(2)}) collective-permute-start(f32[8,2560]{1,0:T(8,128)S(1)} %slice.103), channel_id=1, source_target_pairs={{0,4},{4,8},{8,12},{12,0},{1,5},{5,9},{9,13},{13,1},{2,6},{6,10},{... | collective-permute-start | bytes 245768 | tf_op jit(solution)/shard_map/ppermute | solution.py:433
  122.1 9.4 %collective-permute-start.17 = (f32[8,2560]{1,0:T(8,128)S(1)}, f32[8,2560]{1,0:T(8,128)S(1)}, u32[]{:S(2)}, u32[]{:S(2)}) collective-permute-start(f32[8,2560]{1,0:T(8,128)S(1)} %slice.103), channel_id=1, source_target_pairs={{0,8},{4,12},{8,0},{12,4},{1,9},{5,13},{9,1},{13,5},{2,10},{6,14},... | collective-permute-start | bytes 245768 | tf_op jit(solution)/shard_map/ppermute | solution.py:433
  124.6 6.9 %collective-permute-start.18 = (f32[8,2560]{1,0:T(8,128)S(1)}, f32[8,2560]{1,0:T(8,128)S(1)}, u32[]{:S(2)}, u32[]{:S(2)}) collective-permute-start(f32[8,2560]{1,0:T(8,128)S(1)} %slice.103), channel_id=1, source_target_pairs={{0,12},{4,0},{8,4},{12,8},{1,13},{5,1},{9,5},{13,9},{2,14},{6,2},{... | collective-permute-start | bytes 245768 | tf_op jit(solution)/shard_map/ppermute | solution.py:433
  125.9 5.7 %collective-permute-start.9 = (f32[8,5120]{1,0:T(8,128)S(1)}, f32[8,5120]{1,0:T(8,128)S(1)}, u32[]{:S(2)}, u32[]{:S(2)}) collective-permute-start(f32[8,5120]{1,0:T(8,128)S(1)} %maximum_add_fusion.3.even_ref), channel_id=1, source_target_pairs={{0,1},{1,0},{2,3},{3,2},{4,5},{5,4},{6,7},{7,6},{8,9},{9,8},{10,11... | collective-permute-start | bytes 491528 | tf_op jit(solution)/shard_map/ppermute | solution.py:414
  131.9 6.0 %collective-permute-start.10 = (f32[16,128]{1,0:T(8,128)S(1)}, f32[16,128]{1,0:T(8,128)S(1)}, u32[]{:S(2)}, u32[]{:S(2)}) collective-permute-start(f32[16,128]{1,0:T(8,128)S(1)} %constant_dynamic-update-slice_fusion.4), channel_id=1, source_target_pairs={{0,4},{4,8},{8,12},{12,0},{1,5},{5,9},{9,13},{13,1},{2,6},{6,10},{... | collective-permute-start | bytes 24584 | tf_op jit(solution)/shard_map/ppermute | solution.py:433
  133.4 4.5 %collective-permute-start.11 = (f32[16,128]{1,0:T(8,128)S(1)}, f32[16,128]{1,0:T(8,128)S(1)}, u32[]{:S(2)}, u32[]{:S(2)}) collective-permute-start(f32[16,128]{1,0:T(8,128)S(1)} %constant_dynamic-update-slice_fusion.4), channel_id=1, source_target_pairs={{0,8},{4,12},{8,0},{12,4},{1,9},{5,13},{9,1},{13,5},{2,10},{6,14},... | collective-permute-start | bytes 24584 | tf_op jit(solution)/shard_map/ppermute | solution.py:433
  134.8 3.7 %collective-permute-start.12 = (f32[16,128]{1,0:T(8,128)S(1)}, f32[16,128]{1,0:T(8,128)S(1)}, u32[]{:S(2)}, u32[]{:S(2)}) collective-permute-start(f32[16,128]{1,0:T(8,128)S(1)} %constant_dynamic-update-slice_fusion.4), channel_id=1, source_target_pairs={{0,12},{4,0},{8,4},{12,8},{1,13},{5,1},{9,5},{13,9},{2,14},{6,2},{... | collective-permute-start | bytes 24584 | tf_op jit(solution)/shard_map/ppermute | solution.py:433
  139.1 1.9 collective-permute-start.19
  139.2 5.3 %collective-permute-start.20 = (f32[8,2560]{1,0:T(8,128)S(1)}, f32[8,2560]{1,0:T(8,128)S(1)}, u32[]{:S(2)}, u32[]{:S(2)}) collective-permute-start(f32[8,2560]{1,0:T(8,128)S(1)} %combine.1), channel_id=1, source_target_pairs={{0,2},{1,3},{2,0},{3,1},{4,6},{5,7},{6,4},{7,5},{8,10},{9,11},{10,... | collective-permute-start | bytes 245768 | tf_op jit(solution)/shard_map/ppermute | solution.py:414
  140.5 4.7 %collective-permute-start.21 = (f32[8,2560]{1,0:T(8,128)S(1)}, f32[8,2560]{1,0:T(8,128)S(1)}, u32[]{:S(2)}, u32[]{:S(2)}) collective-permute-start(f32[8,2560]{1,0:T(8,128)S(1)} %combine.1), channel_id=1, source_target_pairs={{0,3},{1,2},{2,1},{3,0},{4,7},{5,6},{6,5},{7,4},{8,11},{9,10},{10,... | collective-permute-start | bytes 245768 | tf_op jit(solution)/shard_map/ppermute | solution.py:414
  165.7 1.5 collective-permute-start.22
  167.1 6.5 %collective-permute-start.23 = (f32[8,5120]{1,0:T(8,128)S(1)}, f32[8,5120]{1,0:T(8,128)S(1)}, u32[]{:S(2)}, u32[]{:S(2)}) collective-permute-start(f32[8,5120]{1,0:T(8,128)S(1)} %maximum_add_fusion.4), channel_id=1, source_target_pairs={{0,2},{1,3},{2,0},{3,1},{4,6},{5,7},{6,4},{7,5},{8,10},{9,11},{10,... | collective-permute-start | bytes 491528 | tf_op jit(solution)/shard_map/ppermute | solution.py:414
  173.7 1.5 collective-permute-start.24
  196.2 1.5 collective-permute-start.25
  197.7 6.3 %collective-permute-start.26 = (f32[8,5120]{1,0:T(8,128)S(1)}, f32[8,5120]{1,0:T(8,128)S(1)}, u32[]{:S(2)}, u32[]{:S(2)}) collective-permute-start(f32[8,5120]{1,0:T(8,128)S(1)} %maximum_add_fusion.6), channel_id=1, source_target_pairs={{0,2},{1,3},{2,0},{3,1},{4,6},{5,7},{6,4},{7,5},{8,10},{9,11},{10,... | collective-permute-start | bytes 491528 | tf_op jit(solution)/shard_map/ppermute | solution.py:414
  204.1 1.5 collective-permute-start.27
  206.3 13.8 %collective-permute-start.28 = (f32[16,2560]{1,0:T(8,128)S(1)}, f32[16,2560]{1,0:T(8,128)S(1)}, u32[]{:S(2)}, u32[]{:S(2)}) collective-permute-start(f32[16,2560]{1,0:T(8,128)S(1)} %pad_maximum_fusion.8), channel_id=1, source_target_pairs={{0,0},{1,4},{2,8},{3,12},{4,1},{5,5},{6,9},{7,13},{8,2},{9,6},{10,... | collective-permute-start | bytes 491528 | tf_op jit(solution)/shard_map/ppermute | solution.py:641
